TPU v7x, 32 devices: a whole 2x2x4 slice. The times are simulated.
32 devices in a mesh: slab: 16 (over z, y, x), sub: 2 (over core).
Axes of the slice: x: 2, y: 2, z: 4, core: 2. Of those that a mesh axis runs over, the one named last changes fastest.
Arguments:
- velocities: float32 [3, 163840], P(None, ('slab', 'sub')), may hold values from -16 to 19
- cell_index: int32 [1, 163840], P(None, ('slab', 'sub')), may hold values from 0 to 511
- axis_choice: int32 [1, 16384], P(None, ('slab', 'sub')), may hold values from 0 to 63
- moves: int32 [1, 4, 4096], P(None, None, ('slab', 'sub')), may hold values from 0 to 5119, as said below
- shear_target: float32 [128], P('sub'), may hold values from -6 to 6
Outputs:
- velocities_final: float32 [3, 163840], P(None, ('slab', 'sub'))
- profile: float32 [16, 128], P('slab', 'sub')
Inputs may be any that keep to these rules, and one draw needn't show every extreme that they name: `moves`: in each step the 512 slots of one device's four lists are distinct.
All inputs are finite; a program needn't handle non-finite values.
Results may differ from a plain program's by a relative error of at most 0.0003.
Values sent between devices are 32-bit elements; how exact they have to be, the bound alone decides.
No kernel may reach another device: no remote copies, remote signals or barrier semaphores. Data moves between devices by JAX's collectives and lax.ppermute only.
A program may use at most 64 MiB of HBM per device.

v0:
```python
import jax
import jax.numpy as jnp
from jax import lax
from jax.sharding import PartitionSpec as P

CX = 1
CY = 64
CZ = 8
NAXES = 64


ROT_COS = -0.6427876096865393
ROT_SIN = 0.766044443118978
RESERVOIR_HEAT = 0.9
FEEDBACK = 1.0
GOLDEN = 2.399963229728653


def from_behind(block, axis, distance):
    devices = range(lax.axis_size(axis))
    route = [((i - distance) % len(devices), i) for i in devices]
    return lax.ppermute(block, axis, route)


def axis_table():
    counter = jnp.arange(NAXES, dtype=jnp.int32).astype(jnp.float32)
    height = 1.0 - (2.0 * counter + 1.0) / NAXES
    radius = jnp.sqrt(1.0 - height * height)
    return jnp.stack(
        [radius * jnp.cos(GOLDEN * counter), radius * jnp.sin(GOLDEN * counter), height]
    )


def bin_cells(values, weights, cells, totals):
    stacked = jnp.concatenate([values, weights[None, :]], 0)
    return totals.at[:, cells].add(stacked)


def cell_state(totals, choices, table):
    counts = jnp.maximum(totals[3], 1.0)
    average_value = totals[:3] / counts
    onehot = (jnp.arange(NAXES, dtype=jnp.int32)[:, None] == choices[None, :]).astype(jnp.float32)
    axes = jnp.dot(table, onehot, precision=lax.Precision.HIGHEST)
    columns = jnp.sum(totals.reshape(4, CX * CY, CZ), 2)
    block = (columns[0] / jnp.maximum(columns[3], 1.0)).reshape(CX, CY)
    return (average_value, axes, block)


def collide(relative, cells, average_value, axes, speed_multiplier, adjustment_factor):
    normal = axes[:, cells]
    cross = jnp.stack(
        [
            normal[1] * relative[2] - normal[2] * relative[1],
            normal[2] * relative[0] - normal[0] * relative[2],
            normal[0] * relative[1] - normal[1] * relative[0],
        ]
    )
    along = jnp.sum(normal * relative, 0)
    rotated = relative * ROT_COS + cross * ROT_SIN + normal * (along * (1.0 - ROT_COS))
    shifted = average_value.at[0].add(adjustment_factor)
    return shifted[:, cells] + speed_multiplier * rotated


def body(velocities, cell_index, axis_choice, moves, shear_target):
    speeds = velocities
    slabs = lax.axis_size("slab")
    sub_count = lax.axis_size("sub")
    inner_position = lax.axis_index("sub")
    count_here = speeds.shape[1]
    whole_swarm = count_here * slabs * sub_count
    width_x = CX * slabs
    block_rows = moves.shape[2]
    table = axis_table()
    slots = moves[0].reshape(-1)
    cells = cell_index[0]
    outgoing = speeds[:, slots].reshape(3, 4, block_rows)
    weights = jnp.ones((count_here,), jnp.float32)
    empty = jnp.zeros((4, CX * CY * CZ), jnp.float32)
    east_in = from_behind(outgoing[:, 1], "slab", -1)
    west_in = from_behind(outgoing[:, 0], "slab", 1)
    north_incoming = from_behind(outgoing[:, 3], "sub", -1)
    south_in = from_behind(outgoing[:, 2], "sub", 1)
    arriving = jnp.stack([east_in, west_in, north_incoming, south_in], 1).reshape(3, 4 * block_rows)
    speeds = speeds.at[:, slots].set(arriving)
    totals = bin_cells(speeds, weights, cells, empty)
    average_value, axes, profile = cell_state(totals, axis_choice[0], table)
    relative = speeds - average_value[:, cells]
    local_energy = jnp.sum(relative * relative)
    line_aggregate = jnp.sum(profile, 0)
    padded = lax.dynamic_update_slice(
        jnp.zeros((CY * sub_count,), jnp.float32), line_aggregate, (inner_position * CY,)
    )
    summed, motion_work = lax.psum((padded, local_energy), ("slab", "sub"))
    column_sum = lax.dynamic_slice(summed, (inner_position * CY,), (CY,))
    speed_multiplier = lax.rsqrt(motion_work / (3.0 * whole_swarm * RESERVOIR_HEAT) + 1e-06)
    adjustment_factor = FEEDBACK * (shear_target - column_sum / width_x)
    per_cell = jnp.broadcast_to(adjustment_factor[None, :, None], (CX, CY, CZ)).reshape(-1)
    speeds = collide(relative, cells, average_value, axes, speed_multiplier, per_cell)
    return (speeds, profile)


def solution(mesh):
    in_specs = (
        P(None, ("slab", "sub")),
        P(None, ("slab", "sub")),
        P(None, ("slab", "sub")),
        P(None, None, ("slab", "sub")),
        P("sub"),
    )
    out_specs = (P(None, ("slab", "sub")), P("slab", "sub"))
    return jax.shard_map(body, mesh=mesh, in_specs=in_specs, out_specs=out_specs, check_vma=False)
```

profile of v0, /device:TPU:0, one launch (start us, length us, event | category | flops | bytes accessed | tf_op | source)
XLA Modules:
  0.0 134.7 jit_solution(16117041994723011014)
XLA Ops:
  0.7 1.7 %copy.103 = f32[3,5120]{0,1:T(8,128)S(1)} copy(f32[3,5120]{1,0:T(4,128)} %param.7) | data formatting | bytes 122880 | tf_op args[0]
  2.4 1.0 gather_fusion
  3.5 0.5 collective-permute-start.3
  4.2 3.0 %collective-permute-start.1 = (f32[3,128]{1,0:T(4,128)S(1)}, f32[3,128]{1,0:T(4,128)S(1)}, u32[]{:S(2)}, u32[]{:S(2)}) collective-permute-start(f32[3,128]{1,0:T(4,128)S(1)} %bitcast.41), channel_id=1, source_target_pairs={{30,0},{0,2},{2,4},{4,6},{6,8},{8,10},{10,12},{12,14},{14,16},{16,... | collective-permute-start | bytes 4616 | tf_op jit(solution)/shard_map/ppermute | solution.py:22
  7.2 4.0 %collective-permute-start = (f32[3,128]{1,0:T(4,128)S(1)}, f32[3,128]{1,0:T(4,128)S(1)}, u32[]{:S(2)}, u32[]{:S(2)}) collective-permute-start(f32[3,128]{1,0:T(4,128)S(1)} %bitcast.42), channel_id=1, source_target_pairs={{2,0},{4,2},{6,4},{8,6},{10,8},{12,10},{14,12},{16,14},{18,16},{20... | collective-permute-start | bytes 4616 | tf_op jit(solution)/shard_map/ppermute | solution.py:22
  11.4 0.4 fusion.5
  11.8 17.7 %gather_fusion.3 = f32[5120,3]{1,0:T(8,128)} fusion(f32[3,512]{0,1:T(8,128)S(1)} %fusion.5, s32[5120]{0:T(1024)S(1)} %broadcast_clamp_fusion), kind=kCustom, calls=%fused_computation.3 | custom fusion | bytes 143360 | tf_op jit(solution)/shard_map/gather | solution.py:50
  29.4 2.5 %copy.111 = f32[5120,3]{0,1:T(4,128)S(1)} copy(f32[5120,3]{1,0:T(8,128)} %gather_fusion.3) | data formatting | bytes 122880 | tf_op jit(solution)/shard_map/gather | solution.py:50
  32.0 0.1 copy.113
  32.2 2.7 %scatter_fusion = f32[3,5120]{0,1:T(8,128)S(1)} fusion(f32[3,5120]{0,1:T(8,128)S(1)} %copy.103, s32[512]{0:T(512)S(1)} %bitcast.37, f32[512,3]{1,0:T(8,128)S(1)} %bitcast.33), kind=kCustom, calls=%fused_computation.4 | custom fusion | bytes 20480 | tf_op jit(solution)/shard_map/scatter | solution.py:84
  34.9 0.8 copy.109
  35.6 27.9 %scatter_custom_fusion.1 = f32[4,512]{0,1:T(8,128)S(1)} fusion(s32[5120]{0:T(1024)S(1)} %bitcast.35, f32[3,5120]{0,1:T(8,128)S(1)} %scatter_fusion, f32[]{:T(128)} %constant.59.clone.1, f32[]{:T(128)} %constant.55.clone.1), kind=kCustom, calls=%fused_computation.6 | custom fusion | flops 20480 | bytes 2629640 | tf_op jit(solution)/shard_map/scatter-add | solution.py:36
  63.6 0.2 fusion.3
  63.9 0.1 slice_divide_fusion
  64.0 13.4 %gather_fusion.2 = f32[5120,3]{1,0:T(8,128)S(1)} fusion(f32[3,512]{0,1:T(8,128)S(1)} %slice_divide_fusion, s32[5120]{0:T(1024)S(1)} %broadcast_clamp_fusion), kind=kCustom, calls=%fused_computation.2 | custom fusion | bytes 143360 | tf_op jit(solution)/shard_map/gather | solution.py:87
  77.5 0.8 copy.108
  78.5 0.7 multiply_reduce_fusion.1
  79.2 0.5 bitcast_dynamic-update-slice_fusion
  79.7 38.0 %all-reduce.1 = (f32[128]{0:T(128)S(1)}, f32[]{:T(128)}) all-reduce(f32[128]{0:T(128)S(1)} %get-tuple-element.29, f32[]{:T(128)} %get-tuple-element.24), channel_id=1, replica_groups=mesh['slab'=16,'sub'=2] {'slab','sub'}, use_global_device_ids=true, to_apply=%region_3.0 | all-reduce | flops 129 | bytes 1032 | tf_op jit(solution)/shard_map/psum | solution.py:93
  117.8 0.1 broadcast_in_dim.12
  118.0 0.9 scatter-add.13
  118.9 13.4 %gather_fusion.1 = f32[5120,3]{1,0:T(8,128)S(1)} fusion(f32[3,512]{0,1:T(8,128)S(1)} %scatter-add.13, s32[5120]{0:T(1024)S(1)} %broadcast_clamp_fusion), kind=kCustom, calls=%fused_computation.1 | custom fusion | bytes 143360 | tf_op jit(solution)/shard_map/gather | solution.py:61
  132.4 0.8 copy.107
  133.9 0.7 fusion.9
  (39 shorter events, 1.0 us)
Async XLA Ops:
  0.6 1.7 %copy-start.2 = (s32[1,4,128]{2,1,0:T(4,128)S(1)}, s32[1,4,128]{2,1,0:T(4,128)}, u32[]{:S(2)}) copy-start(s32[1,4,128]{2,1,0:T(4,128)} %param.10) | copy-start | bytes 6148
  0.6 10.7 %copy-start = (s32[1,5120]{1,0:T(1,128)S(1)}, s32[1,5120]{1,0:T(1,128)}, u32[]{:S(2)}) copy-start(s32[1,5120]{1,0:T(1,128)} %param.8) | copy-start | bytes 61444
  0.7 10.7 %copy-start.1 = (s32[1,512]{1,0:T(1,128)S(1)}, s32[1,512]{1,0:T(1,128)}, u32[]{:S(2)}) copy-start(s32[1,512]{1,0:T(1,128)} %param.9) | copy-start | bytes 6148
  3.5 28.4 %collective-permute-start.3 = (f32[3,128]{1,0:T(4,128)S(1)}, f32[3,128]{1,0:T(4,128)S(1)}, u32[]{:S(2)}, u32[]{:S(2)}) collective-permute-start(f32[3,128]{1,0:T(4,128)S(1)} %bitcast.39), channel_id=1, source_target_pairs={{1,0},{0,1},{3,2},{2,3},{5,4},{4,5},{7,6},{6,7},{9,8},{8,9},{11,10... | collective-permute-start | bytes 4616 | tf_op jit(solution)/shard_map/ppermute | solution.py:22
  4.1 27.9 %collective-permute-start.2 = (f32[3,128]{1,0:T(4,128)S(1)}, f32[3,128]{1,0:T(4,128)S(1)}, u32[]{:S(2)}, u32[]{:S(2)}) collective-permute-start(f32[3,128]{1,0:T(4,128)S(1)} %bitcast.40), channel_id=1, source_target_pairs={{1,0},{0,1},{3,2},{2,3},{5,4},{4,5},{7,6},{6,7},{9,8},{8,9},{11,10... | collective-permute-start | bytes 4616 | tf_op jit(solution)/shard_map/ppermute | solution.py:22
  4.2 27.8 %collective-permute-start.1 = (f32[3,128]{1,0:T(4,128)S(1)}, f32[3,128]{1,0:T(4,128)S(1)}, u32[]{:S(2)}, u32[]{:S(2)}) collective-permute-start(f32[3,128]{1,0:T(4,128)S(1)} %bitcast.41), channel_id=1, source_target_pairs={{30,0},{0,2},{2,4},{4,6},{6,8},{8,10},{10,12},{12,14},{14,16},{16,... | collective-permute-start | bytes 4616 | tf_op jit(solution)/shard_map/ppermute | solution.py:22
  7.2 24.8 %collective-permute-start = (f32[3,128]{1,0:T(4,128)S(1)}, f32[3,128]{1,0:T(4,128)S(1)}, u32[]{:S(2)}, u32[]{:S(2)}) collective-permute-start(f32[3,128]{1,0:T(4,128)S(1)} %bitcast.42), channel_id=1, source_target_pairs={{2,0},{4,2},{6,4},{8,6},{10,8},{12,10},{14,12},{16,14},{18,16},{20... | collective-permute-start | bytes 4616 | tf_op jit(solution)/shard_map/ppermute | solution.py:22
  63.6 54.1 %copy-start.3 = (f32[64]{0:T(128)S(1)}, f32[64]{0:T(128)}, u32[]{:S(2)}) copy-start(f32[64]{0:T(128)} %param.11) | copy-start | bytes 772
where the time goes:
time: 135 us
  local copies, waits for them, and re-layouts  56.5 us (42%)
  blocking collectives  38 us (28%)
  other arithmetic  30.7 us (23%)
  starting transfers between devices  7.58 us (6%)
  between operations  1.62 us (1%)
    psum x1, blocking collectives, body(): summed, motion_work = lax.psum((padded, local_energy), ('slab', 'sub'))  38 us
    scatter-add x1, other arithmetic, bin_cells(): return totals.at[:, cells].add(stacked)  27.9 us
    gather x2, local copies, waits for them, and re-layouts, collide(): normal = axes[:, cells]  20.2 us
    gather x2, local copies, waits for them, and re-layouts, body(): relative = speeds - average_value[:, cells]  14.2 us
    gather x2, local copies, waits for them, and re-layouts, collide(): return shifted[:, cells] + speed_multiplier * rotated  14.2 us
    ppermute x4, starting transfers between devices, from_behind(): return lax.ppermute(block, axis, route)  7.58 us
    scatter x2, local copies, waits for them, and re-layouts, body(): speeds = speeds.at[:, slots].set(arriving)  3.44 us
  transfers between devices with their start and end apart: 4, of which 0 were waited for; matrix products, arithmetic and copies ran while one was open for 15% of the time, Pallas kernels for 0%

commit v1 on v0

v1 whole, which is shorter than its diff:
```python
import functools
import math

import jax
import jax.numpy as jnp
from jax import lax
from jax.experimental import pallas as pl
from jax.experimental.pallas import tpu as pltpu
from jax.sharding import PartitionSpec as P

CX = 1
CY = 64
CZ = 8
NAXES = 64

ROT_COS = -0.6427876096865393
ROT_SIN = 0.766044443118978
RESERVOIR_HEAT = 0.9
FEEDBACK = 1.0
GOLDEN = 2.399963229728653

LANES = 128
SUBLANES = 8
AXES = ("slab", "sub")
VMEM = pl.BlockSpec(memory_space=pltpu.VMEM)
NT = (((1,), (1,)), ((), ()))
TAKE = lax.GatherDimensionNumbers(
    offset_dims=(),
    collapsed_slice_dims=(1,),
    start_index_map=(1,),
    operand_batching_dims=(0,),
    start_indices_batching_dims=(0,),
)


def take(rows, lanes):
    return lax.gather(
        rows,
        lanes[:, :, None],
        dimension_numbers=TAKE,
        slice_sizes=(1, 1),
        mode=lax.GatherScatterMode.PROMISE_IN_BOUNDS,
    )


def lookup(rows, index, shift=7):
    high, low = index >> shift, index & (LANES - 1)
    out = jnp.zeros(index.shape, rows[0].dtype)
    for h, row in enumerate(rows):
        out = jnp.where(high == h, take(jnp.broadcast_to(row, index.shape), low), out)
    return out


def iota(shape, axis):
    return lax.broadcasted_iota(jnp.int32, shape, axis)


def split3(x):
    a = x.astype(jnp.bfloat16).astype(jnp.float32)
    rest = x - a
    b = rest.astype(jnp.bfloat16).astype(jnp.float32)
    return a, b, rest - b


def parity(axis):
    if lax.axis_size(axis) % 2:
        return 0
    return lax.rem(lax.axis_index(axis), 2)


def ordered_lists(moves_ref):
    lists = []
    for base, axis in ((0, "slab"), (2, "sub")):
        odd = parity(axis)
        one, two = moves_ref[base : base + 1], moves_ref[base + 1 : base + 2]
        lists += [jnp.where(odd == 0, one, two), jnp.where(odd == 0, two, one)]
    return lists


def departures(v_ref, moves_ref, *out_refs):
    comps, count = v_ref.shape
    lists = ordered_lists(moves_ref)
    for index, out_ref, lane in zip(
        lists,
        (out_refs[0], out_refs[1], out_refs[2], out_refs[2]),
        (0, 0, 0, LANES),
    ):
        index = jnp.broadcast_to(index, (comps, LANES))
        high, low = index >> 7, index & (LANES - 1)
        out = jnp.zeros((comps, LANES), jnp.float32)
        for r in range(count // LANES):
            tile = v_ref[:, r * LANES : (r + 1) * LANES]
            out = jnp.where(high == r, take(tile, low), out)
        out_ref[:, lane : lane + LANES] = out


def prepare(v_ref, moves_ref, cell_ref, choice_ref, vd_ref, source_ref, celld_ref, base_ref, slotcell_ref, normal_ref, keep_ref):
    comps, count = v_ref.shape
    rows = count // LANES
    cells = choice_ref.shape[1]
    blocks = cells // LANES
    lists = ordered_lists(moves_ref)
    for r in range(rows):
        span = slice(r * LANES, (r + 1) * LANES)
        celld_ref[r : r + 1, :] = cell_ref[0:1, span]
        for c in range(comps):
            vd_ref[c, r : r + 1, :] = v_ref[c : c + 1, span]

    slots = jnp.concatenate(lists, 1)
    many = slots.shape[1]
    low = (iota((LANES, many), 0) == (slots & (LANES - 1))).astype(jnp.bfloat16)
    here = iota((rows, many), 0) == (slots >> 7)
    lane = iota((rows, many), 1)
    marks = jnp.concatenate(
        [
            jnp.where(here, (lane >> 7) + 1, 0).astype(jnp.float32),
            jnp.where(here, lane & (LANES - 1), 0).astype(jnp.float32),
        ]
    ).astype(jnp.bfloat16)
    found = lax.dot_general(marks, low, NT, preferred_element_type=jnp.float32).astype(jnp.int32)
    source = found[:rows] * LANES + found[rows:]
    source_ref[...] = source
    keep_ref[...] = jnp.where(source == 0, 1.0, 0.0)

    celld = celld_ref[...]
    four = jnp.concatenate(lists + lists, 0)
    slotcell_ref[...] = lookup([celld_ref[r : r + 1, :] for r in range(rows)], four)

    counter = (iota((1, LANES), 1) & (NAXES - 1)).astype(jnp.float32)
    height = 1.0 - (2.0 * counter + 1.0) / NAXES
    radius = jnp.sqrt(1.0 - height * height)
    table = (radius * jnp.cos(GOLDEN * counter), radius * jnp.sin(GOLDEN * counter), height)
    picks = [choice_ref[0:1, h * LANES : (h + 1) * LANES] for h in range(blocks)]
    for c in range(comps):
        entries = [take(table[c], pick) for pick in picks]
        normal_ref[c] = lookup(entries, celld)

    ones = (iota((SUBLANES - comps, LANES), 0) == 0).astype(jnp.float32)
    total = jnp.zeros((blocks * 3 * SUBLANES, LANES), jnp.float32)
    group = 4 if rows % 4 == 0 else 1
    for first in range(0, rows, group):
        left, right = [], []
        for r in range(first, first + group):
            cell = cell_ref[0:1, r * LANES : (r + 1) * LANES]
            tile = v_ref[:, r * LANES : (r + 1) * LANES] * keep_ref[r : r + 1, :]
            tile = jnp.concatenate([tile, ones], 0)
            parts = jnp.concatenate(split3(tile), 0)
            left.append(jnp.concatenate([jnp.where((cell >> 7) == h, parts, 0.0) for h in range(blocks)], 0))
            right.append((iota((LANES, LANES), 0) == (cell & (LANES - 1))).astype(jnp.bfloat16))
        left = jnp.concatenate(left, 1).astype(jnp.bfloat16)
        right = jnp.concatenate(right, 1)
        total += lax.dot_general(left, right, NT, preferred_element_type=jnp.float32)
    for h in range(blocks):
        part = total[h * 3 * SUBLANES : (h + 1) * 3 * SUBLANES]
        base_ref[h * SUBLANES : (h + 1) * SUBLANES] = part[:8] + part[8:16] + part[16:]


def relax(a_ref, b_ref, s_ref, vd_ref, source_ref, celld_ref, base_ref, slotcell_ref, normal_ref, send_ref, profile_ref, mean_ref, turned_ref):
    comps, rows, _ = vd_ref.shape
    blocks = base_ref.shape[0] // SUBLANES
    arrived = [a_ref[...], b_ref[...], s_ref[:, :LANES], s_ref[:, LANES:]]

    pad = jnp.zeros((SUBLANES - comps, LANES), jnp.float32)
    left, right = [], []
    for k, block in enumerate(arrived):
        cell = slotcell_ref[k : k + 1, :]
        parts = jnp.concatenate(split3(jnp.concatenate([block, pad], 0)), 0)
        left.append(jnp.concatenate([jnp.where((cell >> 7) == h, parts, 0.0) for h in range(blocks)], 0))
        right.append((iota((LANES, LANES), 0) == (cell & (LANES - 1))).astype(jnp.bfloat16))
    left = jnp.concatenate(left, 1).astype(jnp.bfloat16)
    right = jnp.concatenate(right, 1)
    fresh = lax.dot_general(left, right, NT, preferred_element_type=jnp.float32)
    sums, means = [], []
    for h in range(blocks):
        part = fresh[h * 3 * SUBLANES : (h + 1) * 3 * SUBLANES]
        total = base_ref[h * SUBLANES : (h + 1) * SUBLANES] + (part[:8] + part[8:16] + part[16:])
        sums.append(total)
        means.append(total / jnp.maximum(jnp.broadcast_to(total[comps : comps + 1], total.shape), 1.0))

    both = jnp.concatenate([s[0:1] for s in sums] + [s[comps : comps + 1] for s in sums], 0)
    width = CZ // 2
    while width:
        both = both + pltpu.roll(both, LANES - width, 1)
        width //= 2
    columns = iota((1, LANES), 1)
    start = columns * CZ
    flow = lookup([both[h : h + 1] for h in range(blocks)], start)
    number = lookup([both[blocks + h : blocks + h + 1] for h in range(blocks)], start)
    profile = flow / jnp.maximum(number, 1.0)
    profile_ref[...] = profile[:, :CY]

    source, celld = source_ref[...], celld_ref[...]
    relative, energy = [], jnp.zeros((rows, LANES), jnp.float32)
    for c in range(comps):
        old = vd_ref[c]
        speed = jnp.where(source == 0, old, lookup([x[c : c + 1] for x in arrived], source - LANES))
        mean = lookup([m[c : c + 1] for m in means], celld)
        mean_ref[c] = mean
        relative.append(speed - mean)
        energy += relative[c] * relative[c]
    energy = jnp.sum(energy, 0, keepdims=True)
    energy = energy + pltpu.roll(energy, CY, 1)
    message = jnp.where(columns < CY, profile, energy)
    send_ref[...] = jnp.broadcast_to(message[None], send_ref.shape)

    n = [normal_ref[c] for c in range(comps)]
    along = (n[0] * relative[0] + n[1] * relative[1] + n[2] * relative[2]) * (1.0 - ROT_COS)
    for c in range(comps):
        d, e = (c + 1) % comps, (c + 2) % comps
        cross = n[d] * relative[e] - n[e] * relative[d]
        turned_ref[c] = relative[c] * ROT_COS + cross * ROT_SIN + n[c] * along


def finish(got_ref, shear_ref, mean_ref, turned_ref, celld_ref, out_ref, *, slabs, subs, particles):
    comps, rows, _ = mean_ref.shape
    got = got_ref[...].reshape(slabs * subs, LANES)
    mine = lax.rem(iota(got.shape, 0), subs) == lax.axis_index("sub")
    lane = iota(got.shape, 1)
    drift = jnp.sum(jnp.where(mine, got, 0.0), 0, keepdims=True) / (CX * slabs)
    work = jnp.sum(jnp.where(lane < CY, 0.0, got), 0, keepdims=True)
    work = jnp.sum(work, 1, keepdims=True)
    scale = lax.rsqrt(work / (3.0 * particles * RESERVOIR_HEAT) + 1e-06)
    scale = jnp.broadcast_to(scale, (rows, LANES))
    target = jnp.concatenate([shear_ref[...], jnp.zeros((1, LANES - CY), jnp.float32)], 1)
    extra = FEEDBACK * (target - drift)
    line = (celld_ref[...] // CZ) & (CY - 1)
    extra = take(jnp.broadcast_to(extra, (rows, LANES)), line)
    for c in range(comps):
        base = mean_ref[c] + extra if c == 0 else mean_ref[c]
        out = base + scale * turned_ref[c]
        for r in range(rows):
            out_ref[c : c + 1, r * LANES : (r + 1) * LANES] = out[r : r + 1, :]


def swap(blocks, axis):
    size = lax.axis_size(axis)
    one, two = blocks
    if size % 2:
        forth = [(i, (i + 1) % size) for i in range(size)]
        back = [(i, (i - 1) % size) for i in range(size)]
        return [lax.ppermute(two, axis, back), lax.ppermute(one, axis, forth)]
    even = [(i, i ^ 1) for i in range(size)]
    odd = [(i, (i + 1 if i % 2 else i - 1) % size) for i in range(size)]
    return [lax.ppermute(one, axis, even), lax.ppermute(two, axis, odd)]


def swap_joined(block, axis):
    size = lax.axis_size(axis)
    if size == 2:
        return lax.ppermute(block, axis, [(0, 1), (1, 0)])
    return jnp.concatenate(swap([block[:, :LANES], block[:, LANES:]], axis), 1)


def f32(*shape):
    return jax.ShapeDtypeStruct(shape, jnp.float32)


def i32(*shape):
    return jax.ShapeDtypeStruct(shape, jnp.int32)


def call(kernel, out_shape, inputs, scratch=(), flops=0):
    outs = jax.tree.leaves(out_shape)
    size = sum(4 * math.prod(x.shape) for x in list(inputs) + outs)
    return pl.pallas_call(
        kernel,
        out_shape=out_shape,
        in_specs=[VMEM] * len(inputs),
        out_specs=jax.tree.map(lambda _: VMEM, out_shape),
        scratch_shapes=list(scratch),
        cost_estimate=pl.CostEstimate(flops=flops, bytes_accessed=size, transcendentals=0),
    )(*inputs)


def step(speeds, cells, choices, moves, shear_target):
    slabs, subs = lax.axis_size("slab"), lax.axis_size("sub")
    comps, count = speeds.shape
    rows = count // LANES
    blocks = choices.shape[1] // LANES
    a, b, s = call(
        departures,
        (f32(comps, LANES), f32(comps, LANES), f32(comps, 2 * LANES)),
        (speeds, moves),
    )
    a, b = swap([a, b], "slab")
    s = swap_joined(s, "sub")
    dense = f32(comps, rows, LANES)
    index = i32(rows, LANES)
    vd, source, celld, base, slotcell, normal = call(
        prepare,
        (dense, index, index, f32(blocks * SUBLANES, LANES), i32(SUBLANES, LANES), dense),
        (speeds, moves, cells, choices),
        scratch=[pltpu.VMEM((rows, LANES), jnp.float32)],
        flops=2 * count * LANES * 96,
    )
    send, profile, mean, turned = call(
        relax,
        (f32(slabs * subs, 1, LANES), f32(1, CX * CY), dense, dense),
        (a, b, s, vd, source, celld, base, slotcell, normal),
    )
    got = lax.all_to_all(send, AXES, 0, 0, tiled=True)
    out = call(
        functools.partial(finish, slabs=slabs, subs=subs, particles=count * slabs * subs),
        f32(comps, count),
        (got, shear_target[None, :], mean, turned, celld),
    )
    return out, profile


def body(velocities, cell_index, axis_choice, moves, shear_target):
    speeds, profile = velocities, None
    for t in range(moves.shape[0]):
        speeds, profile = step(speeds, cell_index[t : t + 1], axis_choice[t : t + 1], moves[t], shear_target)
    return speeds, profile


def solution(mesh):
    in_specs = (
        P(None, ("slab", "sub")),
        P(None, ("slab", "sub")),
        P(None, ("slab", "sub")),
        P(None, None, ("slab", "sub")),
        P("sub"),
    )
    out_specs = (P(None, ("slab", "sub")), P("slab", "sub"))
    return jax.shard_map(body, mesh=mesh, in_specs=in_specs, out_specs=out_specs, check_vma=False)
```

time: 135 us -> 29.5 us (0.22)
  local copies, waits for them, and re-layouts: 56.5 us -> 0.6 us
  other arithmetic: 30.7 us -> 0 us
  blocking collectives: 38 us -> 12 us
  Pallas kernels: 0 us -> 7.89 us
    gather x7 -> x0, local copies, waits for them, and re-layouts: 49.6 us -> none  [the longest x2 20.2 us: collide(): normal = axes[:, cells]]
    psum x1 -> x0, blocking collectives: 38 us -> none  [body(): summed, motion_work = lax.psum((padded, local_energy), ('slab', 'sub'))]
    scatter-add x1 -> x0, other arithmetic: 27.9 us -> none  [bin_cells(): return totals.at[:, cells].add(stacked)]
    all_to_all x0 -> x1, blocking collectives: none -> 12 us  [step(): got = lax.all_to_all(send, AXES, 0, 0, tiled=True)]
    pallas_call x0 -> x4, Pallas kernels: none -> 7.89 us  [call(): pl.pallas_call(kernel, out_shape=out_shape, in_specs=[VMEM] * len(inputs)...]
    scatter x2 -> x0, local copies, waits for them, and re-layouts: 3.44 us -> none  [body(): speeds = speeds.at[:, slots].set(arriving)]
    unnamed x15 -> x8, local copies, waits for them, and re-layouts: 2.07 us -> 0.6 us
    ppermute x4 -> x3, starting transfers between devices: 7.58 us -> 7.5 us  [the longest x2 7.5 us: swap(): return [lax.ppermute(one, axis, even), lax.ppermute(two, axis, odd)]]
  transfers between devices with their start and end apart: 4 -> 3, of which waited for: 0 -> 1; matrix products, arithmetic and copies ran while one was open for 15% -> 0% of each run, Pallas kernels for 0% -> 8%
where the time goes in v1:
time: 29.5 us; the launch traced here: 29.2 us
  blocking collectives  12 us (41%)
  Pallas kernels  7.89 us (27%)
  starting transfers between devices  7.5 us (25%)
  between operations  0.64 us (2%)
  local copies, waits for them, and re-layouts  0.6 us (2%)
  waiting for transfers between devices  0.51 us (2%)
    all_to_all x1, blocking collectives, step(): got = lax.all_to_all(send, AXES, 0, 0, tiled=True)  12 us
    pallas_call x4, Pallas kernels, call(): pl.pallas_call(kernel, out_shape=out_shape, in_specs=[VMEM] * len(inputs)...  7.89 us
    ppermute x2, starting transfers between devices, swap(): return [lax.ppermute(one, axis, even), lax.ppermute(two, axis, odd)]  7.5 us
    unnamed x8, local copies, waits for them, and re-layouts  0.6 us
  transfers between devices with their start and end apart: 3, of which 1 were waited for; matrix products, arithmetic and copies ran while one was open for 0% of the time, Pallas kernels for 8%

profile of v1, /device:TPU:0, one launch (start us, length us, event | category | flops | bytes accessed | tf_op | source)
XLA Modules:
  0.0 29.2 jit_solution(2822858548189879373)
XLA Ops:
  0.6 1.7 %shard_map.68 = (f32[3,128]{1,0:T(4,128)}, f32[3,128]{1,0:T(4,128)}, f32[3,256]{1,0:T(4,128)}) custom-call(f32[3,5120]{1,0:T(4,128)} %v_ref.3, s32[4,128]{1,0:T(4,128)} %bitcast.2), custom_call_target="tpu_custom_call" | custom-call | bytes 69632 | tf_op jit(solution)/shard_map/pallas_call | solution.py:265
  2.4 0.0 copy-start.3
  2.4 3.0 %collective-permute-start = (f32[3,128]{1,0:T(4,128)}, f32[3,128]{1,0:T(4,128)S(1)}, u32[]{:S(2)}, u32[]{:S(2)}) collective-permute-start(f32[3,128]{1,0:T(4,128)} %get-tuple-element.15), channel_id=1, source_target_pairs={{0,2},{2,0},{4,6},{6,4},{8,10},{10,8},{12,14},{14,12},{16,18},{18,... | collective-permute-start | bytes 4616 | tf_op jit(solution)/shard_map/ppermute | solution.py:244
  5.3 4.5 %collective-permute-start.1 = (f32[3,128]{1,0:T(4,128)}, f32[3,128]{1,0:T(4,128)S(1)}, u32[]{:S(2)}, u32[]{:S(2)}) collective-permute-start(f32[3,128]{1,0:T(4,128)} %get-tuple-element.16), channel_id=1, source_target_pairs={{0,30},{2,4},{4,2},{6,8},{8,6},{10,12},{12,10},{14,16},{16,14},{18... | collective-permute-start | bytes 4616 | tf_op jit(solution)/shard_map/ppermute | solution.py:244
  9.9 0.0 copy-done.3
  9.9 0.0 collective-permute-start.2
  9.9 2.3 %shard_map.69 = (f32[3,40,128]{2,1,0:T(8,128)}, s32[40,128]{1,0:T(8,128)}, s32[40,128]{1,0:T(8,128)}, f32[32,128]{1,0:T(8,128)}, s32[8,128]{1,0:T(8,128)}, /*index=5*/f32[3,40,128]{2,1,0:T(8,128)}) custom-call(f32[3,5120]{1,0:T(4,128)} %v_ref.3, s32[4,128]{1,0:T(4,128)} %bitcast.3, s32[1,5120]{1,0:T(1,128)} %cell_ref.1, s32[1,512]{1,0:T(1,128)} %choice_ref.1), custom_call_target="tpu_custom_call" | custom-call | flops 125829120 | bytes 270336 | tf_op jit(solution)/shard_map/pallas_call | solution.py:265
  12.2 0.0 collective-permute-done.a_ref
  12.2 0.0 copy-start.1
  12.2 0.5 %collective-permute-done.1.b_ref = f32[3,128]{1,0:T(4,128)S(1)} collective-permute-done((f32[3,128]{1,0:T(4,128)}, f32[3,128]{1,0:T(4,128)S(1)}, u32[]{:S(2)}, u32[]{:S(2)}) %collective-permute-start.1) | collective-permute-done | bytes 1568 | tf_op jit(solution)/shard_map/ppermute | solution.py:244
  12.7 0.0 copy-start.2
  12.7 0.0 collective-permute-done.2.s_ref
  12.7 0.0 copy-start
  12.7 0.1 copy-done.1
  12.8 0.5 %copy-done.2 = f32[3,128]{1,0:T(4,128)} copy-done((f32[3,128]{1,0:T(4,128)}, f32[3,128]{1,0:T(4,128)S(1)}, u32[]{:S(2)}) %copy-start.2) | copy-done | bytes 1560
  13.3 0.0 copy-done
  13.3 2.1 %shard_map.70 = (f32[32,1,128]{2,1,0:T(1,128)}, f32[1,64]{1,0:T(1,128)}, f32[3,40,128]{2,1,0:T(8,128)}, f32[3,40,128]{2,1,0:T(8,128)}) custom-call(f32[3,128]{1,0:T(4,128)} %copy-done.1, f32[3,128]{1,0:T(4,128)} %copy-done.2, f32[3,256]{1,0:T(4,128)} %copy-done, f32[3,40,128]{2,1,0:T(8,128)} %get-tuple-element.18.vd_ref, ...), custom_call_target="tpu_custom_call" | custom-call | bytes 329984 | tf_op jit(solution)/shard_map/pallas_call | solution.py:265
  15.5 12.0 %all_to_all.5.got_ref = f32[32,1,128]{2,1,0:T(1,128)} all-to-all(f32[32,1,128]{2,1,0:T(1,128)} %get-tuple-element.24), channel_id=1, replica_groups=mesh['slab'=16,'sub'=2] {'slab','sub'}, dimensions={0} | all-to-all | bytes 32768 | tf_op jit(solution)/shard_map/all_to_all | solution.py:301
  27.5 1.7 %shard_map.71 = f32[3,5120]{1,0:T(4,128)} custom-call(f32[32,1,128]{2,1,0:T(1,128)} %all_to_all.5.got_ref, f32[1,64]{1,0:T(1,128)} %bitcast.4, f32[3,40,128]{2,1,0:T(8,128)} %get-tuple-element.25.mean_ref, f32[3,40,128]{2,1,0:T(8,128)} %get-tuple-element.26.turned_ref, s32[40,128]{1,0:T(8,128)} %get-tuple-element.20.celld_ref), custom_call_target="tpu_custom_call" | custom-call | bytes 221440 | tf_op jit(solution)/shard_map/pallas_call | solution.py:265
Async XLA Ops:
  2.4 7.5 %copy-start.3 = (f32[3,256]{1,0:T(4,128)S(1)}, f32[3,256]{1,0:T(4,128)}, u32[]{:S(2)}) copy-start(f32[3,256]{1,0:T(4,128)} %get-tuple-element.17) | copy-start | bytes 9220
  2.4 9.8 %collective-permute-start = (f32[3,128]{1,0:T(4,128)}, f32[3,128]{1,0:T(4,128)S(1)}, u32[]{:S(2)}, u32[]{:S(2)}) collective-permute-start(f32[3,128]{1,0:T(4,128)} %get-tuple-element.15), channel_id=1, source_target_pairs={{0,2},{2,0},{4,6},{6,4},{8,10},{10,8},{12,14},{14,12},{16,18},{18,... | collective-permute-start | bytes 4616 | tf_op jit(solution)/shard_map/ppermute | solution.py:244
  5.3 7.4 %collective-permute-start.1 = (f32[3,128]{1,0:T(4,128)}, f32[3,128]{1,0:T(4,128)S(1)}, u32[]{:S(2)}, u32[]{:S(2)}) collective-permute-start(f32[3,128]{1,0:T(4,128)} %get-tuple-element.16), channel_id=1, source_target_pairs={{0,30},{2,4},{4,2},{6,8},{8,6},{10,12},{12,10},{14,16},{16,14},{18... | collective-permute-start | bytes 4616 | tf_op jit(solution)/shard_map/ppermute | solution.py:244
  9.9 2.9 %collective-permute-start.2 = (f32[3,256]{1,0:T(4,128)S(1)}, f32[3,256]{1,0:T(4,128)S(1)}, u32[]{:S(2)}, u32[]{:S(2)}) collective-permute-start(f32[3,256]{1,0:T(4,128)S(1)} %copy-done.3), channel_id=1, source_target_pairs={{0,1},{1,0},{2,3},{3,2},{4,5},{5,4},{6,7},{7,6},{8,9},{9,8},{10,11... | collective-permute-start | bytes 9224 | tf_op jit(solution)/shard_map/ppermute | solution.py:250
  12.2 0.6 %copy-start.1 = (f32[3,128]{1,0:T(4,128)}, f32[3,128]{1,0:T(4,128)S(1)}, u32[]{:S(2)}) copy-start(f32[3,128]{1,0:T(4,128)S(1)} %collective-permute-done.a_ref) | copy-start | bytes 4612
  12.7 0.6 %copy-start.2 = (f32[3,128]{1,0:T(4,128)}, f32[3,128]{1,0:T(4,128)S(1)}, u32[]{:S(2)}) copy-start(f32[3,128]{1,0:T(4,128)S(1)} %collective-permute-done.1.b_ref) | copy-start | bytes 4612
  12.7 0.6 %copy-start = (f32[3,256]{1,0:T(4,128)}, f32[3,256]{1,0:T(4,128)S(1)}, u32[]{:S(2)}) copy-start(f32[3,256]{1,0:T(4,128)S(1)} %collective-permute-done.2.s_ref) | copy-start | bytes 9220

commit v2 on v1

--- a/solution.py
+++ b/solution.py
@@ -94,12 +94,13 @@
         out_ref[:, lane : lane + LANES] = out
 
 
-def prepare(v_ref, moves_ref, cell_ref, choice_ref, vd_ref, source_ref, celld_ref, base_ref, slotcell_ref, normal_ref, keep_ref):
+def prepare(v_ref, moves_ref, cell_ref, choice_ref, shear_ref, vd_ref, source_ref, celld_ref, base_ref, slotcell_ref, normal_ref, target_ref, keep_ref):
     comps, count = v_ref.shape
     rows = count // LANES
     cells = choice_ref.shape[1]
     blocks = cells // LANES
     lists = ordered_lists(moves_ref)
+    target_ref[...] = jnp.concatenate([shear_ref[...], jnp.zeros((1, LANES - CY), jnp.float32)], 1)
     for r in range(rows):
         span = slice(r * LANES, (r + 1) * LANES)
         celld_ref[r : r + 1, :] = cell_ref[0:1, span]
@@ -211,7 +212,7 @@
         turned_ref[c] = relative[c] * ROT_COS + cross * ROT_SIN + n[c] * along
 
 
-def finish(got_ref, shear_ref, mean_ref, turned_ref, celld_ref, out_ref, *, slabs, subs, particles):
+def finish(got_ref, target_ref, mean_ref, turned_ref, celld_ref, out_ref, *, slabs, subs, particles):
     comps, rows, _ = mean_ref.shape
     got = got_ref[...].reshape(slabs * subs, LANES)
     mine = lax.rem(iota(got.shape, 0), subs) == lax.axis_index("sub")
@@ -221,8 +222,7 @@
     work = jnp.sum(work, 1, keepdims=True)
     scale = lax.rsqrt(work / (3.0 * particles * RESERVOIR_HEAT) + 1e-06)
     scale = jnp.broadcast_to(scale, (rows, LANES))
-    target = jnp.concatenate([shear_ref[...], jnp.zeros((1, LANES - CY), jnp.float32)], 1)
-    extra = FEEDBACK * (target - drift)
+    extra = FEEDBACK * (target_ref[...] - drift)
     line = (celld_ref[...] // CZ) & (CY - 1)
     extra = take(jnp.broadcast_to(extra, (rows, LANES)), line)
     for c in range(comps):
@@ -241,7 +241,8 @@
         return [lax.ppermute(two, axis, back), lax.ppermute(one, axis, forth)]
     even = [(i, i ^ 1) for i in range(size)]
     odd = [(i, (i + 1 if i % 2 else i - 1) % size) for i in range(size)]
-    return [lax.ppermute(one, axis, even), lax.ppermute(two, axis, odd)]
+    second = lax.ppermute(two, axis, odd)
+    return [lax.ppermute(one, axis, even), second]
 
 
 def swap_joined(block, axis):
@@ -252,16 +253,17 @@
 
 
 def f32(*shape):
-    return jax.ShapeDtypeStruct(shape, jnp.float32)
+    return pltpu.VMEM(shape, jnp.float32)
 
 
 def i32(*shape):
-    return jax.ShapeDtypeStruct(shape, jnp.int32)
-
-
-def call(kernel, out_shape, inputs, scratch=(), flops=0):
-    outs = jax.tree.leaves(out_shape)
-    size = sum(4 * math.prod(x.shape) for x in list(inputs) + outs)
+    return pltpu.VMEM(shape, jnp.int32)
+
+
+def call(kernel, out_shape, inputs, scratch=(), flops=0, resident=True):
+    size = sum(4 * math.prod(x.shape) for x in inputs)
+    if resident:
+        inputs = [pltpu.with_memory_space_constraint(x, pltpu.VMEM) for x in inputs]
     return pl.pallas_call(
         kernel,
         out_shape=out_shape,
@@ -281,28 +283,29 @@
         departures,
         (f32(comps, LANES), f32(comps, LANES), f32(comps, 2 * LANES)),
         (speeds, moves),
+        resident=False,
     )
     a, b = swap([a, b], "slab")
     s = swap_joined(s, "sub")
     dense = f32(comps, rows, LANES)
     index = i32(rows, LANES)
-    vd, source, celld, base, slotcell, normal = call(
+    vd, source, celld, base, slotcell, normal, target = call(
         prepare,
-        (dense, index, index, f32(blocks * SUBLANES, LANES), i32(SUBLANES, LANES), dense),
-        (speeds, moves, cells, choices),
+        (dense, index, index, f32(blocks * SUBLANES, LANES), i32(SUBLANES, LANES), dense, f32(1, LANES)),
+        (speeds, moves, cells, choices, shear_target[None, :]),
         scratch=[pltpu.VMEM((rows, LANES), jnp.float32)],
         flops=2 * count * LANES * 96,
     )
     send, profile, mean, turned = call(
         relax,
-        (f32(slabs * subs, 1, LANES), f32(1, CX * CY), dense, dense),
+        (f32(slabs * subs, 1, LANES), jax.ShapeDtypeStruct((1, CX * CY), jnp.float32), dense, dense),
         (a, b, s, vd, source, celld, base, slotcell, normal),
     )
     got = lax.all_to_all(send, AXES, 0, 0, tiled=True)
     out = call(
         functools.partial(finish, slabs=slabs, subs=subs, particles=count * slabs * subs),
-        f32(comps, count),
-        (got, shear_target[None, :], mean, turned, celld),
+        jax.ShapeDtypeStruct((comps, count), jnp.float32),
+        (got, target, mean, turned, celld),
     )
     return out, profile
 

time: 29.5 us -> 26 us (0.88)
  Pallas kernels: 7.89 us -> 3.85 us
  local copies, waits for them, and re-layouts: 0.6 us -> 1.37 us
    pallas_call x4, Pallas kernels: 7.89 us -> 3.85 us  [call(): pl.pallas_call(kernel, out_shape=out_shape, in_specs=[VMEM] * len(inputs)...]
    unnamed x8 -> x10, local copies, waits for them, and re-layouts: 0.6 us -> 1.37 us
  transfers between devices with their start and end apart: 3 -> 3, of which waited for: 1 -> 1; matrix products, arithmetic and copies ran while one was open for 0% -> 0% of each run, Pallas kernels for 8% -> 3%
where the time goes in v2:
time: 26 us; the launch traced here: 25.8 us
  blocking collectives  11.9 us (46%)
  starting transfers between devices  7.56 us (29%)
  Pallas kernels  3.85 us (15%)
  local copies, waits for them, and re-layouts  1.37 us (5%)
  between operations  0.68 us (3%)
  waiting for transfers between devices  0.43 us (2%)
    all_to_all x1, blocking collectives, step(): got = lax.all_to_all(send, AXES, 0, 0, tiled=True)  11.9 us
    ppermute x1, starting transfers between devices, swap(): second = lax.ppermute(two, axis, odd)  4.53 us
    pallas_call x4, Pallas kernels, call(): pl.pallas_call(kernel, out_shape=out_shape, in_specs=[VMEM] * len(inputs)...  3.85 us
    ppermute x1, starting transfers between devices, swap(): return [lax.ppermute(one, axis, even), second]  3.03 us
    unnamed x10, local copies, waits for them, and re-layouts  1.37 us
  transfers between devices with their start and end apart: 3, of which 1 were waited for; matrix products, arithmetic and copies ran while one was open for 0% of the time, Pallas kernels for 3%

profile of v2, /device:TPU:0, one launch (start us, length us, event | category | flops | bytes accessed | tf_op | source)
XLA Modules:
  0.0 25.8 jit_solution(13628085911030589885)
XLA Ops:
  0.6 0.0 copy-start
  0.6 1.2 %shard_map.68 = (f32[3,128]{1,0:T(4,128)S(1)}, f32[3,128]{1,0:T(4,128)S(1)}, f32[3,256]{1,0:T(4,128)S(1)}) custom-call(f32[3,5120]{1,0:T(4,128)} %v_ref.3, s32[4,128]{1,0:T(4,128)} %bitcast.2), custom_call_target="tpu_custom_call" | custom-call | bytes 63488 | tf_op jit(solution)/shard_map/pallas_call | solution.py:267
  1.9 3.0 %collective-permute-start = (f32[3,128]{1,0:T(4,128)S(1)}, f32[3,128]{1,0:T(4,128)S(1)}, u32[]{:S(2)}, u32[]{:S(2)}) collective-permute-start(f32[3,128]{1,0:T(4,128)S(1)} %get-tuple-element.16), channel_id=1, source_target_pairs={{0,2},{2,0},{4,6},{6,4},{8,10},{10,8},{12,14},{14,12},{16,18},{18,... | collective-permute-start | bytes 4616 | tf_op jit(solution)/shard_map/ppermute | solution.py:245
  4.9 0.0 copy-start.3
  4.9 0.0 copy-start.1
  4.9 4.5 %collective-permute-start.1 = (f32[3,128]{1,0:T(4,128)S(1)}, f32[3,128]{1,0:T(4,128)S(1)}, u32[]{:S(2)}, u32[]{:S(2)}) collective-permute-start(f32[3,128]{1,0:T(4,128)S(1)} %get-tuple-element.17), channel_id=1, source_target_pairs={{0,30},{2,4},{4,2},{6,8},{8,6},{10,12},{12,10},{14,16},{16,14},{18... | collective-permute-start | bytes 4616 | tf_op jit(solution)/shard_map/ppermute | solution.py:244
  9.4 0.0 copy-start.4
  9.4 0.0 collective-permute-start.2
  9.4 0.0 copy-done
  9.4 0.0 copy-done.3
  9.4 0.0 copy-done.1
  9.4 0.6 %copy-done.4 = f32[64]{0:T(128)S(1)} copy-done((f32[64]{0:T(128)S(1)}, f32[64]{0:T(128)}, u32[]{:S(2)}) %copy-start.4) | copy-done | bytes 280
  10.1 0.0 copy-start.2
  10.1 0.7 %copy-done.2 = s32[1,5120]{1,0:T(1,128)S(1)} copy-done((s32[1,5120]{1,0:T(1,128)S(1)}, s32[1,5120]{1,0:T(1,128)}, u32[]{:S(2)}) %copy-start.2) | copy-done | bytes 20504
  10.8 0.8 %shard_map.69 = (f32[3,40,128]{2,1,0:T(8,128)S(1)}, s32[40,128]{1,0:T(8,128)S(1)}, s32[40,128]{1,0:T(8,128)S(1)}, f32[32,128]{1,0:T(8,128)S(1)}, s32[8,128]{1,0:...) custom-call(f32[3,5120]{1,0:T(4,128)S(1)} %copy-done, s32[4,128]{1,0:T(4,128)S(1)} %bitcast.3, ...), custom_call_target="tpu_custom_call" | custom-call | flops 125829120 | bytes 86272 | tf_op jit(solution)/shard_map/pallas_call | solution.py:267
  11.6 0.0 collective-permute-done.a_ref
  11.6 0.4 %collective-permute-done.1.b_ref = f32[3,128]{1,0:T(4,128)S(1)} collective-permute-done((f32[3,128]{1,0:T(4,128)S(1)}, f32[3,128]{1,0:T(4,128)S(1)}, u32[]{:S(2)}, u32[]{:S(2)}) %collective-permute-start.1) | collective-permute-done | bytes 1568 | tf_op jit(solution)/shard_map/ppermute | solution.py:244
  12.1 0.0 collective-permute-done.2.s_ref
  12.1 1.0 %shard_map.70 = (f32[32,1,128]{2,1,0:T(1,128)S(1)}, f32[1,64]{1,0:T(1,128)}, f32[3,40,128]{2,1,0:T(8,128)S(1)}, f32[3,40,128]{2,1,0:T(8,128)S(1)}) custom-call(f32[3,128]{1,0:T(4,128)S(1)} %collective-permute-done.a_ref, f32[3,128]{1,0:T(4,128)S(1)} %collective-permute-done.1.b_ref, f32[3,256]{1,0:T(4,128)S(1)} %collective-permute-done.2.s_ref, ...), custom_call_target="tpu_custom_call" | custom-call | bytes 190464 | tf_op jit(solution)/shard_map/pallas_call | solution.py:267
  13.1 11.9 %all_to_all.5.got_ref = f32[32,1,128]{2,1,0:T(1,128)S(1)} all-to-all(f32[32,1,128]{2,1,0:T(1,128)S(1)} %get-tuple-element.25), channel_id=1, replica_groups=mesh['slab'=16,'sub'=2] {'slab','sub'}, dimensions={0} | all-to-all | bytes 32768 | tf_op jit(solution)/shard_map/all_to_all | solution.py:304
  25.0 0.8 %shard_map.71 = f32[3,5120]{1,0:T(4,128)} custom-call(f32[32,1,128]{2,1,0:T(1,128)S(1)} %all_to_all.5.got_ref, f32[1,128]{1,0:T(1,128)S(1)} %get-tuple-element.26.target_ref, f32[3,40,128]{2,1,0:T(8,128)S(1)} %get-tuple-element.27.mean_ref, f32[3,40,128]{2,1,0:T(8,128)S(1)} %get-tuple-element.28.turned_ref, s32[40,128]{1,0:T(8,128)S(1)} %get-tuple-element.21.celld_ref), custom_call_target="tpu_custom_call" | custom-call | bytes 160256 | tf_op jit(solution)/shard_map/pallas_call | solution.py:267
Async XLA Ops:
  0.6 8.8 %copy-start = (f32[3,5120]{1,0:T(4,128)S(1)}, f32[3,5120]{1,0:T(4,128)}, u32[]{:S(2)}) copy-start(f32[3,5120]{1,0:T(4,128)} %v_ref.3) | copy-start | bytes 184324
  1.9 9.8 %collective-permute-start = (f32[3,128]{1,0:T(4,128)S(1)}, f32[3,128]{1,0:T(4,128)S(1)}, u32[]{:S(2)}, u32[]{:S(2)}) collective-permute-start(f32[3,128]{1,0:T(4,128)S(1)} %get-tuple-element.16), channel_id=1, source_target_pairs={{0,2},{2,0},{4,6},{6,4},{8,10},{10,8},{12,14},{14,12},{16,18},{18,... | collective-permute-start | bytes 4616 | tf_op jit(solution)/shard_map/ppermute | solution.py:245
  4.9 4.5 %copy-start.3 = (s32[1,512]{1,0:T(1,128)S(1)}, s32[1,512]{1,0:T(1,128)}, u32[]{:S(2)}) copy-start(s32[1,512]{1,0:T(1,128)} %choice_ref.1) | copy-start | bytes 6148
  4.9 4.5 %copy-start.1 = (s32[1,4,128]{2,1,0:T(4,128)S(1)}, s32[1,4,128]{2,1,0:T(4,128)}, u32[]{:S(2)}) copy-start(s32[1,4,128]{2,1,0:T(4,128)} %param.8) | copy-start | bytes 6148
  4.9 7.2 %collective-permute-start.1 = (f32[3,128]{1,0:T(4,128)S(1)}, f32[3,128]{1,0:T(4,128)S(1)}, u32[]{:S(2)}, u32[]{:S(2)}) collective-permute-start(f32[3,128]{1,0:T(4,128)S(1)} %get-tuple-element.17), channel_id=1, source_target_pairs={{0,30},{2,4},{4,2},{6,8},{8,6},{10,12},{12,10},{14,16},{16,14},{18... | collective-permute-start | bytes 4616 | tf_op jit(solution)/shard_map/ppermute | solution.py:244
  9.4 0.7 %copy-start.4 = (f32[64]{0:T(128)S(1)}, f32[64]{0:T(128)}, u32[]{:S(2)}) copy-start(f32[64]{0:T(128)} %param.9) | copy-start | bytes 772
  9.4 2.7 %collective-permute-start.2 = (f32[3,256]{1,0:T(4,128)S(1)}, f32[3,256]{1,0:T(4,128)S(1)}, u32[]{:S(2)}, u32[]{:S(2)}) collective-permute-start(f32[3,256]{1,0:T(4,128)S(1)} %get-tuple-element.18), channel_id=1, source_target_pairs={{0,1},{1,0},{2,3},{3,2},{4,5},{5,4},{6,7},{7,6},{8,9},{9,8},{10,11... | collective-permute-start | bytes 9224 | tf_op jit(solution)/shard_map/ppermute | solution.py:251
  10.1 0.7 %copy-start.2 = (s32[1,5120]{1,0:T(1,128)S(1)}, s32[1,5120]{1,0:T(1,128)}, u32[]{:S(2)}) copy-start(s32[1,5120]{1,0:T(1,128)} %cell_ref.1) | copy-start | bytes 61444

commit v3 on v2

--- a/solution.py
+++ b/solution.py
@@ -7,6 +7,7 @@
 from jax.experimental import pallas as pl
 from jax.experimental.pallas import tpu as pltpu
 from jax.sharding import PartitionSpec as P
+
 
 CX = 1
 CY = 64
@@ -77,14 +78,11 @@
     return lists
 
 
-def departures(v_ref, moves_ref, *out_refs):
+def departures(v_ref, moves_ref, *out_refs, which):
     comps, count = v_ref.shape
     lists = ordered_lists(moves_ref)
-    for index, out_ref, lane in zip(
-        lists,
-        (out_refs[0], out_refs[1], out_refs[2], out_refs[2]),
-        (0, 0, 0, LANES),
-    ):
+    for k, out_ref, lane in zip(which, out_refs[:1] + out_refs[1:] * 2, (0, 0, LANES)):
+        index = lists[k]
         index = jnp.broadcast_to(index, (comps, LANES))
         high, low = index >> 7, index & (LANES - 1)
         out = jnp.zeros((comps, LANES), jnp.float32)
@@ -242,7 +240,8 @@
     even = [(i, i ^ 1) for i in range(size)]
     odd = [(i, (i + 1 if i % 2 else i - 1) % size) for i in range(size)]
     second = lax.ppermute(two, axis, odd)
-    return [lax.ppermute(one, axis, even), second]
+    first = lax.ppermute(one, axis, even)
+    return [first, second]
 
 
 def swap_joined(block, axis):
@@ -279,11 +278,16 @@
     comps, count = speeds.shape
     rows = count // LANES
     blocks = choices.shape[1] // LANES
-    a, b, s = call(
-        departures,
-        (f32(comps, LANES), f32(comps, LANES), f32(comps, 2 * LANES)),
+    (b,) = call(
+        functools.partial(departures, which=(1,)),
+        (f32(comps, LANES),),
         (speeds, moves),
         resident=False,
+    )
+    a, s = call(
+        functools.partial(departures, which=(0, 2, 3)),
+        (f32(comps, LANES), f32(comps, 2 * LANES)),
+        (speeds, moves),
     )
     a, b = swap([a, b], "slab")
     s = swap_joined(s, "sub")

time: 26 us -> 27.7 us (1.065)
  local copies, waits for them, and re-layouts: 1.37 us -> 2.21 us
  waiting for transfers between devices: 0.43 us -> 1.16 us
    unnamed x10 -> x14, local copies, waits for them, and re-layouts: 1.37 us -> 2.21 us
    ppermute x1, waiting for transfers between devices: 0.43 us -> 1.16 us  [swap(): second = lax.ppermute(two, axis, odd)]
    pallas_call x4 -> x5, Pallas kernels: 3.85 us -> 3.87 us  [call(): pl.pallas_call(kernel, out_shape=out_shape, in_specs=[VMEM] * len(inputs)...]
  transfers between devices with their start and end apart: 3 -> 3, of which waited for: 1 -> 1; matrix products, arithmetic and copies ran while one was open for 0% -> 0% of each run, Pallas kernels for 3% -> 7%
where the time goes in v3:
time: 27.7 us; the launch traced here: 27.4 us
  blocking collectives  11.9 us (43%)
  starting transfers between devices  7.63 us (28%)
  Pallas kernels  3.87 us (14%)
  local copies, waits for them, and re-layouts  2.21 us (8%)
  waiting for transfers between devices  1.16 us (4%)
  between operations  0.71 us (3%)
    all_to_all x1, blocking collectives, step(): got = lax.all_to_all(send, AXES, 0, 0, tiled=True)  11.9 us
    ppermute x1, starting transfers between devices, swap(): second = lax.ppermute(two, axis, odd)  4.59 us
    pallas_call x5, Pallas kernels, call(): pl.pallas_call(kernel, out_shape=out_shape, in_specs=[VMEM] * len(inputs)...  3.87 us
    ppermute x1, starting transfers between devices, swap(): first = lax.ppermute(one, axis, even)  3.03 us
    unnamed x14, local copies, waits for them, and re-layouts  2.21 us
    ppermute x1, waiting for transfers between devices, swap(): second = lax.ppermute(two, axis, odd)  1.16 us
  transfers between devices with their start and end apart: 3, of which 1 were waited for; matrix products, arithmetic and copies ran while one was open for 0% of the time, Pallas kernels for 7%

profile of v3, /device:TPU:0, one launch (start us, length us, event | category | flops | bytes accessed | tf_op | source)
XLA Modules:
  0.0 27.4 jit_solution(4600969008040734939)
XLA Ops:
  0.6 0.0 copy-start
  0.6 0.9 %copy-done = f32[3,5120]{1,0:T(4,128)S(1)} copy-done((f32[3,5120]{1,0:T(4,128)S(1)}, f32[3,5120]{1,0:T(4,128)}, u32[]{:S(2)}) %copy-start) | copy-done | bytes 61464
  1.5 0.7 %copy-done.2 = s32[1,4,128]{2,1,0:T(4,128)S(1)} copy-done((s32[1,4,128]{2,1,0:T(4,128)S(1)}, s32[1,4,128]{2,1,0:T(4,128)}, u32[]{:S(2)}) %copy-start.2) | copy-done | bytes 2072
  2.2 0.0 copy-start.1
  2.2 0.2 shard_map.68
  2.4 0.0 copy-start.4
  2.4 3.0 %collective-permute-start = (f32[3,128]{1,0:T(4,128)S(1)}, f32[3,128]{1,0:T(4,128)S(1)}, u32[]{:S(2)}, u32[]{:S(2)}) collective-permute-start(f32[3,128]{1,0:T(4,128)S(1)} %get-tuple-element.15), channel_id=1, source_target_pairs={{0,2},{2,0},{4,6},{6,4},{8,10},{10,8},{12,14},{14,12},{16,18},{18,... | collective-permute-start | bytes 4616 | tf_op jit(solution)/shard_map/ppermute | solution.py:243
  5.5 0.0 copy-start.5
  5.5 1.0 %shard_map.69 = f32[3,128]{1,0:T(4,128)S(1)} custom-call(f32[3,5120]{1,0:T(4,128)} %v_ref.5, s32[4,128]{1,0:T(4,128)} %bitcast.2), custom_call_target="tpu_custom_call" | custom-call | bytes 63488 | tf_op jit(solution)/shard_map/pallas_call | solution.py:266
  6.5 0.0 copy-start.3
  6.5 4.6 %collective-permute-start.1 = (f32[3,128]{1,0:T(4,128)S(1)}, f32[3,128]{1,0:T(4,128)S(1)}, u32[]{:S(2)}, u32[]{:S(2)}) collective-permute-start(f32[3,128]{1,0:T(4,128)S(1)} %shard_map.69), channel_id=1, source_target_pairs={{0,30},{2,4},{4,2},{6,8},{8,6},{10,12},{12,10},{14,16},{16,14},{18... | collective-permute-start | bytes 4616 | tf_op jit(solution)/shard_map/ppermute | solution.py:242
  11.1 0.0 collective-permute-start.2
  11.1 0.0 copy-done.1
  11.1 0.0 copy-done.4
  11.1 0.0 copy-done.5
  11.1 0.0 copy-done.3
  11.1 0.6 %copy-done.6 = f32[64]{0:T(128)S(1)} copy-done((f32[64]{0:T(128)S(1)}, f32[64]{0:T(128)}, u32[]{:S(2)}) %copy-start.6) | copy-done | bytes 280
  11.8 0.8 %shard_map.70 = (f32[3,40,128]{2,1,0:T(8,128)S(1)}, s32[40,128]{1,0:T(8,128)S(1)}, s32[40,128]{1,0:T(8,128)S(1)}, f32[32,128]{1,0:T(8,128)S(1)}, s32[8,128]{1,0:...) custom-call(f32[3,5120]{1,0:T(4,128)S(1)} %copy-done.1, s32[4,128]{1,0:T(4,128)S(1)} %bitcast.4, ...), custom_call_target="tpu_custom_call" | custom-call | flops 125829120 | bytes 86272 | tf_op jit(solution)/shard_map/pallas_call | solution.py:266
  12.6 0.0 collective-permute-done.a_ref
  12.6 1.2 %collective-permute-done.1.b_ref = f32[3,128]{1,0:T(4,128)S(1)} collective-permute-done((f32[3,128]{1,0:T(4,128)S(1)}, f32[3,128]{1,0:T(4,128)S(1)}, u32[]{:S(2)}, u32[]{:S(2)}) %collective-permute-start.1) | collective-permute-done | bytes 1568 | tf_op jit(solution)/shard_map/ppermute | solution.py:242
  13.8 0.0 collective-permute-done.2.s_ref
  13.8 1.0 %shard_map.71 = (f32[32,1,128]{2,1,0:T(1,128)S(1)}, f32[1,64]{1,0:T(1,128)}, f32[3,40,128]{2,1,0:T(8,128)S(1)}, f32[3,40,128]{2,1,0:T(8,128)S(1)}) custom-call(f32[3,128]{1,0:T(4,128)S(1)} %collective-permute-done.a_ref, f32[3,128]{1,0:T(4,128)S(1)} %collective-permute-done.1.b_ref, f32[3,256]{1,0:T(4,128)S(1)} %collective-permute-done.2.s_ref, ...), custom_call_target="tpu_custom_call" | custom-call | bytes 190464 | tf_op jit(solution)/shard_map/pallas_call | solution.py:266
  14.8 11.9 %all_to_all.5.got_ref = f32[32,1,128]{2,1,0:T(1,128)S(1)} all-to-all(f32[32,1,128]{2,1,0:T(1,128)S(1)} %get-tuple-element.23), channel_id=1, replica_groups=mesh['slab'=16,'sub'=2] {'slab','sub'}, dimensions={0} | all-to-all | bytes 32768 | tf_op jit(solution)/shard_map/all_to_all | solution.py:308
  26.6 0.8 %shard_map.72 = f32[3,5120]{1,0:T(4,128)} custom-call(f32[32,1,128]{2,1,0:T(1,128)S(1)} %all_to_all.5.got_ref, f32[1,128]{1,0:T(1,128)S(1)} %get-tuple-element.24.target_ref, f32[3,40,128]{2,1,0:T(8,128)S(1)} %get-tuple-element.25.mean_ref, f32[3,40,128]{2,1,0:T(8,128)S(1)} %get-tuple-element.26.turned_ref, s32[40,128]{1,0:T(8,128)S(1)} %get-tuple-element.19.celld_ref), custom_call_target="tpu_custom_call" | custom-call | bytes 160256 | tf_op jit(solution)/shard_map/pallas_call | solution.py:266
  (2 shorter events, 0.0 us)
Async XLA Ops:
  0.6 0.9 %copy-start = (f32[3,5120]{1,0:T(4,128)S(1)}, f32[3,5120]{1,0:T(4,128)}, u32[]{:S(2)}) copy-start(f32[3,5120]{1,0:T(4,128)} %v_ref.5) | copy-start | bytes 184324
  1.5 0.7 %copy-start.2 = (s32[1,4,128]{2,1,0:T(4,128)S(1)}, s32[1,4,128]{2,1,0:T(4,128)}, u32[]{:S(2)}) copy-start(s32[1,4,128]{2,1,0:T(4,128)} %param.8) | copy-start | bytes 6148
  2.2 8.9 %copy-start.1 = (f32[3,5120]{1,0:T(4,128)S(1)}, f32[3,5120]{1,0:T(4,128)}, u32[]{:S(2)}) copy-start(f32[3,5120]{1,0:T(4,128)} %v_ref.5) | copy-start | bytes 184324
  2.4 8.7 %copy-start.4 = (s32[1,5120]{1,0:T(1,128)S(1)}, s32[1,5120]{1,0:T(1,128)}, u32[]{:S(2)}) copy-start(s32[1,5120]{1,0:T(1,128)} %cell_ref.1) | copy-start | bytes 61444
  2.4 10.2 %collective-permute-start = (f32[3,128]{1,0:T(4,128)S(1)}, f32[3,128]{1,0:T(4,128)S(1)}, u32[]{:S(2)}, u32[]{:S(2)}) collective-permute-start(f32[3,128]{1,0:T(4,128)S(1)} %get-tuple-element.15), channel_id=1, source_target_pairs={{0,2},{2,0},{4,6},{6,4},{8,10},{10,8},{12,14},{14,12},{16,18},{18,... | collective-permute-start | bytes 4616 | tf_op jit(solution)/shard_map/ppermute | solution.py:243
  5.5 5.6 %copy-start.5 = (s32[1,512]{1,0:T(1,128)S(1)}, s32[1,512]{1,0:T(1,128)}, u32[]{:S(2)}) copy-start(s32[1,512]{1,0:T(1,128)} %choice_ref.1) | copy-start | bytes 6148
  6.5 4.6 %copy-start.3 = (s32[1,4,128]{2,1,0:T(4,128)S(1)}, s32[1,4,128]{2,1,0:T(4,128)}, u32[]{:S(2)}) copy-start(s32[1,4,128]{2,1,0:T(4,128)} %param.8) | copy-start | bytes 6148
  6.5 7.2 %collective-permute-start.1 = (f32[3,128]{1,0:T(4,128)S(1)}, f32[3,128]{1,0:T(4,128)S(1)}, u32[]{:S(2)}, u32[]{:S(2)}) collective-permute-start(f32[3,128]{1,0:T(4,128)S(1)} %shard_map.69), channel_id=1, source_target_pairs={{0,30},{2,4},{4,2},{6,8},{8,6},{10,12},{12,10},{14,16},{16,14},{18... | collective-permute-start | bytes 4616 | tf_op jit(solution)/shard_map/ppermute | solution.py:242
  11.1 0.7 %copy-start.6 = (f32[64]{0:T(128)S(1)}, f32[64]{0:T(128)}, u32[]{:S(2)}) copy-start(f32[64]{0:T(128)} %param.9) | copy-start | bytes 772
  11.1 2.7 %collective-permute-start.2 = (f32[3,256]{1,0:T(4,128)S(1)}, f32[3,256]{1,0:T(4,128)S(1)}, u32[]{:S(2)}, u32[]{:S(2)}) collective-permute-start(f32[3,256]{1,0:T(4,128)S(1)} %get-tuple-element.16), channel_id=1, source_target_pairs={{0,1},{1,0},{2,3},{3,2},{4,5},{5,4},{6,7},{7,6},{8,9},{9,8},{10,11... | collective-permute-start | bytes 9224 | tf_op jit(solution)/shard_map/ppermute | solution.py:250

commit v4 on v3

--- a/solution.py
+++ b/solution.py
@@ -78,17 +78,39 @@
     return lists
 
 
-def departures(v_ref, moves_ref, *out_refs, which):
+def chunks(count):
+    size = SUBLANES * LANES if count % (SUBLANES * LANES) == 0 else LANES
+    return [(k, pl.ds(k * size, size), range(k * size // LANES, (k + 1) * size // LANES)) for k in range(count // size)]
+
+
+def first_departure(v_hbm, moves_hbm, out_ref, v_ref, moves_ref, sems):
+    parts = chunks(v_ref.shape[1])
+    copies = [pltpu.make_async_copy(moves_hbm, moves_ref, sems.at[len(parts)])]
+    copies += [pltpu.make_async_copy(v_hbm.at[:, span], v_ref.at[:, span], sems.at[k]) for k, span, _ in parts]
+    for copy in copies:
+        copy.start()
+    copies[0].wait()
+    index = ordered_lists(moves_ref)[1]
+    comps = v_ref.shape[0]
+    index = jnp.broadcast_to(index, (comps, LANES))
+    high, low = index >> 7, index & (LANES - 1)
+    out = jnp.zeros((comps, LANES), jnp.float32)
+    for copy, (_, _, rows) in zip(copies[1:], parts):
+        copy.wait()
+        for r in rows:
+            out = jnp.where(high == r, take(v_ref[:, r * LANES : (r + 1) * LANES], low), out)
+    out_ref[...] = out
+
+
+def other_departures(v_ref, moves_ref, a_ref, s_ref):
     comps, count = v_ref.shape
     lists = ordered_lists(moves_ref)
-    for k, out_ref, lane in zip(which, out_refs[:1] + out_refs[1:] * 2, (0, 0, LANES)):
-        index = lists[k]
-        index = jnp.broadcast_to(index, (comps, LANES))
+    for k, out_ref, lane in ((0, a_ref, 0), (2, s_ref, 0), (3, s_ref, LANES)):
+        index = jnp.broadcast_to(lists[k], (comps, LANES))
         high, low = index >> 7, index & (LANES - 1)
         out = jnp.zeros((comps, LANES), jnp.float32)
         for r in range(count // LANES):
-            tile = v_ref[:, r * LANES : (r + 1) * LANES]
-            out = jnp.where(high == r, take(tile, low), out)
+            out = jnp.where(high == r, take(v_ref[:, r * LANES : (r + 1) * LANES], low), out)
         out_ref[:, lane : lane + LANES] = out
 
 
@@ -210,8 +232,11 @@
         turned_ref[c] = relative[c] * ROT_COS + cross * ROT_SIN + n[c] * along
 
 
-def finish(got_ref, target_ref, mean_ref, turned_ref, celld_ref, out_ref, *, slabs, subs, particles):
-    comps, rows, _ = mean_ref.shape
+def finish(got_ref, target_ref, profile_ref, mean_ref, turned_ref, celld_ref, out_hbm, profile_hbm, out_ref, sems, *, slabs, subs, particles):
+    comps, _, _ = mean_ref.shape
+    parts = chunks(out_ref.shape[1])
+    copies = [pltpu.make_async_copy(profile_ref, profile_hbm, sems.at[len(parts)])]
+    copies[0].start()
     got = got_ref[...].reshape(slabs * subs, LANES)
     mine = lax.rem(iota(got.shape, 0), subs) == lax.axis_index("sub")
     lane = iota(got.shape, 1)
@@ -219,15 +244,22 @@
     work = jnp.sum(jnp.where(lane < CY, 0.0, got), 0, keepdims=True)
     work = jnp.sum(work, 1, keepdims=True)
     scale = lax.rsqrt(work / (3.0 * particles * RESERVOIR_HEAT) + 1e-06)
-    scale = jnp.broadcast_to(scale, (rows, LANES))
     extra = FEEDBACK * (target_ref[...] - drift)
-    line = (celld_ref[...] // CZ) & (CY - 1)
-    extra = take(jnp.broadcast_to(extra, (rows, LANES)), line)
-    for c in range(comps):
-        base = mean_ref[c] + extra if c == 0 else mean_ref[c]
-        out = base + scale * turned_ref[c]
-        for r in range(rows):
-            out_ref[c : c + 1, r * LANES : (r + 1) * LANES] = out[r : r + 1, :]
+    for k, span, own in parts:
+        own = slice(own.start, own.stop)
+        shape = (own.stop - own.start, LANES)
+        line = (celld_ref[own, :] // CZ) & (CY - 1)
+        shift = take(jnp.broadcast_to(extra, shape), line)
+        for c in range(comps):
+            base = mean_ref[c, own, :] + shift if c == 0 else mean_ref[c, own, :]
+            out = base + scale * turned_ref[c, own, :]
+            for r in range(shape[0]):
+                lanes = slice((own.start + r) * LANES, (own.start + r + 1) * LANES)
+                out_ref[c : c + 1, lanes] = out[r : r + 1, :]
+        copies.append(pltpu.make_async_copy(out_ref.at[:, span], out_hbm.at[:, span], sems.at[k]))
+        copies[-1].start()
+    for copy in copies:
+        copy.wait()
 
 
 def swap(blocks, axis):
@@ -261,13 +293,16 @@
 
 def call(kernel, out_shape, inputs, scratch=(), flops=0, resident=True):
     size = sum(4 * math.prod(x.shape) for x in inputs)
+    place = VMEM
     if resident:
         inputs = [pltpu.with_memory_space_constraint(x, pltpu.VMEM) for x in inputs]
+    else:
+        place = pl.BlockSpec(memory_space=pl.ANY)
     return pl.pallas_call(
         kernel,
         out_shape=out_shape,
-        in_specs=[VMEM] * len(inputs),
-        out_specs=jax.tree.map(lambda _: VMEM, out_shape),
+        in_specs=[place] * len(inputs),
+        out_specs=jax.tree.map(lambda x: VMEM if isinstance(x, pl.MemoryRef) else pl.BlockSpec(memory_space=pl.ANY), out_shape),
         scratch_shapes=list(scratch),
         cost_estimate=pl.CostEstimate(flops=flops, bytes_accessed=size, transcendentals=0),
     )(*inputs)
@@ -278,14 +313,16 @@
     comps, count = speeds.shape
     rows = count // LANES
     blocks = choices.shape[1] // LANES
-    (b,) = call(
-        functools.partial(departures, which=(1,)),
-        (f32(comps, LANES),),
+    many = len(chunks(count)) + 1
+    b = call(
+        first_departure,
+        f32(comps, LANES),
         (speeds, moves),
+        scratch=[pltpu.VMEM(speeds.shape, jnp.float32), pltpu.VMEM(moves.shape, jnp.int32), pltpu.SemaphoreType.DMA((many,))],
         resident=False,
     )
     a, s = call(
-        functools.partial(departures, which=(0, 2, 3)),
+        other_departures,
         (f32(comps, LANES), f32(comps, 2 * LANES)),
         (speeds, moves),
     )
@@ -302,16 +339,16 @@
     )
     send, profile, mean, turned = call(
         relax,
-        (f32(slabs * subs, 1, LANES), jax.ShapeDtypeStruct((1, CX * CY), jnp.float32), dense, dense),
+        (f32(slabs * subs, 1, LANES), f32(1, CX * CY), dense, dense),
         (a, b, s, vd, source, celld, base, slotcell, normal),
     )
     got = lax.all_to_all(send, AXES, 0, 0, tiled=True)
-    out = call(
+    return call(
         functools.partial(finish, slabs=slabs, subs=subs, particles=count * slabs * subs),
-        jax.ShapeDtypeStruct((comps, count), jnp.float32),
-        (got, target, mean, turned, celld),
-    )
-    return out, profile
+        (jax.ShapeDtypeStruct((comps, count), jnp.float32), jax.ShapeDtypeStruct((1, CX * CY), jnp.float32)),
+        (got, target, profile, mean, turned, celld),
+        scratch=[pltpu.VMEM((comps, count), jnp.float32), pltpu.SemaphoreType.DMA((many,))],
+    )
 
 
 def body(velocities, cell_index, axis_choice, moves, shear_target):

time: 27.7 us -> 27.5 us (level)
  no operation moved by 1% of the time
where the time goes in v4:
time: 27.5 us; the launch traced here: 27.2 us
  blocking collectives  11.9 us (43%)
  starting transfers between devices  7.63 us (28%)
  Pallas kernels  3.63 us (13%)
  local copies, waits for them, and re-layouts  2.21 us (8%)
  waiting for transfers between devices  1.16 us (4%)
  between operations  0.72 us (3%)
    all_to_all x1, blocking collectives, step(): got = lax.all_to_all(send, AXES, 0, 0, tiled=True)  11.9 us
    ppermute x1, starting transfers between devices, swap(): second = lax.ppermute(two, axis, odd)  4.59 us
    pallas_call x5, Pallas kernels, call(): pl.pallas_call(kernel, out_shape=out_shape, in_specs=[place] * len(inputs...  3.63 us
    ppermute x1, starting transfers between devices, swap(): first = lax.ppermute(one, axis, even)  3.03 us
    unnamed x14, local copies, waits for them, and re-layouts  2.21 us
    ppermute x1, waiting for transfers between devices, swap(): second = lax.ppermute(two, axis, odd)  1.16 us
  transfers between devices with their start and end apart: 3, of which 1 were waited for; matrix products, arithmetic and copies ran while one was open for 0% of the time, Pallas kernels for 7%

profile of v4, /device:TPU:0, one launch (start us, length us, event | category | flops | bytes accessed | tf_op | source)
XLA Modules:
  0.0 27.2 jit_solution(9087172985425526262)
XLA Ops:
  0.6 0.0 copy-start
  0.6 0.9 %copy-done = f32[3,5120]{1,0:T(4,128)S(1)} copy-done((f32[3,5120]{1,0:T(4,128)S(1)}, f32[3,5120]{1,0:T(4,128)}, u32[]{:S(2)}) %copy-start) | copy-done | bytes 61464
  1.5 0.7 %copy-done.2 = s32[1,4,128]{2,1,0:T(4,128)S(1)} copy-done((s32[1,4,128]{2,1,0:T(4,128)S(1)}, s32[1,4,128]{2,1,0:T(4,128)}, u32[]{:S(2)}) %copy-start.2) | copy-done | bytes 2072
  2.2 0.0 copy-start.1
  2.2 0.2 shard_map.68
  2.4 0.0 copy-start.4
  2.4 3.0 %collective-permute-start = (f32[3,128]{1,0:T(4,128)S(1)}, f32[3,128]{1,0:T(4,128)S(1)}, u32[]{:S(2)}, u32[]{:S(2)}) collective-permute-start(f32[3,128]{1,0:T(4,128)S(1)} %get-tuple-element.15), channel_id=1, source_target_pairs={{0,2},{2,0},{4,6},{6,4},{8,10},{10,8},{12,14},{14,12},{16,18},{18,... | collective-permute-start | bytes 4616 | tf_op jit(solution)/shard_map/ppermute | solution.py:275
  5.5 0.0 copy-start.5
  5.5 1.2 %shard_map.69 = f32[3,128]{1,0:T(4,128)S(1)} custom-call(f32[3,5120]{1,0:T(4,128)} %v_ref.3, s32[4,128]{1,0:T(4,128)} %bitcast.2), custom_call_target="tpu_custom_call" | custom-call | bytes 63488 | tf_op jit(solution)/shard_map/pallas_call | solution.py:301
  6.7 0.0 copy-start.3
  6.7 4.6 %collective-permute-start.1 = (f32[3,128]{1,0:T(4,128)S(1)}, f32[3,128]{1,0:T(4,128)S(1)}, u32[]{:S(2)}, u32[]{:S(2)}) collective-permute-start(f32[3,128]{1,0:T(4,128)S(1)} %shard_map.69), channel_id=1, source_target_pairs={{0,30},{2,4},{4,2},{6,8},{8,6},{10,12},{12,10},{14,16},{16,14},{18... | collective-permute-start | bytes 4616 | tf_op jit(solution)/shard_map/ppermute | solution.py:274
  11.3 0.0 collective-permute-start.2
  11.3 0.0 copy-done.1
  11.3 0.0 copy-done.4
  11.3 0.0 copy-done.5
  11.3 0.0 copy-done.3
  11.3 0.6 %copy-done.6 = f32[64]{0:T(128)S(1)} copy-done((f32[64]{0:T(128)S(1)}, f32[64]{0:T(128)}, u32[]{:S(2)}) %copy-start.6) | copy-done | bytes 280
  11.9 0.8 %shard_map.70 = (f32[3,40,128]{2,1,0:T(8,128)S(1)}, s32[40,128]{1,0:T(8,128)S(1)}, s32[40,128]{1,0:T(8,128)S(1)}, f32[32,128]{1,0:T(8,128)S(1)}, s32[8,128]{1,0:...) custom-call(f32[3,5120]{1,0:T(4,128)S(1)} %copy-done.1, s32[4,128]{1,0:T(4,128)S(1)} %bitcast.4, ...), custom_call_target="tpu_custom_call" | custom-call | flops 125829120 | bytes 86272 | tf_op jit(solution)/shard_map/pallas_call | solution.py:301
  12.8 0.0 collective-permute-done.a_ref
  12.8 1.2 %collective-permute-done.1.b_ref = f32[3,128]{1,0:T(4,128)S(1)} collective-permute-done((f32[3,128]{1,0:T(4,128)S(1)}, f32[3,128]{1,0:T(4,128)S(1)}, u32[]{:S(2)}, u32[]{:S(2)}) %collective-permute-start.1) | collective-permute-done | bytes 1568 | tf_op jit(solution)/shard_map/ppermute | solution.py:274
  13.9 0.0 collective-permute-done.2.s_ref
  13.9 0.6 %shard_map.71 = (f32[32,1,128]{2,1,0:T(1,128)S(1)}, f32[1,64]{1,0:T(1,128)S(1)}, f32[3,40,128]{2,1,0:T(8,128)S(1)}, f32[3,40,128]{2,1,0:T(8,128)S(1)}) custom-call(f32[3,128]{1,0:T(4,128)S(1)} %collective-permute-done.a_ref, f32[3,128]{1,0:T(4,128)S(1)} %collective-permute-done.1.b_ref, f32[3,256]{1,0:T(4,128)S(1)} %collective-permute-done.2.s_ref, ...), custom_call_target="tpu_custom_call" | custom-call | bytes 190464 | tf_op jit(solution)/shard_map/pallas_call | solution.py:301
  14.5 11.9 %all_to_all.5.got_ref = f32[32,1,128]{2,1,0:T(1,128)S(1)} all-to-all(f32[32,1,128]{2,1,0:T(1,128)S(1)} %get-tuple-element.23), channel_id=1, replica_groups=mesh['slab'=16,'sub'=2] {'slab','sub'}, dimensions={0} | all-to-all | bytes 32768 | tf_op jit(solution)/shard_map/all_to_all | solution.py:345
  26.4 0.8 %shard_map.72 = (f32[3,5120]{1,0:T(4,128)}, f32[1,64]{1,0:T(1,128)}) custom-call(f32[32,1,128]{2,1,0:T(1,128)S(1)} %all_to_all.5.got_ref, f32[1,128]{1,0:T(1,128)S(1)} %get-tuple-element.24.target_ref, f32[1,64]{1,0:T(1,128)S(1)} %get-tuple-element.25.profile_ref, f32[3,40,128]{2,1,0:T(8,128)S(1)} %get-tuple-element.26.mean_ref, ...), custom_call_target="tpu_custom_call" | custom-call | bytes 160512 | tf_op jit(solution)/shard_map/pallas_call | solution.py:301
  (2 shorter events, 0.0 us)
Async XLA Ops:
  0.6 0.9 %copy-start = (f32[3,5120]{1,0:T(4,128)S(1)}, f32[3,5120]{1,0:T(4,128)}, u32[]{:S(2)}) copy-start(f32[3,5120]{1,0:T(4,128)} %v_ref.3) | copy-start | bytes 184324
  1.5 0.7 %copy-start.2 = (s32[1,4,128]{2,1,0:T(4,128)S(1)}, s32[1,4,128]{2,1,0:T(4,128)}, u32[]{:S(2)}) copy-start(s32[1,4,128]{2,1,0:T(4,128)} %param.8) | copy-start | bytes 6148
  2.2 9.1 %copy-start.1 = (f32[3,5120]{1,0:T(4,128)S(1)}, f32[3,5120]{1,0:T(4,128)}, u32[]{:S(2)}) copy-start(f32[3,5120]{1,0:T(4,128)} %v_ref.3) | copy-start | bytes 184324
  2.4 8.9 %copy-start.4 = (s32[1,5120]{1,0:T(1,128)S(1)}, s32[1,5120]{1,0:T(1,128)}, u32[]{:S(2)}) copy-start(s32[1,5120]{1,0:T(1,128)} %cell_ref.1) | copy-start | bytes 61444
  2.4 10.3 %collective-permute-start = (f32[3,128]{1,0:T(4,128)S(1)}, f32[3,128]{1,0:T(4,128)S(1)}, u32[]{:S(2)}, u32[]{:S(2)}) collective-permute-start(f32[3,128]{1,0:T(4,128)S(1)} %get-tuple-element.15), channel_id=1, source_target_pairs={{0,2},{2,0},{4,6},{6,4},{8,10},{10,8},{12,14},{14,12},{16,18},{18,... | collective-permute-start | bytes 4616 | tf_op jit(solution)/shard_map/ppermute | solution.py:275
  5.5 5.8 %copy-start.5 = (s32[1,512]{1,0:T(1,128)S(1)}, s32[1,512]{1,0:T(1,128)}, u32[]{:S(2)}) copy-start(s32[1,512]{1,0:T(1,128)} %choice_ref.1) | copy-start | bytes 6148
  6.7 4.6 %copy-start.3 = (s32[1,4,128]{2,1,0:T(4,128)S(1)}, s32[1,4,128]{2,1,0:T(4,128)}, u32[]{:S(2)}) copy-start(s32[1,4,128]{2,1,0:T(4,128)} %param.8) | copy-start | bytes 6148
  6.7 7.2 %collective-permute-start.1 = (f32[3,128]{1,0:T(4,128)S(1)}, f32[3,128]{1,0:T(4,128)S(1)}, u32[]{:S(2)}, u32[]{:S(2)}) collective-permute-start(f32[3,128]{1,0:T(4,128)S(1)} %shard_map.69), channel_id=1, source_target_pairs={{0,30},{2,4},{4,2},{6,8},{8,6},{10,12},{12,10},{14,16},{16,14},{18... | collective-permute-start | bytes 4616 | tf_op jit(solution)/shard_map/ppermute | solution.py:274
  11.3 0.7 %copy-start.6 = (f32[64]{0:T(128)S(1)}, f32[64]{0:T(128)}, u32[]{:S(2)}) copy-start(f32[64]{0:T(128)} %param.9) | copy-start | bytes 772
  11.3 2.7 %collective-permute-start.2 = (f32[3,256]{1,0:T(4,128)S(1)}, f32[3,256]{1,0:T(4,128)S(1)}, u32[]{:S(2)}, u32[]{:S(2)}) collective-permute-start(f32[3,256]{1,0:T(4,128)S(1)} %get-tuple-element.16), channel_id=1, source_target_pairs={{0,1},{1,0},{2,3},{3,2},{4,5},{5,4},{6,7},{7,6},{8,9},{9,8},{10,11... | collective-permute-start | bytes 9224 | tf_op jit(solution)/shard_map/ppermute | solution.py:282

commit v5 on v4

--- a/solution.py
+++ b/solution.py
@@ -83,11 +83,13 @@
     return [(k, pl.ds(k * size, size), range(k * size // LANES, (k + 1) * size // LANES)) for k in range(count // size)]
 
 
-def first_departure(v_hbm, moves_hbm, out_ref, v_ref, moves_ref, sems):
+def first_departure(v_hbm, moves_hbm, cell_hbm, choice_hbm, shear_hbm, out_ref, v_ref, moves_ref, cell_ref, choice_ref, shear_ref, sems):
     parts = chunks(v_ref.shape[1])
     copies = [pltpu.make_async_copy(moves_hbm, moves_ref, sems.at[len(parts)])]
     copies += [pltpu.make_async_copy(v_hbm.at[:, span], v_ref.at[:, span], sems.at[k]) for k, span, _ in parts]
-    for copy in copies:
+    pairs = ((cell_hbm, cell_ref), (choice_hbm, choice_ref), (shear_hbm, shear_ref))
+    others = [pltpu.make_async_copy(x, y, sems.at[len(parts) + 1 + k]) for k, (x, y) in enumerate(pairs)]
+    for copy in copies + others:
         copy.start()
     copies[0].wait()
     index = ordered_lists(moves_ref)[1]
@@ -100,6 +102,8 @@
         for r in rows:
             out = jnp.where(high == r, take(v_ref[:, r * LANES : (r + 1) * LANES], low), out)
     out_ref[...] = out
+    for copy in others:
+        copy.wait()
 
 
 def other_departures(v_ref, moves_ref, a_ref, s_ref):
@@ -314,11 +318,12 @@
     rows = count // LANES
     blocks = choices.shape[1] // LANES
     many = len(chunks(count)) + 1
-    b = call(
+    given = (speeds, moves, cells, choices, shear_target[None, :])
+    b, speeds, moves, cells, choices, shear_target = call(
         first_departure,
-        f32(comps, LANES),
-        (speeds, moves),
-        scratch=[pltpu.VMEM(speeds.shape, jnp.float32), pltpu.VMEM(moves.shape, jnp.int32), pltpu.SemaphoreType.DMA((many,))],
+        (f32(comps, LANES), *(pltpu.VMEM(x.shape, x.dtype) for x in given)),
+        given,
+        scratch=[pltpu.SemaphoreType.DMA((many + 3,))],
         resident=False,
     )
     a, s = call(
@@ -333,7 +338,7 @@
     vd, source, celld, base, slotcell, normal, target = call(
         prepare,
         (dense, index, index, f32(blocks * SUBLANES, LANES), i32(SUBLANES, LANES), dense, f32(1, LANES)),
-        (speeds, moves, cells, choices, shear_target[None, :]),
+        (speeds, moves, cells, choices, shear_target),
         scratch=[pltpu.VMEM((rows, LANES), jnp.float32)],
         flops=2 * count * LANES * 96,
     )

time: 27.5 us -> 25.8 us (0.938)
  local copies, waits for them, and re-layouts: 2.21 us -> 0 us
  waiting for transfers between devices: 1.16 us -> 1.82 us
    unnamed x14 -> x0, local copies, waits for them, and re-layouts: 2.21 us -> none
    ppermute x1, waiting for transfers between devices: 1.16 us -> 1.81 us  [swap(): second = lax.ppermute(two, axis, odd)]
  transfers between devices with their start and end apart: 3 -> 3, of which waited for: 1 -> 1; matrix products, arithmetic and copies ran while one was open for 0% -> 0% of each run, Pallas kernels for 7% -> 3%
where the time goes in v5:
time: 25.8 us; the launch traced here: 25.6 us
  blocking collectives  11.9 us (46%)
  starting transfers between devices  7.56 us (29%)
  Pallas kernels  3.65 us (14%)
  waiting for transfers between devices  1.82 us (7%)
  between operations  0.67 us (3%)
    all_to_all x1, blocking collectives, step(): got = lax.all_to_all(send, AXES, 0, 0, tiled=True)  11.9 us
    ppermute x1, starting transfers between devices, swap(): second = lax.ppermute(two, axis, odd)  4.53 us
    pallas_call x5, Pallas kernels, call(): pl.pallas_call(kernel, out_shape=out_shape, in_specs=[place] * len(inputs...  3.65 us
    ppermute x1, starting transfers between devices, swap(): first = lax.ppermute(one, axis, even)  3.03 us
    ppermute x1, waiting for transfers between devices, swap(): second = lax.ppermute(two, axis, odd)  1.81 us
  transfers between devices with their start and end apart: 3, of which 1 were waited for; matrix products, arithmetic and copies ran while one was open for 0% of the time, Pallas kernels for 3%

profile of v5, /device:TPU:0, one launch (start us, length us, event | category | flops | bytes accessed | tf_op | source)
XLA Modules:
  0.0 25.6 jit_solution(5730682010827255960)
XLA Ops:
  0.6 1.2 %shard_map.68 = (f32[3,128]{1,0:T(4,128)S(1)}, f32[3,5120]{1,0:T(4,128)S(1)}, s32[4,128]{1,0:T(4,128)S(1)}, s32[1,5120]{1,0:T(1,128)S(1)}, s32[1,512]{1,0:T(1,128)S(1)}, /*index=5*/f32[1,64]{1,0:T(1,128)S(1)}) custom-call(f32[3,5120]{1,0:T(4,128)} %v_hbm.1, s32[4,128]{1,0:T(4,128)} %bitcast.2, s32[1,5120]{1,0:T(1,128)} %cell_hbm.1, s32[1,512]{1,0:T(1,128)} %choice_hbm.1, ...), custom_call_target="tpu_custom_call" | custom-call | bytes 86272 | tf_op jit(solution)/shard_map/pallas_call | solution.py:305
  1.8 0.2 shard_map.69
  2.1 3.0 %collective-permute-start = (f32[3,128]{1,0:T(4,128)S(1)}, f32[3,128]{1,0:T(4,128)S(1)}, u32[]{:S(2)}, u32[]{:S(2)}) collective-permute-start(f32[3,128]{1,0:T(4,128)S(1)} %get-tuple-element.23), channel_id=1, source_target_pairs={{0,2},{2,0},{4,6},{6,4},{8,10},{10,8},{12,14},{14,12},{16,18},{18,... | collective-permute-start | bytes 4616 | tf_op jit(solution)/shard_map/ppermute | solution.py:279
  5.1 4.5 %collective-permute-start.1 = (f32[3,128]{1,0:T(4,128)S(1)}, f32[3,128]{1,0:T(4,128)S(1)}, u32[]{:S(2)}, u32[]{:S(2)}) collective-permute-start(f32[3,128]{1,0:T(4,128)S(1)} %get-tuple-element.24), channel_id=1, source_target_pairs={{0,30},{2,4},{4,2},{6,8},{8,6},{10,12},{12,10},{14,16},{16,14},{18... | collective-permute-start | bytes 4616 | tf_op jit(solution)/shard_map/ppermute | solution.py:278
  9.6 0.0 collective-permute-start.2
  9.6 0.8 %shard_map.70 = (f32[3,40,128]{2,1,0:T(8,128)S(1)}, s32[40,128]{1,0:T(8,128)S(1)}, s32[40,128]{1,0:T(8,128)S(1)}, f32[32,128]{1,0:T(8,128)S(1)}, s32[8,128]{1,0:...) custom-call(f32[3,5120]{1,0:T(4,128)S(1)} %get-tuple-element.21.v_ref, ...), custom_call_target="tpu_custom_call" | custom-call | flops 125829120 | bytes 86272 | tf_op jit(solution)/shard_map/pallas_call | solution.py:305
  10.5 0.0 collective-permute-done.a_ref
  10.5 1.8 %collective-permute-done.1.b_ref = f32[3,128]{1,0:T(4,128)S(1)} collective-permute-done((f32[3,128]{1,0:T(4,128)S(1)}, f32[3,128]{1,0:T(4,128)S(1)}, u32[]{:S(2)}, u32[]{:S(2)}) %collective-permute-start.1) | collective-permute-done | bytes 1568 | tf_op jit(solution)/shard_map/ppermute | solution.py:278
  12.3 0.0 collective-permute-done.2.s_ref
  12.3 0.6 %shard_map.71 = (f32[32,1,128]{2,1,0:T(1,128)S(1)}, f32[1,64]{1,0:T(1,128)S(1)}, f32[3,40,128]{2,1,0:T(8,128)S(1)}, f32[3,40,128]{2,1,0:T(8,128)S(1)}) custom-call(f32[3,128]{1,0:T(4,128)S(1)} %collective-permute-done.a_ref, f32[3,128]{1,0:T(4,128)S(1)} %collective-permute-done.1.b_ref, f32[3,256]{1,0:T(4,128)S(1)} %collective-permute-done.2.s_ref, ...), custom_call_target="tpu_custom_call" | custom-call | bytes 190464 | tf_op jit(solution)/shard_map/pallas_call | solution.py:305
  12.9 11.9 %all_to_all.5.got_ref = f32[32,1,128]{2,1,0:T(1,128)S(1)} all-to-all(f32[32,1,128]{2,1,0:T(1,128)S(1)} %get-tuple-element.35), channel_id=1, replica_groups=mesh['slab'=16,'sub'=2] {'slab','sub'}, dimensions={0} | all-to-all | bytes 32768 | tf_op jit(solution)/shard_map/all_to_all | solution.py:350
  24.8 0.8 %shard_map.72 = (f32[3,5120]{1,0:T(4,128)}, f32[1,64]{1,0:T(1,128)}) custom-call(f32[32,1,128]{2,1,0:T(1,128)S(1)} %all_to_all.5.got_ref, f32[1,128]{1,0:T(1,128)S(1)} %get-tuple-element.36.target_ref, f32[1,64]{1,0:T(1,128)S(1)} %get-tuple-element.37.profile_ref, f32[3,40,128]{2,1,0:T(8,128)S(1)} %get-tuple-element.38.mean_ref, ...), custom_call_target="tpu_custom_call" | custom-call | bytes 160512 | tf_op jit(solution)/shard_map/pallas_call | solution.py:305
Async XLA Ops:
  2.1 8.4 %collective-permute-start = (f32[3,128]{1,0:T(4,128)S(1)}, f32[3,128]{1,0:T(4,128)S(1)}, u32[]{:S(2)}, u32[]{:S(2)}) collective-permute-start(f32[3,128]{1,0:T(4,128)S(1)} %get-tuple-element.23), channel_id=1, source_target_pairs={{0,2},{2,0},{4,6},{6,4},{8,10},{10,8},{12,14},{14,12},{16,18},{18,... | collective-permute-start | bytes 4616 | tf_op jit(solution)/shard_map/ppermute | solution.py:279
  5.1 7.2 %collective-permute-start.1 = (f32[3,128]{1,0:T(4,128)S(1)}, f32[3,128]{1,0:T(4,128)S(1)}, u32[]{:S(2)}, u32[]{:S(2)}) collective-permute-start(f32[3,128]{1,0:T(4,128)S(1)} %get-tuple-element.24), channel_id=1, source_target_pairs={{0,30},{2,4},{4,2},{6,8},{8,6},{10,12},{12,10},{14,16},{16,14},{18... | collective-permute-start | bytes 4616 | tf_op jit(solution)/shard_map/ppermute | solution.py:278
  9.6 2.7 %collective-permute-start.2 = (f32[3,256]{1,0:T(4,128)S(1)}, f32[3,256]{1,0:T(4,128)S(1)}, u32[]{:S(2)}, u32[]{:S(2)}) collective-permute-start(f32[3,256]{1,0:T(4,128)S(1)} %get-tuple-element.25), channel_id=1, source_target_pairs={{0,1},{1,0},{2,3},{3,2},{4,5},{5,4},{6,7},{7,6},{8,9},{9,8},{10,11... | collective-permute-start | bytes 9224 | tf_op jit(solution)/shard_map/ppermute | solution.py:286

commit v6 on v4

--- a/solution.py
+++ b/solution.py
@@ -78,13 +78,15 @@
     return lists
 
 
-def chunks(count):
-    size = SUBLANES * LANES if count % (SUBLANES * LANES) == 0 else LANES
-    return [(k, pl.ds(k * size, size), range(k * size // LANES, (k + 1) * size // LANES)) for k in range(count // size)]
+def chunks(count, pieces):
+    rows = count // LANES
+    pieces = math.gcd(pieces, rows)
+    size = rows // pieces
+    return [(k, pl.ds(k * size * LANES, size * LANES), range(k * size, (k + 1) * size)) for k in range(pieces)]
 
 
 def first_departure(v_hbm, moves_hbm, out_ref, v_ref, moves_ref, sems):
-    parts = chunks(v_ref.shape[1])
+    parts = chunks(v_ref.shape[1], 2)
     copies = [pltpu.make_async_copy(moves_hbm, moves_ref, sems.at[len(parts)])]
     copies += [pltpu.make_async_copy(v_hbm.at[:, span], v_ref.at[:, span], sems.at[k]) for k, span, _ in parts]
     for copy in copies:
@@ -234,7 +236,7 @@
 
 def finish(got_ref, target_ref, profile_ref, mean_ref, turned_ref, celld_ref, out_hbm, profile_hbm, out_ref, sems, *, slabs, subs, particles):
     comps, _, _ = mean_ref.shape
-    parts = chunks(out_ref.shape[1])
+    parts = chunks(out_ref.shape[1], 1)
     copies = [pltpu.make_async_copy(profile_ref, profile_hbm, sems.at[len(parts)])]
     copies[0].start()
     got = got_ref[...].reshape(slabs * subs, LANES)
@@ -313,12 +315,11 @@
     comps, count = speeds.shape
     rows = count // LANES
     blocks = choices.shape[1] // LANES
-    many = len(chunks(count)) + 1
-    b = call(
+    b, speeds, moves = call(
         first_departure,
-        f32(comps, LANES),
+        (f32(comps, LANES), f32(*speeds.shape), i32(*moves.shape)),
         (speeds, moves),
-        scratch=[pltpu.VMEM(speeds.shape, jnp.float32), pltpu.VMEM(moves.shape, jnp.int32), pltpu.SemaphoreType.DMA((many,))],
+        scratch=[pltpu.SemaphoreType.DMA((len(chunks(count, 2)) + 1,))],
         resident=False,
     )
     a, s = call(
@@ -347,7 +348,7 @@
         functools.partial(finish, slabs=slabs, subs=subs, particles=count * slabs * subs),
         (jax.ShapeDtypeStruct((comps, count), jnp.float32), jax.ShapeDtypeStruct((1, CX * CY), jnp.float32)),
         (got, target, profile, mean, turned, celld),
-        scratch=[pltpu.VMEM((comps, count), jnp.float32), pltpu.SemaphoreType.DMA((many,))],
+        scratch=[pltpu.VMEM((comps, count), jnp.float32), pltpu.SemaphoreType.DMA((2,))],
     )
 
 

time: 27.5 us -> 25.6 us (0.931)
  local copies, waits for them, and re-layouts: 2.21 us -> 0.65 us
    unnamed x14 -> x6, local copies, waits for them, and re-layouts: 2.21 us -> 0.65 us
  transfers between devices with their start and end apart: 3 -> 3, of which waited for: 1 -> 1; matrix products, arithmetic and copies ran while one was open for 0% -> 0% of each run, Pallas kernels for 7% -> 3%
where the time goes in v6:
time: 25.6 us; the launch traced here: 25.4 us
  blocking collectives  11.9 us (46%)
  starting transfers between devices  7.56 us (30%)
  Pallas kernels  3.43 us (13%)
  waiting for transfers between devices  1.16 us (5%)
  between operations  0.68 us (3%)
  local copies, waits for them, and re-layouts  0.65 us (3%)
    all_to_all x1, blocking collectives, step(): got = lax.all_to_all(send, AXES, 0, 0, tiled=True)  11.9 us
    ppermute x1, starting transfers between devices, swap(): second = lax.ppermute(two, axis, odd)  4.53 us
    pallas_call x5, Pallas kernels, call(): pl.pallas_call(kernel, out_shape=out_shape, in_specs=[place] * len(inputs...  3.43 us
    ppermute x1, starting transfers between devices, swap(): first = lax.ppermute(one, axis, even)  3.03 us
    ppermute x1, waiting for transfers between devices, swap(): second = lax.ppermute(two, axis, odd)  1.16 us
    unnamed x6, local copies, waits for them, and re-layouts  0.65 us
  transfers between devices with their start and end apart: 3, of which 1 were waited for; matrix products, arithmetic and copies ran while one was open for 0% of the time, Pallas kernels for 3%

profile of v6, /device:TPU:0, one launch (start us, length us, event | category | flops | bytes accessed | tf_op | source)
XLA Modules:
  0.0 25.4 jit_solution(3668105033167430886)
XLA Ops:
  0.6 1.0 %shard_map.68 = (f32[3,128]{1,0:T(4,128)S(1)}, f32[3,5120]{1,0:T(4,128)S(1)}, s32[4,128]{1,0:T(4,128)S(1)}) custom-call(f32[3,5120]{1,0:T(4,128)} %v_hbm.1, s32[4,128]{1,0:T(4,128)} %bitcast.3), custom_call_target="tpu_custom_call" | custom-call | bytes 63488 | tf_op jit(solution)/shard_map/pallas_call | solution.py:303
  1.6 0.0 copy-start
  1.7 0.2 shard_map.69
  1.9 3.0 %collective-permute-start = (f32[3,128]{1,0:T(4,128)S(1)}, f32[3,128]{1,0:T(4,128)S(1)}, u32[]{:S(2)}, u32[]{:S(2)}) collective-permute-start(f32[3,128]{1,0:T(4,128)S(1)} %get-tuple-element.20), channel_id=1, source_target_pairs={{0,2},{2,0},{4,6},{6,4},{8,10},{10,8},{12,14},{14,12},{16,18},{18,... | collective-permute-start | bytes 4616 | tf_op jit(solution)/shard_map/ppermute | solution.py:277
  4.9 0.0 copy-start.1
  4.9 4.5 %collective-permute-start.1 = (f32[3,128]{1,0:T(4,128)S(1)}, f32[3,128]{1,0:T(4,128)S(1)}, u32[]{:S(2)}, u32[]{:S(2)}) collective-permute-start(f32[3,128]{1,0:T(4,128)S(1)} %get-tuple-element.21), channel_id=1, source_target_pairs={{0,30},{2,4},{4,2},{6,8},{8,6},{10,12},{12,10},{14,16},{16,14},{18... | collective-permute-start | bytes 4616 | tf_op jit(solution)/shard_map/ppermute | solution.py:276
  9.4 0.0 copy-start.2
  9.4 0.0 collective-permute-start.2
  9.4 0.0 copy-done
  9.4 0.0 copy-done.1
  9.4 0.6 %copy-done.2 = f32[64]{0:T(128)S(1)} copy-done((f32[64]{0:T(128)S(1)}, f32[64]{0:T(128)}, u32[]{:S(2)}) %copy-start.2) | copy-done | bytes 280
  10.1 0.8 %shard_map.70 = (f32[3,40,128]{2,1,0:T(8,128)S(1)}, s32[40,128]{1,0:T(8,128)S(1)}, s32[40,128]{1,0:T(8,128)S(1)}, f32[32,128]{1,0:T(8,128)S(1)}, s32[8,128]{1,0:...) custom-call(f32[3,5120]{1,0:T(4,128)S(1)} %get-tuple-element.18.v_ref, ...), custom_call_target="tpu_custom_call" | custom-call | flops 125829120 | bytes 86272 | tf_op jit(solution)/shard_map/pallas_call | solution.py:303
  10.9 0.0 collective-permute-done.a_ref
  10.9 1.2 %collective-permute-done.1.b_ref = f32[3,128]{1,0:T(4,128)S(1)} collective-permute-done((f32[3,128]{1,0:T(4,128)S(1)}, f32[3,128]{1,0:T(4,128)S(1)}, u32[]{:S(2)}, u32[]{:S(2)}) %collective-permute-start.1) | collective-permute-done | bytes 1568 | tf_op jit(solution)/shard_map/ppermute | solution.py:276
  12.1 0.0 collective-permute-done.2.s_ref
  12.1 0.6 %shard_map.71 = (f32[32,1,128]{2,1,0:T(1,128)S(1)}, f32[1,64]{1,0:T(1,128)S(1)}, f32[3,40,128]{2,1,0:T(8,128)S(1)}, f32[3,40,128]{2,1,0:T(8,128)S(1)}) custom-call(f32[3,128]{1,0:T(4,128)S(1)} %collective-permute-done.a_ref, f32[3,128]{1,0:T(4,128)S(1)} %collective-permute-done.1.b_ref, f32[3,256]{1,0:T(4,128)S(1)} %collective-permute-done.2.s_ref, ...), custom_call_target="tpu_custom_call" | custom-call | bytes 190464 | tf_op jit(solution)/shard_map/pallas_call | solution.py:303
  12.7 11.9 %all_to_all.5.got_ref = f32[32,1,128]{2,1,0:T(1,128)S(1)} all-to-all(f32[32,1,128]{2,1,0:T(1,128)S(1)} %get-tuple-element.29), channel_id=1, replica_groups=mesh['slab'=16,'sub'=2] {'slab','sub'}, dimensions={0} | all-to-all | bytes 32768 | tf_op jit(solution)/shard_map/all_to_all | solution.py:346
  24.6 0.8 %shard_map.72 = (f32[3,5120]{1,0:T(4,128)}, f32[1,64]{1,0:T(1,128)}) custom-call(f32[32,1,128]{2,1,0:T(1,128)S(1)} %all_to_all.5.got_ref, f32[1,128]{1,0:T(1,128)S(1)} %get-tuple-element.30.target_ref, f32[1,64]{1,0:T(1,128)S(1)} %get-tuple-element.31.profile_ref, f32[3,40,128]{2,1,0:T(8,128)S(1)} %get-tuple-element.32.mean_ref, ...), custom_call_target="tpu_custom_call" | custom-call | bytes 160512 | tf_op jit(solution)/shard_map/pallas_call | solution.py:303
Async XLA Ops:
  1.6 7.8 %copy-start = (s32[1,5120]{1,0:T(1,128)S(1)}, s32[1,5120]{1,0:T(1,128)}, u32[]{:S(2)}) copy-start(s32[1,5120]{1,0:T(1,128)} %cell_ref.1) | copy-start | bytes 61444
  1.9 9.1 %collective-permute-start = (f32[3,128]{1,0:T(4,128)S(1)}, f32[3,128]{1,0:T(4,128)S(1)}, u32[]{:S(2)}, u32[]{:S(2)}) collective-permute-start(f32[3,128]{1,0:T(4,128)S(1)} %get-tuple-element.20), channel_id=1, source_target_pairs={{0,2},{2,0},{4,6},{6,4},{8,10},{10,8},{12,14},{14,12},{16,18},{18,... | collective-permute-start | bytes 4616 | tf_op jit(solution)/shard_map/ppermute | solution.py:277
  4.9 4.5 %copy-start.1 = (s32[1,512]{1,0:T(1,128)S(1)}, s32[1,512]{1,0:T(1,128)}, u32[]{:S(2)}) copy-start(s32[1,512]{1,0:T(1,128)} %choice_ref.1) | copy-start | bytes 6148
  4.9 7.2 %collective-permute-start.1 = (f32[3,128]{1,0:T(4,128)S(1)}, f32[3,128]{1,0:T(4,128)S(1)}, u32[]{:S(2)}, u32[]{:S(2)}) collective-permute-start(f32[3,128]{1,0:T(4,128)S(1)} %get-tuple-element.21), channel_id=1, source_target_pairs={{0,30},{2,4},{4,2},{6,8},{8,6},{10,12},{12,10},{14,16},{16,14},{18... | collective-permute-start | bytes 4616 | tf_op jit(solution)/shard_map/ppermute | solution.py:276
  9.4 0.7 %copy-start.2 = (f32[64]{0:T(128)S(1)}, f32[64]{0:T(128)}, u32[]{:S(2)}) copy-start(f32[64]{0:T(128)} %param.9) | copy-start | bytes 772
  9.4 2.7 %collective-permute-start.2 = (f32[3,256]{1,0:T(4,128)S(1)}, f32[3,256]{1,0:T(4,128)S(1)}, u32[]{:S(2)}, u32[]{:S(2)}) collective-permute-start(f32[3,256]{1,0:T(4,128)S(1)} %get-tuple-element.22), channel_id=1, source_target_pairs={{0,1},{1,0},{2,3},{3,2},{4,5},{5,4},{6,7},{7,6},{8,9},{9,8},{10,11... | collective-permute-start | bytes 9224 | tf_op jit(solution)/shard_map/ppermute | solution.py:284

commit v7 on v6

--- a/solution.py
+++ b/solution.py
@@ -116,7 +116,22 @@
         out_ref[:, lane : lane + LANES] = out
 
 
-def prepare(v_ref, moves_ref, cell_ref, choice_ref, shear_ref, vd_ref, source_ref, celld_ref, base_ref, slotcell_ref, normal_ref, target_ref, keep_ref):
+def bins(block, cell, blocks):
+    parts = jnp.concatenate(split3(block), 0)
+    left = jnp.concatenate([jnp.where((cell >> 7) == h, parts, 0.0) for h in range(blocks)], 0)
+    right = (iota((LANES, LANES), 0) == (cell & (LANES - 1))).astype(jnp.bfloat16)
+    return left, right
+
+
+def join(parts):
+    return parts[:SUBLANES] + parts[SUBLANES : 2 * SUBLANES] + parts[2 * SUBLANES :]
+
+
+def columns_of(cells):
+    return cells // CZ
+
+
+def prepare(v_ref, moves_ref, cell_ref, choice_ref, shear_ref, a_ref, s_ref, vd_ref, source_ref, celld_ref, base_ref, count_ref, column_ref, spread_ref, normal_ref, target_ref, keep_ref):
     comps, count = v_ref.shape
     rows = count // LANES
     cells = choice_ref.shape[1]
@@ -129,7 +144,8 @@
         for c in range(comps):
             vd_ref[c, r : r + 1, :] = v_ref[c : c + 1, span]
 
-    slots = jnp.concatenate(lists, 1)
+    order = (1, 0, 2, 3)
+    slots = jnp.concatenate([lists[k] for k in order], 1)
     many = slots.shape[1]
     low = (iota((LANES, many), 0) == (slots & (LANES - 1))).astype(jnp.bfloat16)
     here = iota((rows, many), 0) == (slots >> 7)
@@ -142,12 +158,13 @@
     ).astype(jnp.bfloat16)
     found = lax.dot_general(marks, low, NT, preferred_element_type=jnp.float32).astype(jnp.int32)
     source = found[:rows] * LANES + found[rows:]
-    source_ref[...] = source
     keep_ref[...] = jnp.where(source == 0, 1.0, 0.0)
+    late = (source >= LANES) & (source < 2 * LANES)
+    source_ref[...] = jnp.where(late, source - LANES, -1)
 
     celld = celld_ref[...]
-    four = jnp.concatenate(lists + lists, 0)
-    slotcell_ref[...] = lookup([celld_ref[r : r + 1, :] for r in range(rows)], four)
+    four = jnp.concatenate([lists[k] for k in order + order], 0)
+    slotcell = lookup([celld_ref[r : r + 1, :] for r in range(rows)], four)
 
     counter = (iota((1, LANES), 1) & (NAXES - 1)).astype(jnp.float32)
     height = 1.0 - (2.0 * counter + 1.0) / NAXES
@@ -158,72 +175,75 @@
         entries = [take(table[c], pick) for pick in picks]
         normal_ref[c] = lookup(entries, celld)
 
+    arrived = [a_ref[...], s_ref[:, :LANES], s_ref[:, LANES:]]
+    for c in range(comps):
+        old = vd_ref[c]
+        vd_ref[c] = jnp.where(source < 2 * LANES, old, lookup([x[c : c + 1] for x in arrived], source - 2 * LANES))
+
     ones = (iota((SUBLANES - comps, LANES), 0) == 0).astype(jnp.float32)
     total = jnp.zeros((blocks * 3 * SUBLANES, LANES), jnp.float32)
-    group = 4 if rows % 4 == 0 else 1
+    group = math.gcd(4, rows)
     for first in range(0, rows, group):
         left, right = [], []
         for r in range(first, first + group):
-            cell = cell_ref[0:1, r * LANES : (r + 1) * LANES]
-            tile = v_ref[:, r * LANES : (r + 1) * LANES] * keep_ref[r : r + 1, :]
-            tile = jnp.concatenate([tile, ones], 0)
-            parts = jnp.concatenate(split3(tile), 0)
-            left.append(jnp.concatenate([jnp.where((cell >> 7) == h, parts, 0.0) for h in range(blocks)], 0))
-            right.append((iota((LANES, LANES), 0) == (cell & (LANES - 1))).astype(jnp.bfloat16))
+            span = slice(r * LANES, (r + 1) * LANES)
+            tile = v_ref[:, span] * keep_ref[r : r + 1, :]
+            one, two = bins(jnp.concatenate([tile, ones], 0), cell_ref[0:1, span], blocks)
+            left.append(one)
+            right.append(two)
         left = jnp.concatenate(left, 1).astype(jnp.bfloat16)
-        right = jnp.concatenate(right, 1)
-        total += lax.dot_general(left, right, NT, preferred_element_type=jnp.float32)
-    for h in range(blocks):
-        part = total[h * 3 * SUBLANES : (h + 1) * 3 * SUBLANES]
-        base_ref[h * SUBLANES : (h + 1) * SUBLANES] = part[:8] + part[8:16] + part[16:]
-
-
-def relax(a_ref, b_ref, s_ref, vd_ref, source_ref, celld_ref, base_ref, slotcell_ref, normal_ref, send_ref, profile_ref, mean_ref, turned_ref):
-    comps, rows, _ = vd_ref.shape
-    blocks = base_ref.shape[0] // SUBLANES
-    arrived = [a_ref[...], b_ref[...], s_ref[:, :LANES], s_ref[:, LANES:]]
-
-    pad = jnp.zeros((SUBLANES - comps, LANES), jnp.float32)
+        total += lax.dot_general(left, jnp.concatenate(right, 1), NT, preferred_element_type=jnp.float32)
     left, right = [], []
     for k, block in enumerate(arrived):
-        cell = slotcell_ref[k : k + 1, :]
-        parts = jnp.concatenate(split3(jnp.concatenate([block, pad], 0)), 0)
-        left.append(jnp.concatenate([jnp.where((cell >> 7) == h, parts, 0.0) for h in range(blocks)], 0))
-        right.append((iota((LANES, LANES), 0) == (cell & (LANES - 1))).astype(jnp.bfloat16))
+        one, two = bins(jnp.concatenate([block, jnp.zeros_like(ones)], 0), slotcell[k + 1 : k + 2], blocks)
+        left.append(one)
+        right.append(two)
     left = jnp.concatenate(left, 1).astype(jnp.bfloat16)
-    right = jnp.concatenate(right, 1)
-    fresh = lax.dot_general(left, right, NT, preferred_element_type=jnp.float32)
-    sums, means = [], []
-    for h in range(blocks):
-        part = fresh[h * 3 * SUBLANES : (h + 1) * 3 * SUBLANES]
-        total = base_ref[h * SUBLANES : (h + 1) * SUBLANES] + (part[:8] + part[8:16] + part[16:])
-        sums.append(total)
-        means.append(total / jnp.maximum(jnp.broadcast_to(total[comps : comps + 1], total.shape), 1.0))
-
-    both = jnp.concatenate([s[0:1] for s in sums] + [s[comps : comps + 1] for s in sums], 0)
+    total += lax.dot_general(left, jnp.concatenate(right, 1), NT, preferred_element_type=jnp.float32)
+    sums = [join(total[h * 3 * SUBLANES : (h + 1) * 3 * SUBLANES]) for h in range(blocks)]
+
+    both = jnp.concatenate([x[0:1] for x in sums] + [x[comps : comps + 1] for x in sums], 0)
     width = CZ // 2
     while width:
         both = both + pltpu.roll(both, LANES - width, 1)
         width //= 2
-    columns = iota((1, LANES), 1)
-    start = columns * CZ
+    start = iota((1, LANES), 1) * CZ
     flow = lookup([both[h : h + 1] for h in range(blocks)], start)
     number = lookup([both[blocks + h : blocks + h + 1] for h in range(blocks)], start)
-    profile = flow / jnp.maximum(number, 1.0)
+    column_ref[...] = jnp.concatenate([flow, 1.0 / jnp.maximum(number, 1.0)], 0)
+
+    late_cell = jnp.transpose(jnp.broadcast_to(slotcell[0:1].astype(jnp.float32), (LANES, LANES))).astype(jnp.int32)
+    for h in range(blocks):
+        span = slice(h * LANES, (h + 1) * LANES)
+        base_ref[:, span] = sums[h]
+        count_ref[:, span] = 1.0 / jnp.maximum(sums[h][comps : comps + 1], 1.0)
+        spread_ref[:, span] = (late_cell == iota((LANES, LANES), 1) + h * LANES).astype(jnp.bfloat16)
+    spread_ref[:, cells:] = (columns_of(late_cell) == iota((LANES, LANES), 1)).astype(jnp.bfloat16)
+
+
+def relax(b_ref, vd_ref, source_ref, celld_ref, base_ref, count_ref, column_ref, spread_ref, normal_ref, send_ref, profile_ref, mean_ref, turned_ref):
+    comps, rows, _ = vd_ref.shape
+    cells = base_ref.shape[1]
+    late = b_ref[...]
+    block = jnp.concatenate([late, jnp.zeros((SUBLANES - comps, LANES), jnp.float32)], 0)
+    left = jnp.concatenate(split3(block), 0).astype(jnp.bfloat16)
+    fresh = join(jnp.dot(left, spread_ref[...], preferred_element_type=jnp.float32))
+    means = (base_ref[...] + fresh[:, :cells]) * count_ref[...]
+    profile = (column_ref[0:1] + fresh[0:1, cells:]) * column_ref[1:2]
     profile_ref[...] = profile[:, :CY]
 
     source, celld = source_ref[...], celld_ref[...]
     relative, energy = [], jnp.zeros((rows, LANES), jnp.float32)
     for c in range(comps):
-        old = vd_ref[c]
-        speed = jnp.where(source == 0, old, lookup([x[c : c + 1] for x in arrived], source - LANES))
-        mean = lookup([m[c : c + 1] for m in means], celld)
+        fill = take(jnp.broadcast_to(late[c : c + 1], source.shape), source & (LANES - 1))
+        speed = jnp.where(source < 0, vd_ref[c], fill)
+        mean = lookup([means[c : c + 1, h : h + LANES] for h in range(0, cells, LANES)], celld)
         mean_ref[c] = mean
         relative.append(speed - mean)
         energy += relative[c] * relative[c]
     energy = jnp.sum(energy, 0, keepdims=True)
     energy = energy + pltpu.roll(energy, CY, 1)
-    message = jnp.where(columns < CY, profile, energy)
+    message = jnp.where(iota((1, LANES), 1) < CY, profile, energy)
     send_ref[...] = jnp.broadcast_to(message[None], send_ref.shape)
 
     n = [normal_ref[c] for c in range(comps)]
@@ -250,7 +270,7 @@
     for k, span, own in parts:
         own = slice(own.start, own.stop)
         shape = (own.stop - own.start, LANES)
-        line = (celld_ref[own, :] // CZ) & (CY - 1)
+        line = columns_of(celld_ref[own, :]) & (CY - 1)
         shift = take(jnp.broadcast_to(extra, shape), line)
         for c in range(comps):
             base = mean_ref[c, own, :] + shift if c == 0 else mean_ref[c, own, :]
@@ -314,7 +334,6 @@
     slabs, subs = lax.axis_size("slab"), lax.axis_size("sub")
     comps, count = speeds.shape
     rows = count // LANES
-    blocks = choices.shape[1] // LANES
     b, speeds, moves = call(
         first_departure,
         (f32(comps, LANES), f32(*speeds.shape), i32(*moves.shape)),
@@ -331,17 +350,19 @@
     s = swap_joined(s, "sub")
     dense = f32(comps, rows, LANES)
     index = i32(rows, LANES)
-    vd, source, celld, base, slotcell, normal, target = call(
+    cell_count = choices.shape[1]
+    sums = f32(SUBLANES, cell_count)
+    vd, source, celld, base, number, column, spread, normal, target = call(
         prepare,
-        (dense, index, index, f32(blocks * SUBLANES, LANES), i32(SUBLANES, LANES), dense, f32(1, LANES)),
-        (speeds, moves, cells, choices, shear_target[None, :]),
+        (dense, index, index, sums, f32(1, cell_count), f32(2, LANES), pltpu.VMEM((LANES, cell_count + LANES), jnp.bfloat16), dense, f32(1, LANES)),
+        (speeds, moves, cells, choices, shear_target[None, :], a, s),
         scratch=[pltpu.VMEM((rows, LANES), jnp.float32)],
         flops=2 * count * LANES * 96,
     )
     send, profile, mean, turned = call(
         relax,
         (f32(slabs * subs, 1, LANES), f32(1, CX * CY), dense, dense),
-        (a, b, s, vd, source, celld, base, slotcell, normal),
+        (b, vd, source, celld, base, number, column, spread, normal),
     )
     got = lax.all_to_all(send, AXES, 0, 0, tiled=True)
     return call(

time: 25.6 us -> 25.5 us (level)
  local copies, waits for them, and re-layouts: 0.65 us -> 0.01 us
  waiting for transfers between devices: 1.16 us -> 1.47 us
    unnamed x6, local copies, waits for them, and re-layouts: 0.65 us -> 0.01 us
    ppermute x1, starting transfers between devices: 0.01 us -> 0.56 us  [swap_joined(): return lax.ppermute(block, axis, [(0, 1), (1, 0)])]
    ppermute x1, starting transfers between devices: 3.03 us -> 2.56 us  [swap(): first = lax.ppermute(one, axis, even)]
    ppermute x1, waiting for transfers between devices: 1.16 us -> 1.46 us  [swap(): second = lax.ppermute(two, axis, odd)]
  transfers between devices with their start and end apart: 3 -> 3, of which waited for: 1 -> 1; matrix products, arithmetic and copies ran while one was open for 0% -> 0% of each run, Pallas kernels for 3% -> 5%
where the time goes in v7:
time: 25.5 us; the launch traced here: 25.3 us
  blocking collectives  11.9 us (47%)
  starting transfers between devices  7.65 us (30%)
  Pallas kernels  3.62 us (14%)
  waiting for transfers between devices  1.47 us (6%)
  between operations  0.69 us (3%)
    all_to_all x1, blocking collectives, step(): got = lax.all_to_all(send, AXES, 0, 0, tiled=True)  11.9 us
    ppermute x1, starting transfers between devices, swap(): second = lax.ppermute(two, axis, odd)  4.53 us
    pallas_call x5, Pallas kernels, call(): pl.pallas_call(kernel, out_shape=out_shape, in_specs=[place] * len(inputs...  3.62 us
    ppermute x1, starting transfers between devices, swap(): first = lax.ppermute(one, axis, even)  2.56 us
    ppermute x1, waiting for transfers between devices, swap(): second = lax.ppermute(two, axis, odd)  1.46 us
    ppermute x1, starting transfers between devices, swap_joined(): return lax.ppermute(block, axis, [(0, 1), (1, 0)])  0.56 us
  transfers between devices with their start and end apart: 3, of which 1 were waited for; matrix products, arithmetic and copies ran while one was open for 0% of the time, Pallas kernels for 5%

profile of v7, /device:TPU:0, one launch (start us, length us, event | category | flops | bytes accessed | tf_op | source)
XLA Modules:
  0.0 25.3 jit_solution(15724889943352622484)
XLA Ops:
  0.6 1.0 %shard_map.68 = (f32[3,128]{1,0:T(4,128)S(1)}, f32[3,5120]{1,0:T(4,128)S(1)}, s32[4,128]{1,0:T(4,128)S(1)}) custom-call(f32[3,5120]{1,0:T(4,128)} %v_hbm.1, s32[4,128]{1,0:T(4,128)} %bitcast.3), custom_call_target="tpu_custom_call" | custom-call | bytes 63488 | tf_op jit(solution)/shard_map/pallas_call | solution.py:323
  1.6 0.0 copy-start
  1.7 0.2 shard_map.69
  1.9 0.6 %collective-permute-start.2 = (f32[3,256]{1,0:T(4,128)S(1)}, f32[3,256]{1,0:T(4,128)S(1)}, u32[]{:S(2)}, u32[]{:S(2)}) collective-permute-start(f32[3,256]{1,0:T(4,128)S(1)} %get-tuple-element.24), channel_id=1, source_target_pairs={{0,1},{1,0},{2,3},{3,2},{4,5},{5,4},{6,7},{7,6},{8,9},{9,8},{10,11... | collective-permute-start | bytes 9224 | tf_op jit(solution)/shard_map/ppermute | solution.py:304
  2.4 0.0 copy-start.1
  2.4 2.6 %collective-permute-start.1 = (f32[3,128]{1,0:T(4,128)S(1)}, f32[3,128]{1,0:T(4,128)S(1)}, u32[]{:S(2)}, u32[]{:S(2)}) collective-permute-start(f32[3,128]{1,0:T(4,128)S(1)} %get-tuple-element.23), channel_id=1, source_target_pairs={{0,2},{2,0},{4,6},{6,4},{8,10},{10,8},{12,14},{14,12},{16,18},{18,... | collective-permute-start | bytes 4616 | tf_op jit(solution)/shard_map/ppermute | solution.py:297
  5.0 0.0 copy-start.2
  5.0 4.5 %collective-permute-start = (f32[3,128]{1,0:T(4,128)S(1)}, f32[3,128]{1,0:T(4,128)S(1)}, u32[]{:S(2)}, u32[]{:S(2)}) collective-permute-start(f32[3,128]{1,0:T(4,128)S(1)} %get-tuple-element.20), channel_id=1, source_target_pairs={{0,30},{2,4},{4,2},{6,8},{8,6},{10,12},{12,10},{14,16},{16,14},{18... | collective-permute-start | bytes 4616 | tf_op jit(solution)/shard_map/ppermute | solution.py:296
  9.5 0.0 collective-permute-done.1.a_ref
  9.5 0.0 collective-permute-done.2.s_ref
  9.5 0.0 copy-done
  9.5 0.0 copy-done.1
  9.5 0.0 copy-done.2
  9.6 1.2 %shard_map.70 = (f32[3,40,128]{2,1,0:T(8,128)S(1)}, s32[40,128]{1,0:T(8,128)S(1)}, s32[40,128]{1,0:T(8,128)S(1)}, f32[8,512]{1,0:T(8,128)S(1)}, f32[1,512]{1,0:T...) custom-call(f32[3,5120]{1,0:T(4,128)S(1)} %get-tuple-element.21.v_re, ...), custom_call_target="tpu_custom_call" | custom-call | flops 125829120 | bytes 90880 | tf_op jit(solution)/shard_map/pallas_call | solution.py:323
  10.7 1.5 %collective-permute-done.b_ref = f32[3,128]{1,0:T(4,128)S(1)} collective-permute-done((f32[3,128]{1,0:T(4,128)S(1)}, f32[3,128]{1,0:T(4,128)S(1)}, u32[]{:S(2)}, u32[]{:S(2)}) %collective-permute-start) | collective-permute-done | bytes 1568 | tf_op jit(solution)/shard_map/ppermute | solution.py:296
  12.2 0.4 %shard_map.71 = (f32[32,1,128]{2,1,0:T(1,128)S(1)}, f32[1,64]{1,0:T(1,128)S(1)}, f32[3,40,128]{2,1,0:T(8,128)S(1)}, f32[3,40,128]{2,1,0:T(8,128)S(1)}) custom-call(f32[3,128]{1,0:T(4,128)S(1)} %collective-permute-done.b_ref, f32[3,40,128]{2,1,0:T(8,128)S(1)} %get-tuple-element.25.vd_ref, s32[40,128]{1,0:T(8,128)S(1)} %get-tuple-element.26.source_ref, ...), custom_call_target="tpu_custom_call" | custom-call | bytes 512512 | tf_op jit(solution)/shard_map/pallas_call | solution.py:323
  12.6 11.9 %all_to_all.5.got_ref = f32[32,1,128]{2,1,0:T(1,128)S(1)} all-to-all(f32[32,1,128]{2,1,0:T(1,128)S(1)} %get-tuple-element.33), channel_id=1, replica_groups=mesh['slab'=16,'sub'=2] {'slab','sub'}, dimensions={0} | all-to-all | bytes 32768 | tf_op jit(solution)/shard_map/all_to_all | solution.py:367
  24.5 0.8 %shard_map.72 = (f32[3,5120]{1,0:T(4,128)}, f32[1,64]{1,0:T(1,128)}) custom-call(f32[32,1,128]{2,1,0:T(1,128)S(1)} %all_to_all.5.got_ref, f32[1,128]{1,0:T(1,128)S(1)} %get-tuple-element.34.target_ref, f32[1,64]{1,0:T(1,128)S(1)} %get-tuple-element.35.profile_ref, f32[3,40,128]{2,1,0:T(8,128)S(1)} %get-tuple-element.36.mean_ref, ...), custom_call_target="tpu_custom_call" | custom-call | bytes 160512 | tf_op jit(solution)/shard_map/pallas_call | solution.py:323
Async XLA Ops:
  1.6 7.9 %copy-start = (s32[1,5120]{1,0:T(1,128)S(1)}, s32[1,5120]{1,0:T(1,128)}, u32[]{:S(2)}) copy-start(s32[1,5120]{1,0:T(1,128)} %cell_ref.1) | copy-start | bytes 61444
  1.9 7.7 %collective-permute-start.2 = (f32[3,256]{1,0:T(4,128)S(1)}, f32[3,256]{1,0:T(4,128)S(1)}, u32[]{:S(2)}, u32[]{:S(2)}) collective-permute-start(f32[3,256]{1,0:T(4,128)S(1)} %get-tuple-element.24), channel_id=1, source_target_pairs={{0,1},{1,0},{2,3},{3,2},{4,5},{5,4},{6,7},{7,6},{8,9},{9,8},{10,11... | collective-permute-start | bytes 9224 | tf_op jit(solution)/shard_map/ppermute | solution.py:304
  2.4 7.1 %copy-start.1 = (s32[1,512]{1,0:T(1,128)S(1)}, s32[1,512]{1,0:T(1,128)}, u32[]{:S(2)}) copy-start(s32[1,512]{1,0:T(1,128)} %choice_ref.1) | copy-start | bytes 6148
  2.4 7.1 %collective-permute-start.1 = (f32[3,128]{1,0:T(4,128)S(1)}, f32[3,128]{1,0:T(4,128)S(1)}, u32[]{:S(2)}, u32[]{:S(2)}) collective-permute-start(f32[3,128]{1,0:T(4,128)S(1)} %get-tuple-element.23), channel_id=1, source_target_pairs={{0,2},{2,0},{4,6},{6,4},{8,10},{10,8},{12,14},{14,12},{16,18},{18,... | collective-permute-start | bytes 4616 | tf_op jit(solution)/shard_map/ppermute | solution.py:297
  5.0 4.6 %copy-start.2 = (f32[64]{0:T(128)S(1)}, f32[64]{0:T(128)}, u32[]{:S(2)}) copy-start(f32[64]{0:T(128)} %param.9) | copy-start | bytes 772
  5.0 7.2 %collective-permute-start = (f32[3,128]{1,0:T(4,128)S(1)}, f32[3,128]{1,0:T(4,128)S(1)}, u32[]{:S(2)}, u32[]{:S(2)}) collective-permute-start(f32[3,128]{1,0:T(4,128)S(1)} %get-tuple-element.20), channel_id=1, source_target_pairs={{0,30},{2,4},{4,2},{6,8},{8,6},{10,12},{12,10},{14,16},{16,14},{18... | collective-permute-start | bytes 4616 | tf_op jit(solution)/shard_map/ppermute | solution.py:296

commit v8 on v7

--- a/solution.py
+++ b/solution.py
@@ -131,7 +131,7 @@
     return cells // CZ
 
 
-def prepare(v_ref, moves_ref, cell_ref, choice_ref, shear_ref, a_ref, s_ref, vd_ref, source_ref, celld_ref, base_ref, count_ref, column_ref, spread_ref, normal_ref, target_ref, keep_ref):
+def prepare(v_ref, moves_ref, cell_ref, choice_ref, shear_ref, a_ref, s_ref, vd_ref, source_ref, celld_ref, base_ref, count_ref, column_ref, spread_ref, normal_ref, target_ref, shift_ref, slot_ref, energy_ref, keep_ref):
     comps, count = v_ref.shape
     rows = count // LANES
     cells = choice_ref.shape[1]
@@ -213,39 +213,42 @@
     column_ref[...] = jnp.concatenate([flow, 1.0 / jnp.maximum(number, 1.0)], 0)
 
     late_cell = jnp.transpose(jnp.broadcast_to(slotcell[0:1].astype(jnp.float32), (LANES, LANES))).astype(jnp.int32)
+    others = []
     for h in range(blocks):
         span = slice(h * LANES, (h + 1) * LANES)
+        hits = (late_cell == iota((LANES, LANES), 1) + h * LANES).astype(jnp.float32)
+        spread_ref[:, span] = hits.astype(jnp.bfloat16)
         base_ref[:, span] = sums[h]
-        count_ref[:, span] = 1.0 / jnp.maximum(sums[h][comps : comps + 1], 1.0)
-        spread_ref[:, span] = (late_cell == iota((LANES, LANES), 1) + h * LANES).astype(jnp.bfloat16)
+        number = sums[h][comps : comps + 1]
+        count_ref[:, span] = 1.0 / jnp.maximum(number, 1.0)
+        missing = jnp.sum(hits, 0, keepdims=True)
+        other = sums[h] / jnp.maximum(number - missing, 1.0)
+        others.append(other)
+        shift_ref[:, span] = jnp.where(iota((SUBLANES, LANES), 0) < comps, other * missing, 0.0)
     spread_ref[:, cells:] = (columns_of(late_cell) == iota((LANES, LANES), 1)).astype(jnp.bfloat16)
-
-
-def relax(b_ref, vd_ref, source_ref, celld_ref, base_ref, count_ref, column_ref, spread_ref, normal_ref, send_ref, profile_ref, mean_ref, turned_ref):
-    comps, rows, _ = vd_ref.shape
-    cells = base_ref.shape[1]
-    late = b_ref[...]
-    block = jnp.concatenate([late, jnp.zeros((SUBLANES - comps, LANES), jnp.float32)], 0)
-    left = jnp.concatenate(split3(block), 0).astype(jnp.bfloat16)
-    fresh = join(jnp.dot(left, spread_ref[...], preferred_element_type=jnp.float32))
-    means = (base_ref[...] + fresh[:, :cells]) * count_ref[...]
-    profile = (column_ref[0:1] + fresh[0:1, cells:]) * column_ref[1:2]
-    profile_ref[...] = profile[:, :CY]
-
+    energy = jnp.zeros((rows, LANES), jnp.float32)
+    for c in range(comps):
+        parts = [x[c : c + 1] for x in others]
+        slot_ref[c : c + 1, :] = lookup(parts, slotcell[0:1])
+        apart = vd_ref[c] - lookup(parts, celld)
+        energy += apart * apart
+    energy_ref[...] = jnp.sum(jnp.where(late, 0.0, energy), 0, keepdims=True)
+
+
+def on_last_slab():
+    return lax.axis_index("slab") == lax.axis_size("slab") - 1
+
+
+def turn(late, means_ref, vd_ref, source_ref, celld_ref, normal_ref, mean_ref, turned_ref):
+    comps = vd_ref.shape[0]
     source, celld = source_ref[...], celld_ref[...]
-    relative, energy = [], jnp.zeros((rows, LANES), jnp.float32)
+    relative = []
     for c in range(comps):
         fill = take(jnp.broadcast_to(late[c : c + 1], source.shape), source & (LANES - 1))
         speed = jnp.where(source < 0, vd_ref[c], fill)
-        mean = lookup([means[c : c + 1, h : h + LANES] for h in range(0, cells, LANES)], celld)
+        mean = lookup([means_ref[c : c + 1, h : h + LANES] for h in range(0, means_ref.shape[1], LANES)], celld)
         mean_ref[c] = mean
         relative.append(speed - mean)
-        energy += relative[c] * relative[c]
-    energy = jnp.sum(energy, 0, keepdims=True)
-    energy = energy + pltpu.roll(energy, CY, 1)
-    message = jnp.where(iota((1, LANES), 1) < CY, profile, energy)
-    send_ref[...] = jnp.broadcast_to(message[None], send_ref.shape)
-
     n = [normal_ref[c] for c in range(comps)]
     along = (n[0] * relative[0] + n[1] * relative[1] + n[2] * relative[2]) * (1.0 - ROT_COS)
     for c in range(comps):
@@ -254,32 +257,66 @@
         turned_ref[c] = relative[c] * ROT_COS + cross * ROT_SIN + n[c] * along
 
 
-def finish(got_ref, target_ref, profile_ref, mean_ref, turned_ref, celld_ref, out_hbm, profile_hbm, out_ref, sems, *, slabs, subs, particles):
-    comps, _, _ = mean_ref.shape
-    parts = chunks(out_ref.shape[1], 1)
-    copies = [pltpu.make_async_copy(profile_ref, profile_hbm, sems.at[len(parts)])]
+def relax(b_ref, vd_ref, source_ref, celld_ref, base_ref, count_ref, column_ref, spread_ref, normal_ref, shift_ref, slot_ref, energy_ref, send_ref, profile_ref, means_ref, mean_ref, turned_ref):
+    comps = vd_ref.shape[0]
+    cells = base_ref.shape[1]
+    late = b_ref[...]
+    block = jnp.concatenate([late, jnp.zeros((SUBLANES - comps, LANES), jnp.float32)], 0)
+    left = jnp.concatenate(split3(block), 0).astype(jnp.bfloat16)
+    fresh = join(jnp.dot(left, spread_ref[...], preferred_element_type=jnp.float32))
+    means_ref[...] = (base_ref[...] + fresh[:, :cells]) * count_ref[...]
+    profile = (column_ref[0:1] + fresh[0:1, cells:]) * column_ref[1:2]
+    profile_ref[...] = profile[:, :CY]
+
+    moved = fresh[:, :cells] - shift_ref[...]
+    less = jnp.sum(moved * moved, 0, keepdims=True) * count_ref[...]
+    apart = late - slot_ref[...]
+    energy = energy_ref[...] + jnp.sum(apart * apart, 0, keepdims=True)
+    for h in range(0, cells, LANES):
+        energy = energy - less[:, h : h + LANES]
+    energy = energy + pltpu.roll(energy, CY, 1)
+    message = jnp.where(iota((1, LANES), 1) < CY, profile, energy)
+    send_ref[...] = jnp.broadcast_to(message[None], send_ref.shape)
+
+    @pl.when(jnp.logical_not(on_last_slab()))
+    def _():
+        turn(late, means_ref, vd_ref, source_ref, celld_ref, normal_ref, mean_ref, turned_ref)
+
+
+def finish(got_ref, target_ref, profile_ref, mean_ref, turned_ref, b_ref, means_ref, vd_ref, source_ref, celld_ref, normal_ref, out_hbm, profile_hbm, out_ref, own_mean_ref, own_turned_ref, sems, *, slabs, subs, particles):
+    comps, rows, _ = mean_ref.shape
+    copies = [pltpu.make_async_copy(profile_ref, profile_hbm, sems.at[0]), pltpu.make_async_copy(out_ref, out_hbm, sems.at[1])]
     copies[0].start()
     got = got_ref[...].reshape(slabs * subs, LANES)
     mine = lax.rem(iota(got.shape, 0), subs) == lax.axis_index("sub")
     lane = iota(got.shape, 1)
     drift = jnp.sum(jnp.where(mine, got, 0.0), 0, keepdims=True) / (CX * slabs)
     work = jnp.sum(jnp.where(lane < CY, 0.0, got), 0, keepdims=True)
-    work = jnp.sum(work, 1, keepdims=True)
+    work = jnp.maximum(jnp.sum(work, 1, keepdims=True), 0.0)
     scale = lax.rsqrt(work / (3.0 * particles * RESERVOIR_HEAT) + 1e-06)
     extra = FEEDBACK * (target_ref[...] - drift)
-    for k, span, own in parts:
-        own = slice(own.start, own.stop)
-        shape = (own.stop - own.start, LANES)
-        line = columns_of(celld_ref[own, :]) & (CY - 1)
-        shift = take(jnp.broadcast_to(extra, shape), line)
+    line = columns_of(celld_ref[...]) & (CY - 1)
+    shift = take(jnp.broadcast_to(extra, line.shape), line)
+
+    def write(mean_ref, turned_ref):
         for c in range(comps):
-            base = mean_ref[c, own, :] + shift if c == 0 else mean_ref[c, own, :]
-            out = base + scale * turned_ref[c, own, :]
-            for r in range(shape[0]):
-                lanes = slice((own.start + r) * LANES, (own.start + r + 1) * LANES)
-                out_ref[c : c + 1, lanes] = out[r : r + 1, :]
-        copies.append(pltpu.make_async_copy(out_ref.at[:, span], out_hbm.at[:, span], sems.at[k]))
-        copies[-1].start()
+            base = mean_ref[c] + shift if c == 0 else mean_ref[c]
+            out = base + scale * turned_ref[c]
+            for r in range(rows):
+                out_ref[c : c + 1, r * LANES : (r + 1) * LANES] = out[r : r + 1, :]
+
+    last = on_last_slab()
+
+    @pl.when(last)
+    def _():
+        turn(b_ref[...], means_ref, vd_ref, source_ref, celld_ref, normal_ref, own_mean_ref, own_turned_ref)
+        write(own_mean_ref, own_turned_ref)
+
+    @pl.when(jnp.logical_not(last))
+    def _():
+        write(mean_ref, turned_ref)
+
+    copies[1].start()
     for copy in copies:
         copy.wait()
 
@@ -352,24 +389,42 @@
     index = i32(rows, LANES)
     cell_count = choices.shape[1]
     sums = f32(SUBLANES, cell_count)
-    vd, source, celld, base, number, column, spread, normal, target = call(
+    vd, source, celld, base, number, column, spread, normal, target, shift, slot, energy = call(
         prepare,
-        (dense, index, index, sums, f32(1, cell_count), f32(2, LANES), pltpu.VMEM((LANES, cell_count + LANES), jnp.bfloat16), dense, f32(1, LANES)),
+        (
+            dense,
+            index,
+            index,
+            sums,
+            f32(1, cell_count),
+            f32(2, LANES),
+            pltpu.VMEM((LANES, cell_count + LANES), jnp.bfloat16),
+            dense,
+            f32(1, LANES),
+            sums,
+            f32(comps, LANES),
+            f32(1, LANES),
+        ),
         (speeds, moves, cells, choices, shear_target[None, :], a, s),
         scratch=[pltpu.VMEM((rows, LANES), jnp.float32)],
         flops=2 * count * LANES * 96,
     )
-    send, profile, mean, turned = call(
+    send, profile, means, mean, turned = call(
         relax,
-        (f32(slabs * subs, 1, LANES), f32(1, CX * CY), dense, dense),
-        (b, vd, source, celld, base, number, column, spread, normal),
+        (f32(slabs * subs, 1, LANES), f32(1, CX * CY), sums, dense, dense),
+        (b, vd, source, celld, base, number, column, spread, normal, shift, slot, energy),
     )
     got = lax.all_to_all(send, AXES, 0, 0, tiled=True)
     return call(
         functools.partial(finish, slabs=slabs, subs=subs, particles=count * slabs * subs),
         (jax.ShapeDtypeStruct((comps, count), jnp.float32), jax.ShapeDtypeStruct((1, CX * CY), jnp.float32)),
-        (got, target, profile, mean, turned, celld),
-        scratch=[pltpu.VMEM((comps, count), jnp.float32), pltpu.SemaphoreType.DMA((2,))],
+        (got, target, profile, mean, turned, b, means, vd, source, celld, normal),
+        scratch=[
+            pltpu.VMEM((comps, count), jnp.float32),
+            pltpu.VMEM((comps, rows, LANES), jnp.float32),
+            pltpu.VMEM((comps, rows, LANES), jnp.float32),
+            pltpu.SemaphoreType.DMA((2,)),
+        ],
     )
 
 

time: 25.5 us -> 25.3 us (level)
  Pallas kernels: 3.62 us -> 3.94 us
  blocking collectives: 11.9 us -> 11.6 us
    pallas_call x5, Pallas kernels: 3.62 us -> 3.94 us  [call(): pl.pallas_call(kernel, out_shape=out_shape, in_specs=[place] * len(inputs...]
    all_to_all x1, blocking collectives: 11.9 us -> 11.6 us  [step(): got = lax.all_to_all(send, AXES, 0, 0, tiled=True)]
  transfers between devices with their start and end apart: 3 -> 3, of which waited for: 1 -> 1; matrix products, arithmetic and copies ran while one was open for 0% -> 0% of each run, Pallas kernels for 5% -> 6%
where the time goes in v8:
time: 25.3 us; the launch traced here: 25.1 us
  blocking collectives  11.6 us (46%)
  starting transfers between devices  7.65 us (30%)
  Pallas kernels  3.94 us (16%)
  waiting for transfers between devices  1.22 us (5%)
  between operations  0.69 us (3%)
    all_to_all x1, blocking collectives, step(): got = lax.all_to_all(send, AXES, 0, 0, tiled=True)  11.6 us
    ppermute x1, starting transfers between devices, swap(): second = lax.ppermute(two, axis, odd)  4.53 us
    pallas_call x5, Pallas kernels, call(): pl.pallas_call(kernel, out_shape=out_shape, in_specs=[place] * len(inputs...  3.94 us
    ppermute x1, starting transfers between devices, swap(): first = lax.ppermute(one, axis, even)  2.56 us
    ppermute x1, waiting for transfers between devices, swap(): second = lax.ppermute(two, axis, odd)  1.22 us
    ppermute x1, starting transfers between devices, swap_joined(): return lax.ppermute(block, axis, [(0, 1), (1, 0)])  0.56 us
  transfers between devices with their start and end apart: 3, of which 1 were waited for; matrix products, arithmetic and copies ran while one was open for 0% of the time, Pallas kernels for 6%

profile of v8, /device:TPU:0, one launch (start us, length us, event | category | flops | bytes accessed | tf_op | source)
XLA Modules:
  0.0 25.1 jit_solution(10695283493995292420)
XLA Ops:
  0.6 1.0 %shard_map.68 = (f32[3,128]{1,0:T(4,128)S(1)}, f32[3,5120]{1,0:T(4,128)S(1)}, s32[4,128]{1,0:T(4,128)S(1)}) custom-call(f32[3,5120]{1,0:T(4,128)} %v_hbm.1, s32[4,128]{1,0:T(4,128)} %bitcast.3), custom_call_target="tpu_custom_call" | custom-call | bytes 63488 | tf_op jit(solution)/shard_map/pallas_call | solution.py:360
  1.6 0.0 copy-start
  1.7 0.2 shard_map.69
  1.9 0.6 %collective-permute-start.2 = (f32[3,256]{1,0:T(4,128)S(1)}, f32[3,256]{1,0:T(4,128)S(1)}, u32[]{:S(2)}, u32[]{:S(2)}) collective-permute-start(f32[3,256]{1,0:T(4,128)S(1)} %get-tuple-element.28), channel_id=1, source_target_pairs={{0,1},{1,0},{2,3},{3,2},{4,5},{5,4},{6,7},{7,6},{8,9},{9,8},{10,11... | collective-permute-start | bytes 9224 | tf_op jit(solution)/shard_map/ppermute | solution.py:341
  2.4 0.0 copy-start.1
  2.4 2.6 %collective-permute-start.1 = (f32[3,128]{1,0:T(4,128)S(1)}, f32[3,128]{1,0:T(4,128)S(1)}, u32[]{:S(2)}, u32[]{:S(2)}) collective-permute-start(f32[3,128]{1,0:T(4,128)S(1)} %get-tuple-element.27), channel_id=1, source_target_pairs={{0,2},{2,0},{4,6},{6,4},{8,10},{10,8},{12,14},{14,12},{16,18},{18,... | collective-permute-start | bytes 4616 | tf_op jit(solution)/shard_map/ppermute | solution.py:334
  5.0 0.0 copy-start.2
  5.0 4.5 %collective-permute-start = (f32[3,128]{1,0:T(4,128)S(1)}, f32[3,128]{1,0:T(4,128)S(1)}, u32[]{:S(2)}, u32[]{:S(2)}) collective-permute-start(f32[3,128]{1,0:T(4,128)S(1)} %get-tuple-element.24), channel_id=1, source_target_pairs={{0,30},{2,4},{4,2},{6,8},{8,6},{10,12},{12,10},{14,16},{16,14},{18... | collective-permute-start | bytes 4616 | tf_op jit(solution)/shard_map/ppermute | solution.py:333
  9.5 0.0 collective-permute-done.1.a_ref
  9.5 0.0 collective-permute-done.2.s_ref
  9.5 0.0 copy-done
  9.5 0.0 copy-done.1
  9.5 0.0 copy-done.2
  9.6 1.4 %shard_map.70 = (f32[3,40,128]{2,1,0:T(8,128)S(1)}, s32[40,128]{1,0:T(8,128)S(1)}, s32[40,128]{1,0:T(8,128)S(1)}, f32[8,512]{1,0:T(8,128)S(1)}, f32[1,512]{1,0:T...) custom-call(f32[3,5120]{1,0:T(4,128)S(1)} %get-tuple-element.25.v_re, ...), custom_call_target="tpu_custom_call" | custom-call | flops 125829120 | bytes 90880 | tf_op jit(solution)/shard_map/pallas_call | solution.py:360
  11.0 1.2 %collective-permute-done.b_ref = f32[3,128]{1,0:T(4,128)S(1)} collective-permute-done((f32[3,128]{1,0:T(4,128)S(1)}, f32[3,128]{1,0:T(4,128)S(1)}, u32[]{:S(2)}, u32[]{:S(2)}) %collective-permute-start) | collective-permute-done | bytes 1568 | tf_op jit(solution)/shard_map/ppermute | solution.py:333
  12.2 0.5 %shard_map.71 = (f32[32,1,128]{2,1,0:T(1,128)S(1)}, f32[1,64]{1,0:T(1,128)S(1)}, f32[8,512]{1,0:T(8,128)S(1)}, f32[3,40,128]{2,1,0:T(8,128)S(1)}, f32[3,40,128]{2,1,0:T(8,128)S(1)}) custom-call(f32[3,128]{1,0:T(4,128)S(1)} %collective-permute-done.b_ref, f32[3,40,128]{2,1,0:T(8,128)S(1)} %get-tuple-element.29.vd_ref, ...), custom_call_target="tpu_custom_call" | custom-call | bytes 530944 | tf_op jit(solution)/shard_map/pallas_call | solution.py:360
  12.7 11.6 %all_to_all.5.got_ref = f32[32,1,128]{2,1,0:T(1,128)S(1)} all-to-all(f32[32,1,128]{2,1,0:T(1,128)S(1)} %get-tuple-element.40), channel_id=1, replica_groups=mesh['slab'=16,'sub'=2] {'slab','sub'}, dimensions={0} | all-to-all | bytes 32768 | tf_op jit(solution)/shard_map/all_to_all | solution.py:417
  24.3 0.8 %shard_map.72 = (f32[3,5120]{1,0:T(4,128)}, f32[1,64]{1,0:T(1,128)}) custom-call(f32[32,1,128]{2,1,0:T(1,128)S(1)} %all_to_all.5.got_ref, f32[1,128]{1,0:T(1,128)S(1)} %get-tuple-element.41.target_ref, f32[1,64]{1,0:T(1,128)S(1)} %get-tuple-element.42.profile_ref, f32[3,40,128]{2,1,0:T(8,128)S(1)} %get-tuple-element.43.mean_ref, ...), custom_call_target="tpu_custom_call" | custom-call | bytes 321792 | tf_op jit(solution)/shard_map/pallas_call | solution.py:360
Async XLA Ops:
  1.6 7.9 %copy-start = (s32[1,5120]{1,0:T(1,128)S(1)}, s32[1,5120]{1,0:T(1,128)}, u32[]{:S(2)}) copy-start(s32[1,5120]{1,0:T(1,128)} %cell_ref.1) | copy-start | bytes 61444
  1.9 7.7 %collective-permute-start.2 = (f32[3,256]{1,0:T(4,128)S(1)}, f32[3,256]{1,0:T(4,128)S(1)}, u32[]{:S(2)}, u32[]{:S(2)}) collective-permute-start(f32[3,256]{1,0:T(4,128)S(1)} %get-tuple-element.28), channel_id=1, source_target_pairs={{0,1},{1,0},{2,3},{3,2},{4,5},{5,4},{6,7},{7,6},{8,9},{9,8},{10,11... | collective-permute-start | bytes 9224 | tf_op jit(solution)/shard_map/ppermute | solution.py:341
  2.4 7.1 %copy-start.1 = (s32[1,512]{1,0:T(1,128)S(1)}, s32[1,512]{1,0:T(1,128)}, u32[]{:S(2)}) copy-start(s32[1,512]{1,0:T(1,128)} %choice_ref.1) | copy-start | bytes 6148
  2.4 7.1 %collective-permute-start.1 = (f32[3,128]{1,0:T(4,128)S(1)}, f32[3,128]{1,0:T(4,128)S(1)}, u32[]{:S(2)}, u32[]{:S(2)}) collective-permute-start(f32[3,128]{1,0:T(4,128)S(1)} %get-tuple-element.27), channel_id=1, source_target_pairs={{0,2},{2,0},{4,6},{6,4},{8,10},{10,8},{12,14},{14,12},{16,18},{18,... | collective-permute-start | bytes 4616 | tf_op jit(solution)/shard_map/ppermute | solution.py:334
  5.0 4.6 %copy-start.2 = (f32[64]{0:T(128)S(1)}, f32[64]{0:T(128)}, u32[]{:S(2)}) copy-start(f32[64]{0:T(128)} %param.9) | copy-start | bytes 772
  5.0 7.2 %collective-permute-start = (f32[3,128]{1,0:T(4,128)S(1)}, f32[3,128]{1,0:T(4,128)S(1)}, u32[]{:S(2)}, u32[]{:S(2)}) collective-permute-start(f32[3,128]{1,0:T(4,128)S(1)} %get-tuple-element.24), channel_id=1, source_target_pairs={{0,30},{2,4},{4,2},{6,8},{8,6},{10,12},{12,10},{14,16},{16,14},{18... | collective-permute-start | bytes 4616 | tf_op jit(solution)/shard_map/ppermute | solution.py:333

commit v9 on v8

--- a/solution.py
+++ b/solution.py
@@ -96,12 +96,12 @@
     comps = v_ref.shape[0]
     index = jnp.broadcast_to(index, (comps, LANES))
     high, low = index >> 7, index & (LANES - 1)
-    out = jnp.zeros((comps, LANES), jnp.float32)
+    outs = [jnp.zeros((comps, LANES), jnp.float32) for _ in range(4)]
     for copy, (_, _, rows) in zip(copies[1:], parts):
         copy.wait()
         for r in rows:
-            out = jnp.where(high == r, take(v_ref[:, r * LANES : (r + 1) * LANES], low), out)
-    out_ref[...] = out
+            outs[r % 4] = jnp.where(high == r, take(v_ref[:, r * LANES : (r + 1) * LANES], low), outs[r % 4])
+    out_ref[...] = (outs[0] + outs[1]) + (outs[2] + outs[3])
 
 
 def other_departures(v_ref, moves_ref, a_ref, s_ref):
@@ -220,19 +220,21 @@
         spread_ref[:, span] = hits.astype(jnp.bfloat16)
         base_ref[:, span] = sums[h]
         number = sums[h][comps : comps + 1]
-        count_ref[:, span] = 1.0 / jnp.maximum(number, 1.0)
+        count_ref[:, span] = jnp.broadcast_to(1.0 / jnp.maximum(number, 1.0), (SUBLANES, LANES))
         missing = jnp.sum(hits, 0, keepdims=True)
         other = sums[h] / jnp.maximum(number - missing, 1.0)
         others.append(other)
         shift_ref[:, span] = jnp.where(iota((SUBLANES, LANES), 0) < comps, other * missing, 0.0)
     spread_ref[:, cells:] = (columns_of(late_cell) == iota((LANES, LANES), 1)).astype(jnp.bfloat16)
+    slot_ref[...] = jnp.zeros_like(slot_ref)
     energy = jnp.zeros((rows, LANES), jnp.float32)
     for c in range(comps):
         parts = [x[c : c + 1] for x in others]
         slot_ref[c : c + 1, :] = lookup(parts, slotcell[0:1])
         apart = vd_ref[c] - lookup(parts, celld)
         energy += apart * apart
-    energy_ref[...] = jnp.sum(jnp.where(late, 0.0, energy), 0, keepdims=True)
+    energy = jnp.sum(jnp.where(late, 0.0, energy), 0, keepdims=True)
+    energy_ref[...] = energy + pltpu.roll(energy, CY, 1)
 
 
 def on_last_slab():
@@ -268,13 +270,13 @@
     profile = (column_ref[0:1] + fresh[0:1, cells:]) * column_ref[1:2]
     profile_ref[...] = profile[:, :CY]
 
+    apart = block - slot_ref[...]
     moved = fresh[:, :cells] - shift_ref[...]
-    less = jnp.sum(moved * moved, 0, keepdims=True) * count_ref[...]
-    apart = late - slot_ref[...]
-    energy = energy_ref[...] + jnp.sum(apart * apart, 0, keepdims=True)
+    less = moved * moved * count_ref[...]
+    energy = apart * apart
     for h in range(0, cells, LANES):
         energy = energy - less[:, h : h + LANES]
-    energy = energy + pltpu.roll(energy, CY, 1)
+    energy = jnp.sum(energy + pltpu.roll(energy, CY, 1), 0, keepdims=True) + energy_ref[...]
     message = jnp.where(iota((1, LANES), 1) < CY, profile, energy)
     send_ref[...] = jnp.broadcast_to(message[None], send_ref.shape)
 
@@ -287,12 +289,19 @@
     comps, rows, _ = mean_ref.shape
     copies = [pltpu.make_async_copy(profile_ref, profile_hbm, sems.at[0]), pltpu.make_async_copy(out_ref, out_hbm, sems.at[1])]
     copies[0].start()
-    got = got_ref[...].reshape(slabs * subs, LANES)
-    mine = lax.rem(iota(got.shape, 0), subs) == lax.axis_index("sub")
-    lane = iota(got.shape, 1)
-    drift = jnp.sum(jnp.where(mine, got, 0.0), 0, keepdims=True) / (CX * slabs)
-    work = jnp.sum(jnp.where(lane < CY, 0.0, got), 0, keepdims=True)
-    work = jnp.maximum(jnp.sum(work, 1, keepdims=True), 0.0)
+    heard = []
+    for b in range(subs):
+        terms = [got_ref[a * subs + b] for a in range(slabs)]
+        while len(terms) > 1:
+            terms = [sum(terms[k + 1 : k + 2], terms[k]) for k in range(0, len(terms), 2)]
+        heard.append(terms[0])
+    drift = heard[0]
+    for b in range(1, subs):
+        drift = jnp.where(lax.axis_index("sub") == b, heard[b], drift)
+    drift = drift / (CX * slabs)
+    work = sum(heard[1:], heard[0])
+    work = jnp.sum(jnp.where(iota(work.shape, 1) < CY, 0.0, work), 1, keepdims=True)
+    work = jnp.maximum(work, 0.0)
     scale = lax.rsqrt(work / (3.0 * particles * RESERVOIR_HEAT) + 1e-06)
     extra = FEEDBACK * (target_ref[...] - drift)
     line = columns_of(celld_ref[...]) & (CY - 1)
@@ -396,13 +405,13 @@
             index,
             index,
             sums,
-            f32(1, cell_count),
+            sums,
             f32(2, LANES),
             pltpu.VMEM((LANES, cell_count + LANES), jnp.bfloat16),
             dense,
             f32(1, LANES),
             sums,
-            f32(comps, LANES),
+            f32(SUBLANES, LANES),
             f32(1, LANES),
         ),
         (speeds, moves, cells, choices, shear_target[None, :], a, s),

time: 25.3 us -> 25.3 us (level)
  no operation moved by 1% of the time
where the time goes in v9:
time: 25.3 us; the launch traced here: 25.1 us
  blocking collectives  11.6 us (46%)
  starting transfers between devices  7.65 us (30%)
  Pallas kernels  3.94 us (16%)
  waiting for transfers between devices  1.2 us (5%)
  between operations  0.68 us (3%)
    all_to_all x1, blocking collectives, step(): got = lax.all_to_all(send, AXES, 0, 0, tiled=True)  11.6 us
    ppermute x1, starting transfers between devices, swap(): second = lax.ppermute(two, axis, odd)  4.53 us
    pallas_call x5, Pallas kernels, call(): pl.pallas_call(kernel, out_shape=out_shape, in_specs=[place] * len(inputs...  3.94 us
    ppermute x1, starting transfers between devices, swap(): first = lax.ppermute(one, axis, even)  2.56 us
    ppermute x1, waiting for transfers between devices, swap(): second = lax.ppermute(two, axis, odd)  1.2 us
    ppermute x1, starting transfers between devices, swap_joined(): return lax.ppermute(block, axis, [(0, 1), (1, 0)])  0.56 us
  transfers between devices with their start and end apart: 3, of which 1 were waited for; matrix products, arithmetic and copies ran while one was open for 0% of the time, Pallas kernels for 6%

profile of v9, /device:TPU:0, one launch (start us, length us, event | category | flops | bytes accessed | tf_op | source)
XLA Modules:
  0.0 25.1 jit_solution(12188691904200237245)
XLA Ops:
  0.6 1.0 %shard_map.68 = (f32[3,128]{1,0:T(4,128)S(1)}, f32[3,5120]{1,0:T(4,128)S(1)}, s32[4,128]{1,0:T(4,128)S(1)}) custom-call(f32[3,5120]{1,0:T(4,128)} %v_hbm.1, s32[4,128]{1,0:T(4,128)} %bitcast.3), custom_call_target="tpu_custom_call" | custom-call | bytes 63488 | tf_op jit(solution)/shard_map/pallas_call | solution.py:369
  1.6 0.0 copy-start
  1.7 0.2 shard_map.69
  1.9 0.6 %collective-permute-start.2 = (f32[3,256]{1,0:T(4,128)S(1)}, f32[3,256]{1,0:T(4,128)S(1)}, u32[]{:S(2)}, u32[]{:S(2)}) collective-permute-start(f32[3,256]{1,0:T(4,128)S(1)} %get-tuple-element.28), channel_id=1, source_target_pairs={{0,1},{1,0},{2,3},{3,2},{4,5},{5,4},{6,7},{7,6},{8,9},{9,8},{10,11... | collective-permute-start | bytes 9224 | tf_op jit(solution)/shard_map/ppermute | solution.py:350
  2.4 0.0 copy-start.1
  2.4 2.6 %collective-permute-start.1 = (f32[3,128]{1,0:T(4,128)S(1)}, f32[3,128]{1,0:T(4,128)S(1)}, u32[]{:S(2)}, u32[]{:S(2)}) collective-permute-start(f32[3,128]{1,0:T(4,128)S(1)} %get-tuple-element.27), channel_id=1, source_target_pairs={{0,2},{2,0},{4,6},{6,4},{8,10},{10,8},{12,14},{14,12},{16,18},{18,... | collective-permute-start | bytes 4616 | tf_op jit(solution)/shard_map/ppermute | solution.py:343
  5.0 0.0 copy-start.2
  5.0 4.5 %collective-permute-start = (f32[3,128]{1,0:T(4,128)S(1)}, f32[3,128]{1,0:T(4,128)S(1)}, u32[]{:S(2)}, u32[]{:S(2)}) collective-permute-start(f32[3,128]{1,0:T(4,128)S(1)} %get-tuple-element.24), channel_id=1, source_target_pairs={{0,30},{2,4},{4,2},{6,8},{8,6},{10,12},{12,10},{14,16},{16,14},{18... | collective-permute-start | bytes 4616 | tf_op jit(solution)/shard_map/ppermute | solution.py:342
  9.5 0.0 collective-permute-done.1.a_ref
  9.5 0.0 collective-permute-done.2.s_ref
  9.5 0.0 copy-done
  9.5 0.0 copy-done.1
  9.5 0.0 copy-done.2
  9.6 1.4 %shard_map.70 = (f32[3,40,128]{2,1,0:T(8,128)S(1)}, s32[40,128]{1,0:T(8,128)S(1)}, s32[40,128]{1,0:T(8,128)S(1)}, f32[8,512]{1,0:T(8,128)S(1)}, f32[8,512]{1,0:T...) custom-call(f32[3,5120]{1,0:T(4,128)S(1)} %get-tuple-element.25.v_re, ...), custom_call_target="tpu_custom_call" | custom-call | flops 125829120 | bytes 90880 | tf_op jit(solution)/shard_map/pallas_call | solution.py:369
  11.0 1.2 %collective-permute-done.b_ref = f32[3,128]{1,0:T(4,128)S(1)} collective-permute-done((f32[3,128]{1,0:T(4,128)S(1)}, f32[3,128]{1,0:T(4,128)S(1)}, u32[]{:S(2)}, u32[]{:S(2)}) %collective-permute-start) | collective-permute-done | bytes 1568 | tf_op jit(solution)/shard_map/ppermute | solution.py:342
  12.2 0.5 %shard_map.71 = (f32[32,1,128]{2,1,0:T(1,128)S(1)}, f32[1,64]{1,0:T(1,128)S(1)}, f32[8,512]{1,0:T(8,128)S(1)}, f32[3,40,128]{2,1,0:T(8,128)S(1)}, f32[3,40,128]{2,1,0:T(8,128)S(1)}) custom-call(f32[3,128]{1,0:T(4,128)S(1)} %collective-permute-done.b_ref, f32[3,40,128]{2,1,0:T(8,128)S(1)} %get-tuple-element.29.vd_ref, ...), custom_call_target="tpu_custom_call" | custom-call | bytes 547840 | tf_op jit(solution)/shard_map/pallas_call | solution.py:369
  12.7 11.6 %all_to_all.5.got_ref = f32[32,1,128]{2,1,0:T(1,128)S(1)} all-to-all(f32[32,1,128]{2,1,0:T(1,128)S(1)} %get-tuple-element.40), channel_id=1, replica_groups=mesh['slab'=16,'sub'=2] {'slab','sub'}, dimensions={0} | all-to-all | bytes 32768 | tf_op jit(solution)/shard_map/all_to_all | solution.py:426
  24.3 0.8 %shard_map.72 = (f32[3,5120]{1,0:T(4,128)}, f32[1,64]{1,0:T(1,128)}) custom-call(f32[32,1,128]{2,1,0:T(1,128)S(1)} %all_to_all.5.got_ref, f32[1,128]{1,0:T(1,128)S(1)} %get-tuple-element.41.target_ref, f32[1,64]{1,0:T(1,128)S(1)} %get-tuple-element.42.profile_ref, f32[3,40,128]{2,1,0:T(8,128)S(1)} %get-tuple-element.43.mean_ref, ...), custom_call_target="tpu_custom_call" | custom-call | bytes 321792 | tf_op jit(solution)/shard_map/pallas_call | solution.py:369
Async XLA Ops:
  1.6 7.9 %copy-start = (s32[1,5120]{1,0:T(1,128)S(1)}, s32[1,5120]{1,0:T(1,128)}, u32[]{:S(2)}) copy-start(s32[1,5120]{1,0:T(1,128)} %cell_ref.1) | copy-start | bytes 61444
  1.9 7.7 %collective-permute-start.2 = (f32[3,256]{1,0:T(4,128)S(1)}, f32[3,256]{1,0:T(4,128)S(1)}, u32[]{:S(2)}, u32[]{:S(2)}) collective-permute-start(f32[3,256]{1,0:T(4,128)S(1)} %get-tuple-element.28), channel_id=1, source_target_pairs={{0,1},{1,0},{2,3},{3,2},{4,5},{5,4},{6,7},{7,6},{8,9},{9,8},{10,11... | collective-permute-start | bytes 9224 | tf_op jit(solution)/shard_map/ppermute | solution.py:350
  2.4 7.1 %copy-start.1 = (s32[1,512]{1,0:T(1,128)S(1)}, s32[1,512]{1,0:T(1,128)}, u32[]{:S(2)}) copy-start(s32[1,512]{1,0:T(1,128)} %choice_ref.1) | copy-start | bytes 6148
  2.4 7.1 %collective-permute-start.1 = (f32[3,128]{1,0:T(4,128)S(1)}, f32[3,128]{1,0:T(4,128)S(1)}, u32[]{:S(2)}, u32[]{:S(2)}) collective-permute-start(f32[3,128]{1,0:T(4,128)S(1)} %get-tuple-element.27), channel_id=1, source_target_pairs={{0,2},{2,0},{4,6},{6,4},{8,10},{10,8},{12,14},{14,12},{16,18},{18,... | collective-permute-start | bytes 4616 | tf_op jit(solution)/shard_map/ppermute | solution.py:343
  5.0 4.6 %copy-start.2 = (f32[64]{0:T(128)S(1)}, f32[64]{0:T(128)}, u32[]{:S(2)}) copy-start(f32[64]{0:T(128)} %param.9) | copy-start | bytes 772
  5.0 7.2 %collective-permute-start = (f32[3,128]{1,0:T(4,128)S(1)}, f32[3,128]{1,0:T(4,128)S(1)}, u32[]{:S(2)}, u32[]{:S(2)}) collective-permute-start(f32[3,128]{1,0:T(4,128)S(1)} %get-tuple-element.24), channel_id=1, source_target_pairs={{0,30},{2,4},{4,2},{6,8},{8,6},{10,12},{12,10},{14,16},{16,14},{18... | collective-permute-start | bytes 4616 | tf_op jit(solution)/shard_map/ppermute | solution.py:342

commit v10 on v8

--- a/solution.py
+++ b/solution.py
@@ -220,19 +220,21 @@
         spread_ref[:, span] = hits.astype(jnp.bfloat16)
         base_ref[:, span] = sums[h]
         number = sums[h][comps : comps + 1]
-        count_ref[:, span] = 1.0 / jnp.maximum(number, 1.0)
+        count_ref[:, span] = jnp.broadcast_to(1.0 / jnp.maximum(number, 1.0), (SUBLANES, LANES))
         missing = jnp.sum(hits, 0, keepdims=True)
         other = sums[h] / jnp.maximum(number - missing, 1.0)
         others.append(other)
         shift_ref[:, span] = jnp.where(iota((SUBLANES, LANES), 0) < comps, other * missing, 0.0)
     spread_ref[:, cells:] = (columns_of(late_cell) == iota((LANES, LANES), 1)).astype(jnp.bfloat16)
+    slot_ref[...] = jnp.zeros_like(slot_ref)
     energy = jnp.zeros((rows, LANES), jnp.float32)
     for c in range(comps):
         parts = [x[c : c + 1] for x in others]
         slot_ref[c : c + 1, :] = lookup(parts, slotcell[0:1])
         apart = vd_ref[c] - lookup(parts, celld)
         energy += apart * apart
-    energy_ref[...] = jnp.sum(jnp.where(late, 0.0, energy), 0, keepdims=True)
+    energy = jnp.sum(jnp.where(late, 0.0, energy), 0, keepdims=True)
+    energy_ref[...] = energy + pltpu.roll(energy, CY, 1)
 
 
 def on_last_slab():
@@ -268,13 +270,13 @@
     profile = (column_ref[0:1] + fresh[0:1, cells:]) * column_ref[1:2]
     profile_ref[...] = profile[:, :CY]
 
+    apart = block - slot_ref[...]
     moved = fresh[:, :cells] - shift_ref[...]
-    less = jnp.sum(moved * moved, 0, keepdims=True) * count_ref[...]
-    apart = late - slot_ref[...]
-    energy = energy_ref[...] + jnp.sum(apart * apart, 0, keepdims=True)
+    less = moved * moved * count_ref[...]
+    energy = apart * apart
     for h in range(0, cells, LANES):
         energy = energy - less[:, h : h + LANES]
-    energy = energy + pltpu.roll(energy, CY, 1)
+    energy = jnp.sum(energy + pltpu.roll(energy, CY, 1), 0, keepdims=True) + energy_ref[...]
     message = jnp.where(iota((1, LANES), 1) < CY, profile, energy)
     send_ref[...] = jnp.broadcast_to(message[None], send_ref.shape)
 
@@ -284,8 +286,10 @@
 
 
 def finish(got_ref, target_ref, profile_ref, mean_ref, turned_ref, b_ref, means_ref, vd_ref, source_ref, celld_ref, normal_ref, out_hbm, profile_hbm, out_ref, own_mean_ref, own_turned_ref, sems, *, slabs, subs, particles):
-    comps, rows, _ = mean_ref.shape
-    copies = [pltpu.make_async_copy(profile_ref, profile_hbm, sems.at[0]), pltpu.make_async_copy(out_ref, out_hbm, sems.at[1])]
+    comps, _, _ = mean_ref.shape
+    parts = chunks(out_ref.shape[1], 2)
+    copies = [pltpu.make_async_copy(profile_ref, profile_hbm, sems.at[0])]
+    copies += [pltpu.make_async_copy(out_ref.at[:, span], out_hbm.at[:, span], sems.at[1 + k]) for k, span, _ in parts]
     copies[0].start()
     got = got_ref[...].reshape(slabs * subs, LANES)
     mine = lax.rem(iota(got.shape, 0), subs) == lax.axis_index("sub")
@@ -299,11 +303,15 @@
     shift = take(jnp.broadcast_to(extra, line.shape), line)
 
     def write(mean_ref, turned_ref):
-        for c in range(comps):
-            base = mean_ref[c] + shift if c == 0 else mean_ref[c]
-            out = base + scale * turned_ref[c]
-            for r in range(rows):
-                out_ref[c : c + 1, r * LANES : (r + 1) * LANES] = out[r : r + 1, :]
+        for (_, _, own), copy in zip(parts, copies[1:]):
+            span = slice(own.start // SUBLANES * SUBLANES, -(-own.stop // SUBLANES) * SUBLANES)
+            for c in range(comps):
+                base = mean_ref[c, span, :] + shift[span] if c == 0 else mean_ref[c, span, :]
+                out = base + scale * turned_ref[c, span, :]
+                for r in own:
+                    at = r - span.start
+                    out_ref[c : c + 1, r * LANES : (r + 1) * LANES] = out[at : at + 1, :]
+            copy.start()
 
     last = on_last_slab()
 
@@ -316,7 +324,6 @@
     def _():
         write(mean_ref, turned_ref)
 
-    copies[1].start()
     for copy in copies:
         copy.wait()
 
@@ -396,13 +403,13 @@
             index,
             index,
             sums,
-            f32(1, cell_count),
+            sums,
             f32(2, LANES),
             pltpu.VMEM((LANES, cell_count + LANES), jnp.bfloat16),
             dense,
             f32(1, LANES),
             sums,
-            f32(comps, LANES),
+            f32(SUBLANES, LANES),
             f32(1, LANES),
         ),
         (speeds, moves, cells, choices, shear_target[None, :], a, s),
@@ -423,7 +430,7 @@
             pltpu.VMEM((comps, count), jnp.float32),
             pltpu.VMEM((comps, rows, LANES), jnp.float32),
             pltpu.VMEM((comps, rows, LANES), jnp.float32),
-            pltpu.SemaphoreType.DMA((2,)),
+            pltpu.SemaphoreType.DMA((3,)),
         ],
     )
 

time: 25.3 us -> 25.3 us (level)
  no operation moved by 1% of the time
where the time goes in v10:
time: 25.3 us; the launch traced here: 25.1 us
  blocking collectives  11.6 us (46%)
  starting transfers between devices  7.65 us (30%)
  Pallas kernels  3.95 us (16%)
  waiting for transfers between devices  1.2 us (5%)
  between operations  0.68 us (3%)
    all_to_all x1, blocking collectives, step(): got = lax.all_to_all(send, AXES, 0, 0, tiled=True)  11.6 us
    ppermute x1, starting transfers between devices, swap(): second = lax.ppermute(two, axis, odd)  4.53 us
    pallas_call x5, Pallas kernels, call(): pl.pallas_call(kernel, out_shape=out_shape, in_specs=[place] * len(inputs...  3.95 us
    ppermute x1, starting transfers between devices, swap(): first = lax.ppermute(one, axis, even)  2.56 us
    ppermute x1, waiting for transfers between devices, swap(): second = lax.ppermute(two, axis, odd)  1.2 us
    ppermute x1, starting transfers between devices, swap_joined(): return lax.ppermute(block, axis, [(0, 1), (1, 0)])  0.56 us
  transfers between devices with their start and end apart: 3, of which 1 were waited for; matrix products, arithmetic and copies ran while one was open for 0% of the time, Pallas kernels for 6%

profile of v10, /device:TPU:0, one launch (start us, length us, event | category | flops | bytes accessed | tf_op | source)
XLA Modules:
  0.0 25.1 jit_solution(2040101954932611227)
XLA Ops:
  0.6 1.0 %shard_map.68 = (f32[3,128]{1,0:T(4,128)S(1)}, f32[3,5120]{1,0:T(4,128)S(1)}, s32[4,128]{1,0:T(4,128)S(1)}) custom-call(f32[3,5120]{1,0:T(4,128)} %v_hbm.1, s32[4,128]{1,0:T(4,128)} %bitcast.3), custom_call_target="tpu_custom_call" | custom-call | bytes 63488 | tf_op jit(solution)/shard_map/pallas_call | solution.py:367
  1.6 0.0 copy-start
  1.7 0.2 shard_map.69
  1.9 0.6 %collective-permute-start.2 = (f32[3,256]{1,0:T(4,128)S(1)}, f32[3,256]{1,0:T(4,128)S(1)}, u32[]{:S(2)}, u32[]{:S(2)}) collective-permute-start(f32[3,256]{1,0:T(4,128)S(1)} %get-tuple-element.28), channel_id=1, source_target_pairs={{0,1},{1,0},{2,3},{3,2},{4,5},{5,4},{6,7},{7,6},{8,9},{9,8},{10,11... | collective-permute-start | bytes 9224 | tf_op jit(solution)/shard_map/ppermute | solution.py:348
  2.4 0.0 copy-start.1
  2.4 2.6 %collective-permute-start.1 = (f32[3,128]{1,0:T(4,128)S(1)}, f32[3,128]{1,0:T(4,128)S(1)}, u32[]{:S(2)}, u32[]{:S(2)}) collective-permute-start(f32[3,128]{1,0:T(4,128)S(1)} %get-tuple-element.27), channel_id=1, source_target_pairs={{0,2},{2,0},{4,6},{6,4},{8,10},{10,8},{12,14},{14,12},{16,18},{18,... | collective-permute-start | bytes 4616 | tf_op jit(solution)/shard_map/ppermute | solution.py:341
  5.0 0.0 copy-start.2
  5.0 4.5 %collective-permute-start = (f32[3,128]{1,0:T(4,128)S(1)}, f32[3,128]{1,0:T(4,128)S(1)}, u32[]{:S(2)}, u32[]{:S(2)}) collective-permute-start(f32[3,128]{1,0:T(4,128)S(1)} %get-tuple-element.24), channel_id=1, source_target_pairs={{0,30},{2,4},{4,2},{6,8},{8,6},{10,12},{12,10},{14,16},{16,14},{18... | collective-permute-start | bytes 4616 | tf_op jit(solution)/shard_map/ppermute | solution.py:340
  9.5 0.0 collective-permute-done.1.a_ref
  9.5 0.0 collective-permute-done.2.s_ref
  9.5 0.0 copy-done
  9.5 0.0 copy-done.1
  9.5 0.0 copy-done.2
  9.6 1.4 %shard_map.70 = (f32[3,40,128]{2,1,0:T(8,128)S(1)}, s32[40,128]{1,0:T(8,128)S(1)}, s32[40,128]{1,0:T(8,128)S(1)}, f32[8,512]{1,0:T(8,128)S(1)}, f32[8,512]{1,0:T...) custom-call(f32[3,5120]{1,0:T(4,128)S(1)} %get-tuple-element.25.v_re, ...), custom_call_target="tpu_custom_call" | custom-call | flops 125829120 | bytes 90880 | tf_op jit(solution)/shard_map/pallas_call | solution.py:367
  11.0 1.2 %collective-permute-done.b_ref = f32[3,128]{1,0:T(4,128)S(1)} collective-permute-done((f32[3,128]{1,0:T(4,128)S(1)}, f32[3,128]{1,0:T(4,128)S(1)}, u32[]{:S(2)}, u32[]{:S(2)}) %collective-permute-start) | collective-permute-done | bytes 1568 | tf_op jit(solution)/shard_map/ppermute | solution.py:340
  12.2 0.5 %shard_map.71 = (f32[32,1,128]{2,1,0:T(1,128)S(1)}, f32[1,64]{1,0:T(1,128)S(1)}, f32[8,512]{1,0:T(8,128)S(1)}, f32[3,40,128]{2,1,0:T(8,128)S(1)}, f32[3,40,128]{2,1,0:T(8,128)S(1)}) custom-call(f32[3,128]{1,0:T(4,128)S(1)} %collective-permute-done.b_ref, f32[3,40,128]{2,1,0:T(8,128)S(1)} %get-tuple-element.29.vd_ref, ...), custom_call_target="tpu_custom_call" | custom-call | bytes 547840 | tf_op jit(solution)/shard_map/pallas_call | solution.py:367
  12.7 11.6 %all_to_all.5.got_ref = f32[32,1,128]{2,1,0:T(1,128)S(1)} all-to-all(f32[32,1,128]{2,1,0:T(1,128)S(1)} %get-tuple-element.40), channel_id=1, replica_groups=mesh['slab'=16,'sub'=2] {'slab','sub'}, dimensions={0} | all-to-all | bytes 32768 | tf_op jit(solution)/shard_map/all_to_all | solution.py:424
  24.3 0.8 %shard_map.72 = (f32[3,5120]{1,0:T(4,128)}, f32[1,64]{1,0:T(1,128)}) custom-call(f32[32,1,128]{2,1,0:T(1,128)S(1)} %all_to_all.5.got_ref, f32[1,128]{1,0:T(1,128)S(1)} %get-tuple-element.41.target_ref, f32[1,64]{1,0:T(1,128)S(1)} %get-tuple-element.42.profile_ref, f32[3,40,128]{2,1,0:T(8,128)S(1)} %get-tuple-element.43.mean_ref, ...), custom_call_target="tpu_custom_call" | custom-call | bytes 321792 | tf_op jit(solution)/shard_map/pallas_call | solution.py:367
Async XLA Ops:
  1.6 7.9 %copy-start = (s32[1,5120]{1,0:T(1,128)S(1)}, s32[1,5120]{1,0:T(1,128)}, u32[]{:S(2)}) copy-start(s32[1,5120]{1,0:T(1,128)} %cell_ref.1) | copy-start | bytes 61444
  1.9 7.7 %collective-permute-start.2 = (f32[3,256]{1,0:T(4,128)S(1)}, f32[3,256]{1,0:T(4,128)S(1)}, u32[]{:S(2)}, u32[]{:S(2)}) collective-permute-start(f32[3,256]{1,0:T(4,128)S(1)} %get-tuple-element.28), channel_id=1, source_target_pairs={{0,1},{1,0},{2,3},{3,2},{4,5},{5,4},{6,7},{7,6},{8,9},{9,8},{10,11... | collective-permute-start | bytes 9224 | tf_op jit(solution)/shard_map/ppermute | solution.py:348
  2.4 7.1 %copy-start.1 = (s32[1,512]{1,0:T(1,128)S(1)}, s32[1,512]{1,0:T(1,128)}, u32[]{:S(2)}) copy-start(s32[1,512]{1,0:T(1,128)} %choice_ref.1) | copy-start | bytes 6148
  2.4 7.1 %collective-permute-start.1 = (f32[3,128]{1,0:T(4,128)S(1)}, f32[3,128]{1,0:T(4,128)S(1)}, u32[]{:S(2)}, u32[]{:S(2)}) collective-permute-start(f32[3,128]{1,0:T(4,128)S(1)} %get-tuple-element.27), channel_id=1, source_target_pairs={{0,2},{2,0},{4,6},{6,4},{8,10},{10,8},{12,14},{14,12},{16,18},{18,... | collective-permute-start | bytes 4616 | tf_op jit(solution)/shard_map/ppermute | solution.py:341
  5.0 4.6 %copy-start.2 = (f32[64]{0:T(128)S(1)}, f32[64]{0:T(128)}, u32[]{:S(2)}) copy-start(f32[64]{0:T(128)} %param.9) | copy-start | bytes 772
  5.0 7.2 %collective-permute-start = (f32[3,128]{1,0:T(4,128)S(1)}, f32[3,128]{1,0:T(4,128)S(1)}, u32[]{:S(2)}, u32[]{:S(2)}) collective-permute-start(f32[3,128]{1,0:T(4,128)S(1)} %get-tuple-element.24), channel_id=1, source_target_pairs={{0,30},{2,4},{4,2},{6,8},{8,6},{10,12},{12,10},{14,16},{16,14},{18... | collective-permute-start | bytes 4616 | tf_op jit(solution)/shard_map/ppermute | solution.py:340

commit v11 on v8

--- a/solution.py
+++ b/solution.py
@@ -90,7 +90,7 @@
     copies = [pltpu.make_async_copy(moves_hbm, moves_ref, sems.at[len(parts)])]
     copies += [pltpu.make_async_copy(v_hbm.at[:, span], v_ref.at[:, span], sems.at[k]) for k, span, _ in parts]
     for copy in copies:
-        copy.start()
+        copy.start(priority=1)
     copies[0].wait()
     index = ordered_lists(moves_ref)[1]
     comps = v_ref.shape[0]
@@ -220,19 +220,21 @@
         spread_ref[:, span] = hits.astype(jnp.bfloat16)
         base_ref[:, span] = sums[h]
         number = sums[h][comps : comps + 1]
-        count_ref[:, span] = 1.0 / jnp.maximum(number, 1.0)
+        count_ref[:, span] = jnp.broadcast_to(1.0 / jnp.maximum(number, 1.0), (SUBLANES, LANES))
         missing = jnp.sum(hits, 0, keepdims=True)
         other = sums[h] / jnp.maximum(number - missing, 1.0)
         others.append(other)
         shift_ref[:, span] = jnp.where(iota((SUBLANES, LANES), 0) < comps, other * missing, 0.0)
     spread_ref[:, cells:] = (columns_of(late_cell) == iota((LANES, LANES), 1)).astype(jnp.bfloat16)
+    slot_ref[...] = jnp.zeros_like(slot_ref)
     energy = jnp.zeros((rows, LANES), jnp.float32)
     for c in range(comps):
         parts = [x[c : c + 1] for x in others]
         slot_ref[c : c + 1, :] = lookup(parts, slotcell[0:1])
         apart = vd_ref[c] - lookup(parts, celld)
         energy += apart * apart
-    energy_ref[...] = jnp.sum(jnp.where(late, 0.0, energy), 0, keepdims=True)
+    energy = jnp.sum(jnp.where(late, 0.0, energy), 0, keepdims=True)
+    energy_ref[...] = energy + pltpu.roll(energy, CY, 1)
 
 
 def on_last_slab():
@@ -268,13 +270,13 @@
     profile = (column_ref[0:1] + fresh[0:1, cells:]) * column_ref[1:2]
     profile_ref[...] = profile[:, :CY]
 
+    apart = block - slot_ref[...]
     moved = fresh[:, :cells] - shift_ref[...]
-    less = jnp.sum(moved * moved, 0, keepdims=True) * count_ref[...]
-    apart = late - slot_ref[...]
-    energy = energy_ref[...] + jnp.sum(apart * apart, 0, keepdims=True)
+    less = moved * moved * count_ref[...]
+    energy = apart * apart
     for h in range(0, cells, LANES):
         energy = energy - less[:, h : h + LANES]
-    energy = energy + pltpu.roll(energy, CY, 1)
+    energy = jnp.sum(energy + pltpu.roll(energy, CY, 1), 0, keepdims=True) + energy_ref[...]
     message = jnp.where(iota((1, LANES), 1) < CY, profile, energy)
     send_ref[...] = jnp.broadcast_to(message[None], send_ref.shape)
 
@@ -396,13 +398,13 @@
             index,
             index,
             sums,
-            f32(1, cell_count),
+            sums,
             f32(2, LANES),
             pltpu.VMEM((LANES, cell_count + LANES), jnp.bfloat16),
             dense,
             f32(1, LANES),
             sums,
-            f32(comps, LANES),
+            f32(SUBLANES, LANES),
             f32(1, LANES),
         ),
         (speeds, moves, cells, choices, shear_target[None, :], a, s),

time: 25.3 us -> 25.3 us (level)
  no operation moved by 1% of the time
where the time goes in v11:
time: 25.3 us; the launch traced here: 25.1 us
  blocking collectives  11.6 us (46%)
  starting transfers between devices  7.65 us (30%)
  Pallas kernels  3.95 us (16%)
  waiting for transfers between devices  1.2 us (5%)
  between operations  0.68 us (3%)
    all_to_all x1, blocking collectives, step(): got = lax.all_to_all(send, AXES, 0, 0, tiled=True)  11.6 us
    ppermute x1, starting transfers between devices, swap(): second = lax.ppermute(two, axis, odd)  4.53 us
    pallas_call x5, Pallas kernels, call(): pl.pallas_call(kernel, out_shape=out_shape, in_specs=[place] * len(inputs...  3.95 us
    ppermute x1, starting transfers between devices, swap(): first = lax.ppermute(one, axis, even)  2.56 us
    ppermute x1, waiting for transfers between devices, swap(): second = lax.ppermute(two, axis, odd)  1.2 us
    ppermute x1, starting transfers between devices, swap_joined(): return lax.ppermute(block, axis, [(0, 1), (1, 0)])  0.56 us
  transfers between devices with their start and end apart: 3, of which 1 were waited for; matrix products, arithmetic and copies ran while one was open for 0% of the time, Pallas kernels for 6%

profile of v11, /device:TPU:0, one launch (start us, length us, event | category | flops | bytes accessed | tf_op | source)
XLA Modules:
  0.0 25.1 jit_solution(15966836170280947123)
XLA Ops:
  0.6 1.0 %shard_map.68 = (f32[3,128]{1,0:T(4,128)S(1)}, f32[3,5120]{1,0:T(4,128)S(1)}, s32[4,128]{1,0:T(4,128)S(1)}) custom-call(f32[3,5120]{1,0:T(4,128)} %v_hbm.1, s32[4,128]{1,0:T(4,128)} %bitcast.3), custom_call_target="tpu_custom_call" | custom-call | bytes 63488 | tf_op jit(solution)/shard_map/pallas_call | solution.py:362
  1.6 0.0 copy-start
  1.7 0.2 shard_map.69
  1.9 0.6 %collective-permute-start.2 = (f32[3,256]{1,0:T(4,128)S(1)}, f32[3,256]{1,0:T(4,128)S(1)}, u32[]{:S(2)}, u32[]{:S(2)}) collective-permute-start(f32[3,256]{1,0:T(4,128)S(1)} %get-tuple-element.28), channel_id=1, source_target_pairs={{0,1},{1,0},{2,3},{3,2},{4,5},{5,4},{6,7},{7,6},{8,9},{9,8},{10,11... | collective-permute-start | bytes 9224 | tf_op jit(solution)/shard_map/ppermute | solution.py:343
  2.4 0.0 copy-start.1
  2.4 2.6 %collective-permute-start.1 = (f32[3,128]{1,0:T(4,128)S(1)}, f32[3,128]{1,0:T(4,128)S(1)}, u32[]{:S(2)}, u32[]{:S(2)}) collective-permute-start(f32[3,128]{1,0:T(4,128)S(1)} %get-tuple-element.27), channel_id=1, source_target_pairs={{0,2},{2,0},{4,6},{6,4},{8,10},{10,8},{12,14},{14,12},{16,18},{18,... | collective-permute-start | bytes 4616 | tf_op jit(solution)/shard_map/ppermute | solution.py:336
  5.0 0.0 copy-start.2
  5.0 4.5 %collective-permute-start = (f32[3,128]{1,0:T(4,128)S(1)}, f32[3,128]{1,0:T(4,128)S(1)}, u32[]{:S(2)}, u32[]{:S(2)}) collective-permute-start(f32[3,128]{1,0:T(4,128)S(1)} %get-tuple-element.24), channel_id=1, source_target_pairs={{0,30},{2,4},{4,2},{6,8},{8,6},{10,12},{12,10},{14,16},{16,14},{18... | collective-permute-start | bytes 4616 | tf_op jit(solution)/shard_map/ppermute | solution.py:335
  9.5 0.0 collective-permute-done.1.a_ref
  9.5 0.0 collective-permute-done.2.s_ref
  9.5 0.0 copy-done
  9.5 0.0 copy-done.1
  9.5 0.0 copy-done.2
  9.6 1.4 %shard_map.70 = (f32[3,40,128]{2,1,0:T(8,128)S(1)}, s32[40,128]{1,0:T(8,128)S(1)}, s32[40,128]{1,0:T(8,128)S(1)}, f32[8,512]{1,0:T(8,128)S(1)}, f32[8,512]{1,0:T...) custom-call(f32[3,5120]{1,0:T(4,128)S(1)} %get-tuple-element.25.v_re, ...), custom_call_target="tpu_custom_call" | custom-call | flops 125829120 | bytes 90880 | tf_op jit(solution)/shard_map/pallas_call | solution.py:362
  11.0 1.2 %collective-permute-done.b_ref = f32[3,128]{1,0:T(4,128)S(1)} collective-permute-done((f32[3,128]{1,0:T(4,128)S(1)}, f32[3,128]{1,0:T(4,128)S(1)}, u32[]{:S(2)}, u32[]{:S(2)}) %collective-permute-start) | collective-permute-done | bytes 1568 | tf_op jit(solution)/shard_map/ppermute | solution.py:335
  12.2 0.5 %shard_map.71 = (f32[32,1,128]{2,1,0:T(1,128)S(1)}, f32[1,64]{1,0:T(1,128)S(1)}, f32[8,512]{1,0:T(8,128)S(1)}, f32[3,40,128]{2,1,0:T(8,128)S(1)}, f32[3,40,128]{2,1,0:T(8,128)S(1)}) custom-call(f32[3,128]{1,0:T(4,128)S(1)} %collective-permute-done.b_ref, f32[3,40,128]{2,1,0:T(8,128)S(1)} %get-tuple-element.29.vd_ref, ...), custom_call_target="tpu_custom_call" | custom-call | bytes 547840 | tf_op jit(solution)/shard_map/pallas_call | solution.py:362
  12.7 11.6 %all_to_all.5.got_ref = f32[32,1,128]{2,1,0:T(1,128)S(1)} all-to-all(f32[32,1,128]{2,1,0:T(1,128)S(1)} %get-tuple-element.40), channel_id=1, replica_groups=mesh['slab'=16,'sub'=2] {'slab','sub'}, dimensions={0} | all-to-all | bytes 32768 | tf_op jit(solution)/shard_map/all_to_all | solution.py:419
  24.3 0.8 %shard_map.72 = (f32[3,5120]{1,0:T(4,128)}, f32[1,64]{1,0:T(1,128)}) custom-call(f32[32,1,128]{2,1,0:T(1,128)S(1)} %all_to_all.5.got_ref, f32[1,128]{1,0:T(1,128)S(1)} %get-tuple-element.41.target_ref, f32[1,64]{1,0:T(1,128)S(1)} %get-tuple-element.42.profile_ref, f32[3,40,128]{2,1,0:T(8,128)S(1)} %get-tuple-element.43.mean_ref, ...), custom_call_target="tpu_custom_call" | custom-call | bytes 321792 | tf_op jit(solution)/shard_map/pallas_call | solution.py:362
Async XLA Ops:
  1.6 7.9 %copy-start = (s32[1,5120]{1,0:T(1,128)S(1)}, s32[1,5120]{1,0:T(1,128)}, u32[]{:S(2)}) copy-start(s32[1,5120]{1,0:T(1,128)} %cell_ref.1) | copy-start | bytes 61444
  1.9 7.7 %collective-permute-start.2 = (f32[3,256]{1,0:T(4,128)S(1)}, f32[3,256]{1,0:T(4,128)S(1)}, u32[]{:S(2)}, u32[]{:S(2)}) collective-permute-start(f32[3,256]{1,0:T(4,128)S(1)} %get-tuple-element.28), channel_id=1, source_target_pairs={{0,1},{1,0},{2,3},{3,2},{4,5},{5,4},{6,7},{7,6},{8,9},{9,8},{10,11... | collective-permute-start | bytes 9224 | tf_op jit(solution)/shard_map/ppermute | solution.py:343
  2.4 7.1 %copy-start.1 = (s32[1,512]{1,0:T(1,128)S(1)}, s32[1,512]{1,0:T(1,128)}, u32[]{:S(2)}) copy-start(s32[1,512]{1,0:T(1,128)} %choice_ref.1) | copy-start | bytes 6148
  2.4 7.1 %collective-permute-start.1 = (f32[3,128]{1,0:T(4,128)S(1)}, f32[3,128]{1,0:T(4,128)S(1)}, u32[]{:S(2)}, u32[]{:S(2)}) collective-permute-start(f32[3,128]{1,0:T(4,128)S(1)} %get-tuple-element.27), channel_id=1, source_target_pairs={{0,2},{2,0},{4,6},{6,4},{8,10},{10,8},{12,14},{14,12},{16,18},{18,... | collective-permute-start | bytes 4616 | tf_op jit(solution)/shard_map/ppermute | solution.py:336
  5.0 4.6 %copy-start.2 = (f32[64]{0:T(128)S(1)}, f32[64]{0:T(128)}, u32[]{:S(2)}) copy-start(f32[64]{0:T(128)} %param.9) | copy-start | bytes 772
  5.0 7.2 %collective-permute-start = (f32[3,128]{1,0:T(4,128)S(1)}, f32[3,128]{1,0:T(4,128)S(1)}, u32[]{:S(2)}, u32[]{:S(2)}) collective-permute-start(f32[3,128]{1,0:T(4,128)S(1)} %get-tuple-element.24), channel_id=1, source_target_pairs={{0,30},{2,4},{4,2},{6,8},{8,6},{10,12},{12,10},{14,16},{16,14},{18... | collective-permute-start | bytes 4616 | tf_op jit(solution)/shard_map/ppermute | solution.py:335
